TPU v7x, 1024 devices: a whole 8x8x8 slice. The times are simulated.
1024 devices in a mesh: gx: 16 (over x, core), gy: 64 (over y, z).
Axes of the slice: x: 8, y: 8, z: 8, core: 2. Of those that a mesh axis runs over, the one named last changes fastest.
Arguments:
- solution: float32 [128, 512, 512], P('gx', 'gy'), may hold values from -6 to 6
- right_side: float32 [128, 512, 512], P('gx', 'gy'), may hold values from -6 to 6
- alpha: bfloat16 [128, 512, 512], P('gx', 'gy'), may hold values from 0.5 to 2
- beta_x: bfloat16 [128, 512, 512], P('gx', 'gy'), may hold values from 0.25 to 2.5
- beta_y: bfloat16 [128, 512, 512], P('gx', 'gy'), may hold values from 0.25 to 2.5
- beta_z: bfloat16 [128, 512, 512], P('gx', 'gy'), may hold values from 0.25 to 2.5
Outputs:
- fine_iterate: float32 [128, 512, 512], P('gx', 'gy')
- middle_iterate: float32 [64, 256, 256], P('gx', 'gy')
- coarse_iterate: float32 [32, 128, 128], P('gx', 'gy')
All inputs are finite; a program needn't handle non-finite values.
Results may differ from a plain program's by a relative error of at most 0.0003.
Values sent between devices are 32-bit elements; how exact they have to be, the bound alone decides.
No kernel may reach another device: no remote copies, remote signals or barrier semaphores. Data moves between devices by JAX's collectives and lax.ppermute only.
A program may use at most 64 MiB of HBM per device.

v0:
```python
import jax
import jax.numpy as jnp
from jax import lax
from jax.sharding import PartitionSpec as P

LEVELS = 3
SWEEPS = 2


def from_behind(block, axis, distance):
    devices = range(lax.axis_size(axis))
    route = [(i - distance, i) for i in devices if i - distance in devices]
    return lax.ppermute(block, axis, route)


def padded_2(shard, sides, width):
    for axis, dim in sides:
        count, length = (lax.axis_size(axis), shard.shape[dim])
        up = [(i, (i + 1) % count) for i in range(count - 1)]
        down = [(j, i) for i, j in up]
        last = lax.slice_in_dim(shard, length - width, length, axis=dim)
        first = lax.slice_in_dim(shard, 0, width, axis=dim)
        before = lax.ppermute(last, axis, up)
        after = lax.ppermute(first, axis, down)
        shard = jnp.concatenate([before, shard, after], axis=dim)
    return shard


def shift_up(field, axis):
    size = field.shape[axis]
    rest = lax.slice_in_dim(field, 1, size, axis=axis)
    edge = jnp.zeros_like(lax.slice_in_dim(field, 0, 1, axis=axis))
    return jnp.concatenate([rest, edge], axis=axis)


def shift_down(field, axis):
    size = field.shape[axis]
    rest = lax.slice_in_dim(field, 0, size - 1, axis=axis)
    edge = jnp.zeros_like(lax.slice_in_dim(field, 0, 1, axis=axis))
    return jnp.concatenate([edge, rest], axis=axis)


def stencil(field, beside, coefs, scale):
    out = coefs[0] * field
    for direc in range(3):
        upper_face = coefs[1 + 2 * direc]
        lower_face = coefs[2 + 2 * direc]
        out = out + scale * (
            upper_face * (field - beside[2 * direc]) + lower_face * (field - beside[2 * direc + 1])
        )
    return out


def diagonal_of(coefs, scale):
    return coefs[0] + scale * (coefs[1] + coefs[2] + (coefs[3] + coefs[4]) + (coefs[5] + coefs[6]))


def parity_of(shape):
    total = (
        lax.broadcasted_iota(jnp.int32, shape, 0)
        + lax.broadcasted_iota(jnp.int32, shape, 1)
        + lax.broadcasted_iota(jnp.int32, shape, 2)
    )
    return total % 2


def coarsen_cells(field):
    nx, ny, nz = field.shape
    return field.reshape(nx // 2, 2, ny // 2, 2, nz // 2, 2).mean(axis=(1, 3, 5))


def coarsen_faces(bx, by, bz):
    nx, ny, nz = bx.shape
    cx = bx[1::2].reshape(nx // 2, ny // 2, 2, nz // 2, 2).mean(axis=(2, 4))
    cy = by[:, 1::2].reshape(nx // 2, 2, ny // 2, nz // 2, 2).mean(axis=(1, 4))
    cz = bz[:, :, 1::2].reshape(nx // 2, 2, ny // 2, 2, nz // 2).mean(axis=(1, 3))
    return (cx, cy, cz)


def from_x(layer, stride):
    return from_behind(layer, "gx", stride)


def from_y(layer, stride):
    return from_behind(layer, "gy", stride)


def neighbours(field):
    padded = padded_2(field, (("gx", 0), ("gy", 1)), 1)
    return (
        padded[2:, 1:-1],
        padded[:-2, 1:-1],
        padded[1:-1, 2:],
        padded[1:-1, :-2],
        shift_up(field, 2),
        shift_down(field, 2),
    )


def lower_faces(face_x, face_y, face_z, group):
    edge_x = from_x(face_x[-1:], group)
    edge_y = from_y(face_y[:, -1:], group)
    below_x = jnp.concatenate([edge_x, face_x[:-1]], axis=0)
    below_y = jnp.concatenate([edge_y, face_y[:, :-1]], axis=1)
    return (below_x, below_y, shift_down(face_z, 2))


def shards(solution, right_side, alpha, beta_x, beta_y, beta_z):
    iterate = solution
    source = right_side
    cell_coef = alpha.astype(jnp.float32)
    face_x = beta_x.astype(jnp.float32)
    face_y = beta_y.astype(jnp.float32)
    face_z = beta_z.astype(jnp.float32)
    results = []
    for level in range(LEVELS):
        scale = 0.25**level
        group = 1
        below_x, below_y, below_z = lower_faces(face_x, face_y, face_z, group)
        coefs = (cell_coef, face_x, below_x, face_y, below_y, face_z, below_z)
        diag = diagonal_of(coefs, scale)
        parity = parity_of(iterate.shape)
        for sweep in range(SWEEPS):
            for colour in (0, 1):
                resid = source - stencil(iterate, neighbours(iterate), coefs, scale)
                iterate = jnp.where(parity == colour, iterate + resid / diag, iterate)
        results.append(iterate)
        if level + 1 < LEVELS:
            resid = source - stencil(iterate, neighbours(iterate), coefs, scale)
            source = coarsen_cells(resid)
            cell_coef = coarsen_cells(cell_coef)
            face_x, face_y, face_z = coarsen_faces(face_x, face_y, face_z)
            iterate = jnp.zeros_like(source)
    return (results[0], results[1], results[2])


def solution(mesh):
    placed = (
        P("gx", "gy", None),
        P("gx", "gy", None),
        P("gx", "gy", None),
        P("gx", "gy", None),
        P("gx", "gy", None),
        P("gx", "gy", None),
    )
    return jax.shard_map(
        shards,
        mesh=mesh,
        in_specs=placed,
        out_specs=(P("gx", "gy", None), P("gx", "gy", None), P("gx", "gy", None)),
        check_vma=False,
    )
```

profile of v0, /device:TPU:72, one launch (start us, length us, event | category | flops | bytes accessed | tf_op | source)
XLA Modules:
  0.0 323.5 jit_solution(13235005306741292083)
XLA Ops:
  3.3 4.9 %collective-permute-start = (f32[1,8,512]{2,1,0:T(8,128)S(1)}, f32[1,8,512]{2,1,0:T(8,128)S(1)}, u32[]{:S(2)}, u32[]{:S(2)}) collective-permute-start(f32[1,8,512]{2,1,0:T(8,128)S(1)} %get-tuple-element.37), channel_id=1, source_target_pairs={{64,0},{128,64},{192,128},{256,192},{320,256},{384,320},{448,384},... | collective-permute-start | bytes 49160 | tf_op jit(solution)/shard_map/ppermute | solution.py:24
  11.7 5.2 %collective-permute-start.4 = (f32[8,1,512]{2,1,0:T(1,128)S(1)}, f32[8,1,512]{2,1,0:T(1,128)S(1)}, u32[]{:S(2)}, u32[]{:S(2)}) collective-permute-start(f32[8,1,512]{2,1,0:T(1,128)S(1)} %slice.671), channel_id=1, source_target_pairs={{0,1},{1,2},{2,3},{3,4},{4,5},{5,6},{6,7},{7,8},{8,9},{9,10},{10,1... | collective-permute-start | bytes 49160 | tf_op jit(solution)/shard_map/ppermute | solution.py:13
  16.9 4.6 %collective-permute-start.22 = (f32[1,4,256]{2,1,0:T(4,128)S(1)}, f32[1,4,256]{2,1,0:T(4,128)S(1)}, u32[]{:S(2)}, u32[]{:S(2)}) collective-permute-start(f32[1,4,256]{2,1,0:T(4,128)S(1)} %broadcast.134), channel_id=1, source_target_pairs={{64,0},{128,64},{192,128},{256,192},{320,256},{384,320},{448,384},... | collective-permute-start | bytes 12296 | tf_op jit(solution)/shard_map/ppermute | solution.py:24
  30.6 9.7 %reshape.38 = f32[4,2,4,2,256,2]{5,4,3,2,1,0:T(8,128)} reshape(bf16[8,8,512]{2,1,0:T(8,128)(2,1)S(1)} %copy-done.6) | data formatting | bytes 196608 | tf_op jit(solution)/shard_map/reshape | solution.py:69
  40.4 4.0 %reduce_sum.91 = f32[4,4,256]{2,1,0:T(4,128)S(1)} reduce(f32[4,2,4,2,256,2]{5,4,3,2,1,0:T(8,128)} %reshape.38, f32[]{:T(128)} %constant.65.clone.1), dimensions={1,3,5}, to_apply=%region_1.2 | reduce | flops 28672 | bytes 147460 | tf_op jit(solution)/shard_map/reduce_sum | solution.py:69
  44.5 14.1 %collective-permute-start.3 = (f32[10,1,512]{2,1,0:T(1,128)S(1)}, f32[10,1,512]{2,1,0:T(1,128)S(1)}, u32[]{:S(2)}, u32[]{:S(2)}) collective-permute-start(f32[10,1,512]{2,1,0:T(1,128)S(1)} %get-tuple-element.17), channel_id=1, source_target_pairs={{1,0},{2,1},{3,2},{4,3},{5,4},{6,5},{7,6},{8,7},{9,8},{10,9},{11,1... | collective-permute-start | bytes 61448 | tf_op jit(solution)/shard_map/ppermute | solution.py:24
  65.2 2.4 collective-permute-done.5
  67.9 2.4 collective-permute-start.6
  72.9 3.6 %collective-permute-done.7 = f32[1,8,512]{2,1,0:T(8,128)S(1)} collective-permute-done((f32[1,8,512]{2,1,0:T(8,128)S(1)}, f32[1,8,512]{2,1,0:T(8,128)S(1)}, u32[]{:S(2)}, u32[]{:S(2)}) %collective-permute-start.7) | collective-permute-done | bytes 16416 | tf_op jit(solution)/shard_map/ppermute | solution.py:23
  76.6 7.2 %collective-permute-start.8 = (f32[10,1,512]{2,1,0:T(1,128)S(1)}, f32[10,1,512]{2,1,0:T(1,128)S(1)}, u32[]{:S(2)}, u32[]{:S(2)}) collective-permute-start(f32[10,1,512]{2,1,0:T(1,128)S(1)} %get-tuple-element.15), channel_id=1, source_target_pairs={{1,0},{2,1},{3,2},{4,3},{5,4},{6,5},{7,6},{8,7},{9,8},{10,9},{11,1... | collective-permute-start | bytes 61448 | tf_op jit(solution)/shard_map/ppermute | solution.py:24
  85.9 7.0 %collective-permute-done.9 = f32[10,1,512]{2,1,0:T(1,128)S(1)} collective-permute-done((f32[10,1,512]{2,1,0:T(1,128)S(1)}, f32[10,1,512]{2,1,0:T(1,128)S(1)}, u32[]{:S(2)}, u32[]{:S(2)}) %collective-permute-start.9) | collective-permute-done | bytes 20512 | tf_op jit(solution)/shard_map/ppermute | solution.py:23
  95.1 2.4 collective-permute-start.11
  97.5 3.8 %collective-permute-done.11 = f32[1,8,512]{2,1,0:T(8,128)S(1)} collective-permute-done((f32[1,8,512]{2,1,0:T(8,128)S(1)}, f32[1,8,512]{2,1,0:T(8,128)S(1)}, u32[]{:S(2)}, u32[]{:S(2)}) %collective-permute-start.11) | collective-permute-done | bytes 16416 | tf_op jit(solution)/shard_map/ppermute | solution.py:23
  103.3 3.9 %collective-permute-start.13 = (f32[10,1,512]{2,1,0:T(1,128)S(1)}, f32[10,1,512]{2,1,0:T(1,128)S(1)}, u32[]{:S(2)}, u32[]{:S(2)}) collective-permute-start(f32[10,1,512]{2,1,0:T(1,128)S(1)} %get-tuple-element.14), channel_id=1, source_target_pairs={{0,1},{1,2},{2,3},{3,4},{4,5},{5,6},{6,7},{7,8},{8,9},{9,10},{10,1... | collective-permute-start | bytes 61448 | tf_op jit(solution)/shard_map/ppermute | solution.py:23
  107.3 5.0 %collective-permute-done.13 = f32[10,1,512]{2,1,0:T(1,128)S(1)} collective-permute-done((f32[10,1,512]{2,1,0:T(1,128)S(1)}, f32[10,1,512]{2,1,0:T(1,128)S(1)}, u32[]{:S(2)}, u32[]{:S(2)}) %collective-permute-start.13) | collective-permute-done | bytes 20512 | tf_op jit(solution)/shard_map/ppermute | solution.py:23
  114.5 2.4 collective-permute-start.15
  117.0 3.8 %collective-permute-done.15 = f32[1,8,512]{2,1,0:T(8,128)S(1)} collective-permute-done((f32[1,8,512]{2,1,0:T(8,128)S(1)}, f32[1,8,512]{2,1,0:T(8,128)S(1)}, u32[]{:S(2)}, u32[]{:S(2)}) %collective-permute-start.15) | collective-permute-done | bytes 16416 | tf_op jit(solution)/shard_map/ppermute | solution.py:23
  122.7 3.9 %collective-permute-start.17 = (f32[10,1,512]{2,1,0:T(1,128)S(1)}, f32[10,1,512]{2,1,0:T(1,128)S(1)}, u32[]{:S(2)}, u32[]{:S(2)}) collective-permute-start(f32[10,1,512]{2,1,0:T(1,128)S(1)} %get-tuple-element.12), channel_id=1, source_target_pairs={{0,1},{1,2},{2,3},{3,4},{4,5},{5,6},{6,7},{7,8},{8,9},{9,10},{10,1... | collective-permute-start | bytes 61448 | tf_op jit(solution)/shard_map/ppermute | solution.py:23
  128.7 3.0 collective-permute-done.17
  135.9 2.4 collective-permute-start.19
  138.3 3.8 %collective-permute-done.19 = f32[1,8,512]{2,1,0:T(8,128)S(1)} collective-permute-done((f32[1,8,512]{2,1,0:T(8,128)S(1)}, f32[1,8,512]{2,1,0:T(8,128)S(1)}, u32[]{:S(2)}, u32[]{:S(2)}) %collective-permute-start.19) | collective-permute-done | bytes 16416 | tf_op jit(solution)/shard_map/ppermute | solution.py:23
  142.2 4.2 %collective-permute-start.20 = (f32[10,1,512]{2,1,0:T(1,128)S(1)}, f32[10,1,512]{2,1,0:T(1,128)S(1)}, u32[]{:S(2)}, u32[]{:S(2)}) collective-permute-start(f32[10,1,512]{2,1,0:T(1,128)S(1)} %get-tuple-element.9), channel_id=1, source_target_pairs={{1,0},{2,1},{3,2},{4,3},{5,4},{6,5},{7,6},{8,7},{9,8},{10,9},{11,1... | collective-permute-start | bytes 61448 | tf_op jit(solution)/shard_map/ppermute | solution.py:24
  148.5 7.2 %collective-permute-start.25 = (f32[6,1,256]{2,1,0:T(1,128)S(1)}, f32[6,1,256]{2,1,0:T(1,128)S(1)}, u32[]{:S(2)}, u32[]{:S(2)}) collective-permute-start(f32[6,1,256]{2,1,0:T(1,128)S(1)} %get-tuple-element.47), channel_id=1, source_target_pairs={{1,0},{2,1},{3,2},{4,3},{5,4},{6,5},{7,6},{8,7},{9,8},{10,9},{11,1... | collective-permute-start | bytes 18440 | tf_op jit(solution)/shard_map/ppermute | solution.py:24
  158.0 9.8 %reshape.37 = f32[4,2,4,2,256,2]{5,4,3,2,1,0:T(8,128)} reshape(f32[8,8,512]{2,1,0:T(8,128)S(1)} %fusion.24) | data formatting | bytes 262144 | tf_op jit(solution)/shard_map/reshape | solution.py:69
  167.8 4.0 %reduce_sum.90 = f32[4,4,256]{2,1,0:T(4,128)S(1)} reduce(f32[4,2,4,2,256,2]{5,4,3,2,1,0:T(8,128)} %reshape.37, f32[]{:T(128)} %constant.65.clone.1), dimensions={1,3,5}, to_apply=%region_0.1 | reduce | flops 28672 | bytes 147460 | tf_op jit(solution)/shard_map/reduce_sum | solution.py:69
  173.8 2.9 collective-permute-start.45
  176.9 3.9 %collective-permute-start.28 = (f32[1,4,256]{2,1,0:T(4,128)S(1)}, f32[1,4,256]{2,1,0:T(4,128)S(1)}, u32[]{:S(2)}, u32[]{:S(2)}) collective-permute-start(f32[1,4,256]{2,1,0:T(4,128)S(1)} %get-tuple-element.64), channel_id=1, source_target_pairs={{64,0},{128,64},{192,128},{256,192},{320,256},{384,320},{448,384},... | collective-permute-start | bytes 12296 | tf_op jit(solution)/shard_map/ppermute | solution.py:24
  183.1 3.8 %collective-permute-done.29 = f32[1,4,256]{2,1,0:T(4,128)S(1)} collective-permute-done((f32[1,4,256]{2,1,0:T(4,128)S(1)}, f32[1,4,256]{2,1,0:T(4,128)S(1)}, u32[]{:S(2)}, u32[]{:S(2)}) %collective-permute-start.29) | collective-permute-done | bytes 4128 | tf_op jit(solution)/shard_map/ppermute | solution.py:23
  186.9 7.2 %collective-permute-start.30 = (f32[6,1,256]{2,1,0:T(1,128)S(1)}, f32[6,1,256]{2,1,0:T(1,128)S(1)}, u32[]{:S(2)}, u32[]{:S(2)}) collective-permute-start(f32[6,1,256]{2,1,0:T(1,128)S(1)} %get-tuple-element.45), channel_id=1, source_target_pairs={{1,0},{2,1},{3,2},{4,3},{5,4},{6,5},{7,6},{8,7},{9,8},{10,9},{11,1... | collective-permute-start | bytes 18440 | tf_op jit(solution)/shard_map/ppermute | solution.py:24
  196.1 6.8 %collective-permute-done.31 = f32[6,1,256]{2,1,0:T(1,128)S(1)} collective-permute-done((f32[6,1,256]{2,1,0:T(1,128)S(1)}, f32[6,1,256]{2,1,0:T(1,128)S(1)}, u32[]{:S(2)}, u32[]{:S(2)}) %collective-permute-start.31) | collective-permute-done | bytes 6176 | tf_op jit(solution)/shard_map/ppermute | solution.py:23
  208.6 2.5 collective-permute-done.33
  213.1 3.9 %collective-permute-start.35 = (f32[6,1,256]{2,1,0:T(1,128)S(1)}, f32[6,1,256]{2,1,0:T(1,128)S(1)}, u32[]{:S(2)}, u32[]{:S(2)}) collective-permute-start(f32[6,1,256]{2,1,0:T(1,128)S(1)} %get-tuple-element.44), channel_id=1, source_target_pairs={{0,1},{1,2},{2,3},{3,4},{4,5},{5,6},{6,7},{7,8},{8,9},{9,10},{10,1... | collective-permute-start | bytes 18440 | tf_op jit(solution)/shard_map/ppermute | solution.py:23
  219.0 2.9 collective-permute-done.35
  226.4 3.7 %collective-permute-done.37 = f32[1,4,256]{2,1,0:T(4,128)S(1)} collective-permute-done((f32[1,4,256]{2,1,0:T(4,128)S(1)}, f32[1,4,256]{2,1,0:T(4,128)S(1)}, u32[]{:S(2)}, u32[]{:S(2)}) %collective-permute-start.37) | collective-permute-done | bytes 4128 | tf_op jit(solution)/shard_map/ppermute | solution.py:23
  230.1 4.3 %collective-permute-start.38 = (f32[6,1,256]{2,1,0:T(1,128)S(1)}, f32[6,1,256]{2,1,0:T(1,128)S(1)}, u32[]{:S(2)}, u32[]{:S(2)}) collective-permute-start(f32[6,1,256]{2,1,0:T(1,128)S(1)} %get-tuple-element.41), channel_id=1, source_target_pairs={{1,0},{2,1},{3,2},{4,3},{5,4},{6,5},{7,6},{8,7},{9,8},{10,9},{11,1... | collective-permute-start | bytes 18440 | tf_op jit(solution)/shard_map/ppermute | solution.py:24
  236.5 6.8 %collective-permute-done.39 = f32[6,1,256]{2,1,0:T(1,128)S(1)} collective-permute-done((f32[6,1,256]{2,1,0:T(1,128)S(1)}, f32[6,1,256]{2,1,0:T(1,128)S(1)}, u32[]{:S(2)}, u32[]{:S(2)}) %collective-permute-start.39) | collective-permute-done | bytes 6176 | tf_op jit(solution)/shard_map/ppermute | solution.py:23
  253.5 3.9 %collective-permute-start.43 = (f32[6,1,256]{2,1,0:T(1,128)S(1)}, f32[6,1,256]{2,1,0:T(1,128)S(1)}, u32[]{:S(2)}, u32[]{:S(2)}) collective-permute-start(f32[6,1,256]{2,1,0:T(1,128)S(1)} %get-tuple-element.40), channel_id=1, source_target_pairs={{0,1},{1,2},{2,3},{3,4},{4,5},{5,6},{6,7},{7,8},{8,9},{9,10},{10,1... | collective-permute-start | bytes 18440 | tf_op jit(solution)/shard_map/ppermute | solution.py:23
  259.6 2.7 collective-permute-done.43
  263.6 2.7 collective-permute-done.49
  270.7 3.7 %collective-permute-done.51 = f32[1,2,128]{2,1,0:T(2,128)S(1)} collective-permute-done((f32[1,2,128]{2,1,0:T(2,128)S(1)}, f32[1,2,128]{2,1,0:T(2,128)S(1)}, u32[]{:S(2)}, u32[]{:S(2)}) %collective-permute-start.51) | collective-permute-done | bytes 1056 | tf_op jit(solution)/shard_map/ppermute | solution.py:23
  276.3 3.9 %collective-permute-start.53 = (f32[4,1,128]{2,1,0:T(1,128)S(1)}, f32[4,1,128]{2,1,0:T(1,128)S(1)}, u32[]{:S(2)}, u32[]{:S(2)}) collective-permute-start(f32[4,1,128]{2,1,0:T(1,128)S(1)} %get-tuple-element.70), channel_id=1, source_target_pairs={{0,1},{1,2},{2,3},{3,4},{4,5},{5,6},{6,7},{7,8},{8,9},{9,10},{10,1... | collective-permute-start | bytes 6152 | tf_op jit(solution)/shard_map/ppermute | solution.py:23
  280.3 4.8 %collective-permute-done.53 = f32[4,1,128]{2,1,0:T(1,128)S(1)} collective-permute-done((f32[4,1,128]{2,1,0:T(1,128)S(1)}, f32[4,1,128]{2,1,0:T(1,128)S(1)}, u32[]{:S(2)}, u32[]{:S(2)}) %collective-permute-start.53) | collective-permute-done | bytes 2080 | tf_op jit(solution)/shard_map/ppermute | solution.py:23
  289.6 3.7 %collective-permute-done.55 = f32[1,2,128]{2,1,0:T(2,128)S(1)} collective-permute-done((f32[1,2,128]{2,1,0:T(2,128)S(1)}, f32[1,2,128]{2,1,0:T(2,128)S(1)}, u32[]{:S(2)}, u32[]{:S(2)}) %collective-permute-start.55) | collective-permute-done | bytes 1056 | tf_op jit(solution)/shard_map/ppermute | solution.py:23
  295.2 3.9 %collective-permute-start.57 = (f32[4,1,128]{2,1,0:T(1,128)S(1)}, f32[4,1,128]{2,1,0:T(1,128)S(1)}, u32[]{:S(2)}, u32[]{:S(2)}) collective-permute-start(f32[4,1,128]{2,1,0:T(1,128)S(1)} %get-tuple-element.68), channel_id=1, source_target_pairs={{0,1},{1,2},{2,3},{3,4},{4,5},{5,6},{6,7},{7,8},{8,9},{9,10},{10,1... | collective-permute-start | bytes 6152 | tf_op jit(solution)/shard_map/ppermute | solution.py:23
  299.2 4.8 %collective-permute-done.57 = f32[4,1,128]{2,1,0:T(1,128)S(1)} collective-permute-done((f32[4,1,128]{2,1,0:T(1,128)S(1)}, f32[4,1,128]{2,1,0:T(1,128)S(1)}, u32[]{:S(2)}, u32[]{:S(2)}) %collective-permute-start.57) | collective-permute-done | bytes 2080 | tf_op jit(solution)/shard_map/ppermute | solution.py:23
  308.4 3.7 %collective-permute-done.59 = f32[1,2,128]{2,1,0:T(2,128)S(1)} collective-permute-done((f32[1,2,128]{2,1,0:T(2,128)S(1)}, f32[1,2,128]{2,1,0:T(2,128)S(1)}, u32[]{:S(2)}, u32[]{:S(2)}) %collective-permute-start.59) | collective-permute-done | bytes 1056 | tf_op jit(solution)/shard_map/ppermute | solution.py:23
  314.1 3.9 %collective-permute-start.61 = (f32[4,1,128]{2,1,0:T(1,128)S(1)}, f32[4,1,128]{2,1,0:T(1,128)S(1)}, u32[]{:S(2)}, u32[]{:S(2)}) collective-permute-start(f32[4,1,128]{2,1,0:T(1,128)S(1)} %get-tuple-element.66), channel_id=1, source_target_pairs={{0,1},{1,2},{2,3},{3,4},{4,5},{5,6},{6,7},{7,8},{8,9},{9,10},{10,1... | collective-permute-start | bytes 6152 | tf_op jit(solution)/shard_map/ppermute | solution.py:23
  318.1 4.8 %collective-permute-done.61 = f32[4,1,128]{2,1,0:T(1,128)S(1)} collective-permute-done((f32[4,1,128]{2,1,0:T(1,128)S(1)}, f32[4,1,128]{2,1,0:T(1,128)S(1)}, u32[]{:S(2)}, u32[]{:S(2)}) %collective-permute-start.61) | collective-permute-done | bytes 2080 | tf_op jit(solution)/shard_map/ppermute | solution.py:23
  (199 shorter events, 101.3 us)
Async XLA Ops:
  1.4 43.0 %collective-permute-start.2 = (f32[1,8,512]{2,1,0:T(8,128)S(1)}, f32[1,8,512]{2,1,0:T(8,128)S(1)}, u32[]{:S(2)}, u32[]{:S(2)}) collective-permute-start(f32[1,8,512]{2,1,0:T(8,128)S(1)} %get-tuple-element.38), channel_id=1, source_target_pairs={{0,64},{64,128},{128,192},{192,256},{256,320},{320,384},{384,448},... | collective-permute-start | bytes 49160 | tf_op jit(solution)/shard_map/ppermute | solution.py:23
  3.3 41.1 %collective-permute-start = (f32[1,8,512]{2,1,0:T(8,128)S(1)}, f32[1,8,512]{2,1,0:T(8,128)S(1)}, u32[]{:S(2)}, u32[]{:S(2)}) collective-permute-start(f32[1,8,512]{2,1,0:T(8,128)S(1)} %get-tuple-element.37), channel_id=1, source_target_pairs={{64,0},{128,64},{192,128},{256,192},{320,256},{384,320},{448,384},... | collective-permute-start | bytes 49160 | tf_op jit(solution)/shard_map/ppermute | solution.py:24
  8.9 52.4 %collective-permute-start.1 = (f32[1,8,512]{2,1,0:T(8,128)S(1)}, f32[1,8,512]{2,1,0:T(8,128)S(1)}, u32[]{:S(2)}, u32[]{:S(2)}) collective-permute-start(f32[1,8,512]{2,1,0:T(8,128)S(1)} %slice.668), channel_id=1, source_target_pairs={{0,64},{64,128},{128,192},{192,256},{256,320},{320,384},{384,448},... | collective-permute-start | bytes 49160 | tf_op jit(solution)/shard_map/ppermute | solution.py:13
  11.7 51.5 %collective-permute-start.4 = (f32[8,1,512]{2,1,0:T(1,128)S(1)}, f32[8,1,512]{2,1,0:T(1,128)S(1)}, u32[]{:S(2)}, u32[]{:S(2)}) collective-permute-start(f32[8,1,512]{2,1,0:T(1,128)S(1)} %slice.671), channel_id=1, source_target_pairs={{0,1},{1,2},{2,3},{3,4},{4,5},{5,6},{6,7},{7,8},{8,9},{9,10},{10,1... | collective-permute-start | bytes 49160 | tf_op jit(solution)/shard_map/ppermute | solution.py:13
  16.9 117.0 %collective-permute-start.22 = (f32[1,4,256]{2,1,0:T(4,128)S(1)}, f32[1,4,256]{2,1,0:T(4,128)S(1)}, u32[]{:S(2)}, u32[]{:S(2)}) collective-permute-start(f32[1,4,256]{2,1,0:T(4,128)S(1)} %broadcast.134), channel_id=1, source_target_pairs={{64,0},{128,64},{192,128},{256,192},{320,256},{384,320},{448,384},... | collective-permute-start | bytes 12296 | tf_op jit(solution)/shard_map/ppermute | solution.py:24
  44.5 20.7 %collective-permute-start.3 = (f32[10,1,512]{2,1,0:T(1,128)S(1)}, f32[10,1,512]{2,1,0:T(1,128)S(1)}, u32[]{:S(2)}, u32[]{:S(2)}) collective-permute-start(f32[10,1,512]{2,1,0:T(1,128)S(1)} %get-tuple-element.17), channel_id=1, source_target_pairs={{1,0},{2,1},{3,2},{4,3},{5,4},{6,5},{7,6},{8,7},{9,8},{10,9},{11,1... | collective-permute-start | bytes 61448 | tf_op jit(solution)/shard_map/ppermute | solution.py:24
  58.6 9.0 %collective-permute-start.5 = (f32[10,1,512]{2,1,0:T(1,128)S(1)}, f32[10,1,512]{2,1,0:T(1,128)S(1)}, u32[]{:S(2)}, u32[]{:S(2)}) collective-permute-start(f32[10,1,512]{2,1,0:T(1,128)S(1)} %get-tuple-element.18), channel_id=1, source_target_pairs={{0,1},{1,2},{2,3},{3,4},{4,5},{5,6},{6,7},{7,8},{8,9},{9,10},{10,1... | collective-permute-start | bytes 61448 | tf_op jit(solution)/shard_map/ppermute | solution.py:23
  61.3 74.6 %collective-permute-start.24 = (f32[1,4,256]{2,1,0:T(4,128)S(1)}, f32[1,4,256]{2,1,0:T(4,128)S(1)}, u32[]{:S(2)}, u32[]{:S(2)}) collective-permute-start(f32[1,4,256]{2,1,0:T(4,128)S(1)} %broadcast.134), channel_id=1, source_target_pairs={{0,64},{64,128},{128,192},{192,256},{256,320},{320,384},{384,448},... | collective-permute-start | bytes 12296 | tf_op jit(solution)/shard_map/ppermute | solution.py:23
  63.2 108.6 %collective-permute-start.23 = (f32[1,4,256]{2,1,0:T(4,128)S(1)}, f32[1,4,256]{2,1,0:T(4,128)S(1)}, u32[]{:S(2)}, u32[]{:S(2)}) collective-permute-start(f32[1,4,256]{2,1,0:T(4,128)S(1)} %slice.691), channel_id=1, source_target_pairs={{0,64},{64,128},{128,192},{192,256},{256,320},{320,384},{384,448},... | collective-permute-start | bytes 12296 | tf_op jit(solution)/shard_map/ppermute | solution.py:13
  70.3 6.3 %collective-permute-start.7 = (f32[1,8,512]{2,1,0:T(8,128)S(1)}, f32[1,8,512]{2,1,0:T(8,128)S(1)}, u32[]{:S(2)}, u32[]{:S(2)}) collective-permute-start(f32[1,8,512]{2,1,0:T(8,128)S(1)} %get-tuple-element.33), channel_id=1, source_target_pairs={{0,64},{64,128},{128,192},{192,256},{256,320},{320,384},{384,448},... | collective-permute-start | bytes 49160 | tf_op jit(solution)/shard_map/ppermute | solution.py:23
  76.6 9.3 %collective-permute-start.8 = (f32[10,1,512]{2,1,0:T(1,128)S(1)}, f32[10,1,512]{2,1,0:T(1,128)S(1)}, u32[]{:S(2)}, u32[]{:S(2)}) collective-permute-start(f32[10,1,512]{2,1,0:T(1,128)S(1)} %get-tuple-element.15), channel_id=1, source_target_pairs={{1,0},{2,1},{3,2},{4,3},{5,4},{6,5},{7,6},{8,7},{9,8},{10,9},{11,1... | collective-permute-start | bytes 61448 | tf_op jit(solution)/shard_map/ppermute | solution.py:24
  83.9 9.0 %collective-permute-start.9 = (f32[10,1,512]{2,1,0:T(1,128)S(1)}, f32[10,1,512]{2,1,0:T(1,128)S(1)}, u32[]{:S(2)}, u32[]{:S(2)}) collective-permute-start(f32[10,1,512]{2,1,0:T(1,128)S(1)} %get-tuple-element.16), channel_id=1, source_target_pairs={{0,1},{1,2},{2,3},{3,4},{4,5},{5,6},{6,7},{7,8},{8,9},{9,10},{10,1... | collective-permute-start | bytes 61448 | tf_op jit(solution)/shard_map/ppermute | solution.py:23
  95.1 6.3 %collective-permute-start.11 = (f32[1,8,512]{2,1,0:T(8,128)S(1)}, f32[1,8,512]{2,1,0:T(8,128)S(1)}, u32[]{:S(2)}, u32[]{:S(2)}) collective-permute-start(f32[1,8,512]{2,1,0:T(8,128)S(1)} %get-tuple-element.29), channel_id=1, source_target_pairs={{0,64},{64,128},{128,192},{192,256},{256,320},{320,384},{384,448},... | collective-permute-start | bytes 49160 | tf_op jit(solution)/shard_map/ppermute | solution.py:23
  101.4 6.0 %collective-permute-start.12 = (f32[10,1,512]{2,1,0:T(1,128)S(1)}, f32[10,1,512]{2,1,0:T(1,128)S(1)}, u32[]{:S(2)}, u32[]{:S(2)}) collective-permute-start(f32[10,1,512]{2,1,0:T(1,128)S(1)} %get-tuple-element.13), channel_id=1, source_target_pairs={{1,0},{2,1},{3,2},{4,3},{5,4},{6,5},{7,6},{8,7},{9,8},{10,9},{11,1... | collective-permute-start | bytes 61448 | tf_op jit(solution)/shard_map/ppermute | solution.py:24
  103.3 9.0 %collective-permute-start.13 = (f32[10,1,512]{2,1,0:T(1,128)S(1)}, f32[10,1,512]{2,1,0:T(1,128)S(1)}, u32[]{:S(2)}, u32[]{:S(2)}) collective-permute-start(f32[10,1,512]{2,1,0:T(1,128)S(1)} %get-tuple-element.14), channel_id=1, source_target_pairs={{0,1},{1,2},{2,3},{3,4},{4,5},{5,6},{6,7},{7,8},{8,9},{9,10},{10,1... | collective-permute-start | bytes 61448 | tf_op jit(solution)/shard_map/ppermute | solution.py:23
  114.5 6.3 %collective-permute-start.15 = (f32[1,8,512]{2,1,0:T(8,128)S(1)}, f32[1,8,512]{2,1,0:T(8,128)S(1)}, u32[]{:S(2)}, u32[]{:S(2)}) collective-permute-start(f32[1,8,512]{2,1,0:T(8,128)S(1)} %get-tuple-element.25), channel_id=1, source_target_pairs={{0,64},{64,128},{128,192},{192,256},{256,320},{320,384},{384,448},... | collective-permute-start | bytes 49160 | tf_op jit(solution)/shard_map/ppermute | solution.py:23
  120.8 6.0 %collective-permute-start.16 = (f32[10,1,512]{2,1,0:T(1,128)S(1)}, f32[10,1,512]{2,1,0:T(1,128)S(1)}, u32[]{:S(2)}, u32[]{:S(2)}) collective-permute-start(f32[10,1,512]{2,1,0:T(1,128)S(1)} %get-tuple-element.11), channel_id=1, source_target_pairs={{1,0},{2,1},{3,2},{4,3},{5,4},{6,5},{7,6},{8,7},{9,8},{10,9},{11,1... | collective-permute-start | bytes 61448 | tf_op jit(solution)/shard_map/ppermute | solution.py:24
  122.7 9.0 %collective-permute-start.17 = (f32[10,1,512]{2,1,0:T(1,128)S(1)}, f32[10,1,512]{2,1,0:T(1,128)S(1)}, u32[]{:S(2)}, u32[]{:S(2)}) collective-permute-start(f32[10,1,512]{2,1,0:T(1,128)S(1)} %get-tuple-element.12), channel_id=1, source_target_pairs={{0,1},{1,2},{2,3},{3,4},{4,5},{5,6},{6,7},{7,8},{8,9},{9,10},{10,1... | collective-permute-start | bytes 61448 | tf_op jit(solution)/shard_map/ppermute | solution.py:23
  126.8 47.0 %collective-permute-start.26 = (f32[4,1,256]{2,1,0:T(1,128)S(1)}, f32[4,1,256]{2,1,0:T(1,128)S(1)}, u32[]{:S(2)}, u32[]{:S(2)}) collective-permute-start(f32[4,1,256]{2,1,0:T(1,128)S(1)} %slice.693), channel_id=1, source_target_pairs={{0,1},{1,2},{2,3},{3,4},{4,5},{5,6},{6,7},{7,8},{8,9},{9,10},{10,1... | collective-permute-start | bytes 12296 | tf_op jit(solution)/shard_map/ppermute | solution.py:13
  131.7 92.3 %collective-permute-start.44 = (f32[1,2,128]{2,1,0:T(2,128)S(1)}, f32[1,2,128]{2,1,0:T(2,128)S(1)}, u32[]{:S(2)}, u32[]{:S(2)}) collective-permute-start(f32[1,2,128]{2,1,0:T(2,128)S(1)} %broadcast.138), channel_id=1, source_target_pairs={{64,0},{128,64},{192,128},{256,192},{320,256},{384,320},{448,384},... | collective-permute-start | bytes 3080 | tf_op jit(solution)/shard_map/ppermute | solution.py:24
  135.9 6.3 %collective-permute-start.19 = (f32[1,8,512]{2,1,0:T(8,128)S(1)}, f32[1,8,512]{2,1,0:T(8,128)S(1)}, u32[]{:S(2)}, u32[]{:S(2)}) collective-permute-start(f32[1,8,512]{2,1,0:T(8,128)S(1)} %get-tuple-element.21), channel_id=1, source_target_pairs={{0,64},{64,128},{128,192},{192,256},{256,320},{320,384},{384,448},... | collective-permute-start | bytes 49160 | tf_op jit(solution)/shard_map/ppermute | solution.py:23
  142.2 6.3 %collective-permute-start.20 = (f32[10,1,512]{2,1,0:T(1,128)S(1)}, f32[10,1,512]{2,1,0:T(1,128)S(1)}, u32[]{:S(2)}, u32[]{:S(2)}) collective-permute-start(f32[10,1,512]{2,1,0:T(1,128)S(1)} %get-tuple-element.9), channel_id=1, source_target_pairs={{1,0},{2,1},{3,2},{4,3},{5,4},{6,5},{7,6},{8,7},{9,8},{10,9},{11,1... | collective-permute-start | bytes 61448 | tf_op jit(solution)/shard_map/ppermute | solution.py:24
  146.4 9.3 %collective-permute-start.21 = (f32[10,1,512]{2,1,0:T(1,128)S(1)}, f32[10,1,512]{2,1,0:T(1,128)S(1)}, u32[]{:S(2)}, u32[]{:S(2)}) collective-permute-start(f32[10,1,512]{2,1,0:T(1,128)S(1)} %get-tuple-element.10), channel_id=1, source_target_pairs={{0,1},{1,2},{2,3},{3,4},{4,5},{5,6},{6,7},{7,8},{8,9},{9,10},{10,1... | collective-permute-start | bytes 61448 | tf_op jit(solution)/shard_map/ppermute | solution.py:23
  148.5 28.3 %collective-permute-start.25 = (f32[6,1,256]{2,1,0:T(1,128)S(1)}, f32[6,1,256]{2,1,0:T(1,128)S(1)}, u32[]{:S(2)}, u32[]{:S(2)}) collective-permute-start(f32[6,1,256]{2,1,0:T(1,128)S(1)} %get-tuple-element.47), channel_id=1, source_target_pairs={{1,0},{2,1},{3,2},{4,3},{5,4},{6,5},{7,6},{8,7},{9,8},{10,9},{11,1... | collective-permute-start | bytes 18440 | tf_op jit(solution)/shard_map/ppermute | solution.py:24
  155.7 21.0 %collective-permute-start.27 = (f32[6,1,256]{2,1,0:T(1,128)S(1)}, f32[6,1,256]{2,1,0:T(1,128)S(1)}, u32[]{:S(2)}, u32[]{:S(2)}) collective-permute-start(f32[6,1,256]{2,1,0:T(1,128)S(1)} %get-tuple-element.48), channel_id=1, source_target_pairs={{0,1},{1,2},{2,3},{3,4},{4,5},{5,6},{6,7},{7,8},{8,9},{9,10},{10,1... | collective-permute-start | bytes 18440 | tf_op jit(solution)/shard_map/ppermute | solution.py:23
  171.9 54.5 %collective-permute-start.46 = (f32[1,2,128]{2,1,0:T(2,128)S(1)}, f32[1,2,128]{2,1,0:T(2,128)S(1)}, u32[]{:S(2)}, u32[]{:S(2)}) collective-permute-start(f32[1,2,128]{2,1,0:T(2,128)S(1)} %broadcast.138), channel_id=1, source_target_pairs={{0,64},{64,128},{128,192},{192,256},{256,320},{320,384},{384,448},... | collective-permute-start | bytes 3080 | tf_op jit(solution)/shard_map/ppermute | solution.py:23
  173.8 89.8 %collective-permute-start.45 = (f32[1,2,128]{2,1,0:T(2,128)S(1)}, f32[1,2,128]{2,1,0:T(2,128)S(1)}, u32[]{:S(2)}, u32[]{:S(2)}) collective-permute-start(f32[1,2,128]{2,1,0:T(2,128)S(1)} %get-tuple-element.85), channel_id=1, source_target_pairs={{0,64},{64,128},{128,192},{192,256},{256,320},{320,384},{384,448},... | collective-permute-start | bytes 3080 | tf_op jit(solution)/shard_map/ppermute | solution.py:13
  176.9 6.2 %collective-permute-start.28 = (f32[1,4,256]{2,1,0:T(4,128)S(1)}, f32[1,4,256]{2,1,0:T(4,128)S(1)}, u32[]{:S(2)}, u32[]{:S(2)}) collective-permute-start(f32[1,4,256]{2,1,0:T(4,128)S(1)} %get-tuple-element.64), channel_id=1, source_target_pairs={{64,0},{128,64},{192,128},{256,192},{320,256},{384,320},{448,384},... | collective-permute-start | bytes 12296 | tf_op jit(solution)/shard_map/ppermute | solution.py:24
  180.7 6.1 %collective-permute-start.29 = (f32[1,4,256]{2,1,0:T(4,128)S(1)}, f32[1,4,256]{2,1,0:T(4,128)S(1)}, u32[]{:S(2)}, u32[]{:S(2)}) collective-permute-start(f32[1,4,256]{2,1,0:T(4,128)S(1)} %get-tuple-element.63), channel_id=1, source_target_pairs={{0,64},{64,128},{128,192},{192,256},{256,320},{320,384},{384,448},... | collective-permute-start | bytes 12296 | tf_op jit(solution)/shard_map/ppermute | solution.py:23
  186.9 9.3 %collective-permute-start.30 = (f32[6,1,256]{2,1,0:T(1,128)S(1)}, f32[6,1,256]{2,1,0:T(1,128)S(1)}, u32[]{:S(2)}, u32[]{:S(2)}) collective-permute-start(f32[6,1,256]{2,1,0:T(1,128)S(1)} %get-tuple-element.45), channel_id=1, source_target_pairs={{1,0},{2,1},{3,2},{4,3},{5,4},{6,5},{7,6},{8,7},{9,8},{10,9},{11,1... | collective-permute-start | bytes 18440 | tf_op jit(solution)/shard_map/ppermute | solution.py:24
  194.1 8.8 %collective-permute-start.31 = (f32[6,1,256]{2,1,0:T(1,128)S(1)}, f32[6,1,256]{2,1,0:T(1,128)S(1)}, u32[]{:S(2)}, u32[]{:S(2)}) collective-permute-start(f32[6,1,256]{2,1,0:T(1,128)S(1)} %get-tuple-element.46), channel_id=1, source_target_pairs={{0,1},{1,2},{2,3},{3,4},{4,5},{5,6},{6,7},{7,8},{8,9},{9,10},{10,1... | collective-permute-start | bytes 18440 | tf_op jit(solution)/shard_map/ppermute | solution.py:23
  205.0 6.1 %collective-permute-start.33 = (f32[1,4,256]{2,1,0:T(4,128)S(1)}, f32[1,4,256]{2,1,0:T(4,128)S(1)}, u32[]{:S(2)}, u32[]{:S(2)}) collective-permute-start(f32[1,4,256]{2,1,0:T(4,128)S(1)} %get-tuple-element.59), channel_id=1, source_target_pairs={{0,64},{64,128},{128,192},{192,256},{256,320},{320,384},{384,448},... | collective-permute-start | bytes 12296 | tf_op jit(solution)/shard_map/ppermute | solution.py:23
  213.1 8.8 %collective-permute-start.35 = (f32[6,1,256]{2,1,0:T(1,128)S(1)}, f32[6,1,256]{2,1,0:T(1,128)S(1)}, u32[]{:S(2)}, u32[]{:S(2)}) collective-permute-start(f32[6,1,256]{2,1,0:T(1,128)S(1)} %get-tuple-element.44), channel_id=1, source_target_pairs={{0,1},{1,2},{2,3},{3,4},{4,5},{5,6},{6,7},{7,8},{8,9},{9,10},{10,1... | collective-permute-start | bytes 18440 | tf_op jit(solution)/shard_map/ppermute | solution.py:23
  217.1 46.5 %collective-permute-start.48 = (f32[2,1,128]{2,1,0:T(1,128)S(1)}, f32[2,1,128]{2,1,0:T(1,128)S(1)}, u32[]{:S(2)}, u32[]{:S(2)}) collective-permute-start(f32[2,1,128]{2,1,0:T(1,128)S(1)} %get-tuple-element.87), channel_id=1, source_target_pairs={{0,1},{1,2},{2,3},{3,4},{4,5},{5,6},{6,7},{7,8},{8,9},{9,10},{10,1... | collective-permute-start | bytes 3080 | tf_op jit(solution)/shard_map/ppermute | solution.py:13
  224.0 6.1 %collective-permute-start.37 = (f32[1,4,256]{2,1,0:T(4,128)S(1)}, f32[1,4,256]{2,1,0:T(4,128)S(1)}, u32[]{:S(2)}, u32[]{:S(2)}) collective-permute-start(f32[1,4,256]{2,1,0:T(4,128)S(1)} %get-tuple-element.55), channel_id=1, source_target_pairs={{0,64},{64,128},{128,192},{192,256},{256,320},{320,384},{384,448},... | collective-permute-start | bytes 12296 | tf_op jit(solution)/shard_map/ppermute | solution.py:23
  230.1 6.4 %collective-permute-start.38 = (f32[6,1,256]{2,1,0:T(1,128)S(1)}, f32[6,1,256]{2,1,0:T(1,128)S(1)}, u32[]{:S(2)}, u32[]{:S(2)}) collective-permute-start(f32[6,1,256]{2,1,0:T(1,128)S(1)} %get-tuple-element.41), channel_id=1, source_target_pairs={{1,0},{2,1},{3,2},{4,3},{5,4},{6,5},{7,6},{8,7},{9,8},{10,9},{11,1... | collective-permute-start | bytes 18440 | tf_op jit(solution)/shard_map/ppermute | solution.py:24
  234.5 8.8 %collective-permute-start.39 = (f32[6,1,256]{2,1,0:T(1,128)S(1)}, f32[6,1,256]{2,1,0:T(1,128)S(1)}, u32[]{:S(2)}, u32[]{:S(2)}) collective-permute-start(f32[6,1,256]{2,1,0:T(1,128)S(1)} %get-tuple-element.42), channel_id=1, source_target_pairs={{0,1},{1,2},{2,3},{3,4},{4,5},{5,6},{6,7},{7,8},{8,9},{9,10},{10,1... | collective-permute-start | bytes 18440 | tf_op jit(solution)/shard_map/ppermute | solution.py:23
  243.5 6.3 %collective-permute-start.40 = (f32[1,4,256]{2,1,0:T(4,128)S(1)}, f32[1,4,256]{2,1,0:T(4,128)S(1)}, u32[]{:S(2)}, u32[]{:S(2)}) collective-permute-start(f32[1,4,256]{2,1,0:T(4,128)S(1)} %get-tuple-element.52), channel_id=1, source_target_pairs={{64,0},{128,64},{192,128},{256,192},{320,256},{384,320},{448,384},... | collective-permute-start | bytes 12296 | tf_op jit(solution)/shard_map/ppermute | solution.py:24
  245.4 6.1 %collective-permute-start.41 = (f32[1,4,256]{2,1,0:T(4,128)S(1)}, f32[1,4,256]{2,1,0:T(4,128)S(1)}, u32[]{:S(2)}, u32[]{:S(2)}) collective-permute-start(f32[1,4,256]{2,1,0:T(4,128)S(1)} %get-tuple-element.51), channel_id=1, source_target_pairs={{0,64},{64,128},{128,192},{192,256},{256,320},{320,384},{384,448},... | collective-permute-start | bytes 12296 | tf_op jit(solution)/shard_map/ppermute | solution.py:23
  247.8 15.8 %collective-permute-start.47 = (f32[4,1,128]{2,1,0:T(1,128)S(1)}, f32[4,1,128]{2,1,0:T(1,128)S(1)}, u32[]{:S(2)}, u32[]{:S(2)}) collective-permute-start(f32[4,1,128]{2,1,0:T(1,128)S(1)} %get-tuple-element.71), channel_id=1, source_target_pairs={{1,0},{2,1},{3,2},{4,3},{5,4},{6,5},{7,6},{8,7},{9,8},{10,9},{11,1... | collective-permute-start | bytes 6152 | tf_op jit(solution)/shard_map/ppermute | solution.py:24
  253.5 8.8 %collective-permute-start.43 = (f32[6,1,256]{2,1,0:T(1,128)S(1)}, f32[6,1,256]{2,1,0:T(1,128)S(1)}, u32[]{:S(2)}, u32[]{:S(2)}) collective-permute-start(f32[6,1,256]{2,1,0:T(1,128)S(1)} %get-tuple-element.40), channel_id=1, source_target_pairs={{0,1},{1,2},{2,3},{3,4},{4,5},{5,6},{6,7},{7,8},{8,9},{9,10},{10,1... | collective-permute-start | bytes 18440 | tf_op jit(solution)/shard_map/ppermute | solution.py:23
  257.5 8.8 %collective-permute-start.49 = (f32[4,1,128]{2,1,0:T(1,128)S(1)}, f32[4,1,128]{2,1,0:T(1,128)S(1)}, u32[]{:S(2)}, u32[]{:S(2)}) collective-permute-start(f32[4,1,128]{2,1,0:T(1,128)S(1)} %get-tuple-element.72), channel_id=1, source_target_pairs={{0,1},{1,2},{2,3},{3,4},{4,5},{5,6},{6,7},{7,8},{8,9},{9,10},{10,1... | collective-permute-start | bytes 6152 | tf_op jit(solution)/shard_map/ppermute | solution.py:23
  268.3 6.1 %collective-permute-start.51 = (f32[1,2,128]{2,1,0:T(2,128)S(1)}, f32[1,2,128]{2,1,0:T(2,128)S(1)}, u32[]{:S(2)}, u32[]{:S(2)}) collective-permute-start(f32[1,2,128]{2,1,0:T(2,128)S(1)} %get-tuple-element.82), channel_id=1, source_target_pairs={{0,64},{64,128},{128,192},{192,256},{256,320},{320,384},{384,448},... | collective-permute-start | bytes 3080 | tf_op jit(solution)/shard_map/ppermute | solution.py:23
  276.3 8.8 %collective-permute-start.53 = (f32[4,1,128]{2,1,0:T(1,128)S(1)}, f32[4,1,128]{2,1,0:T(1,128)S(1)}, u32[]{:S(2)}, u32[]{:S(2)}) collective-permute-start(f32[4,1,128]{2,1,0:T(1,128)S(1)} %get-tuple-element.70), channel_id=1, source_target_pairs={{0,1},{1,2},{2,3},{3,4},{4,5},{5,6},{6,7},{7,8},{8,9},{9,10},{10,1... | collective-permute-start | bytes 6152 | tf_op jit(solution)/shard_map/ppermute | solution.py:23
  287.2 6.1 %collective-permute-start.55 = (f32[1,2,128]{2,1,0:T(2,128)S(1)}, f32[1,2,128]{2,1,0:T(2,128)S(1)}, u32[]{:S(2)}, u32[]{:S(2)}) collective-permute-start(f32[1,2,128]{2,1,0:T(2,128)S(1)} %get-tuple-element.78), channel_id=1, source_target_pairs={{0,64},{64,128},{128,192},{192,256},{256,320},{320,384},{384,448},... | collective-permute-start | bytes 3080 | tf_op jit(solution)/shard_map/ppermute | solution.py:23
  295.2 8.8 %collective-permute-start.57 = (f32[4,1,128]{2,1,0:T(1,128)S(1)}, f32[4,1,128]{2,1,0:T(1,128)S(1)}, u32[]{:S(2)}, u32[]{:S(2)}) collective-permute-start(f32[4,1,128]{2,1,0:T(1,128)S(1)} %get-tuple-element.68), channel_id=1, source_target_pairs={{0,1},{1,2},{2,3},{3,4},{4,5},{5,6},{6,7},{7,8},{8,9},{9,10},{10,1... | collective-permute-start | bytes 6152 | tf_op jit(solution)/shard_map/ppermute | solution.py:23
  306.0 6.1 %collective-permute-start.59 = (f32[1,2,128]{2,1,0:T(2,128)S(1)}, f32[1,2,128]{2,1,0:T(2,128)S(1)}, u32[]{:S(2)}, u32[]{:S(2)}) collective-permute-start(f32[1,2,128]{2,1,0:T(2,128)S(1)} %get-tuple-element.74), channel_id=1, source_target_pairs={{0,64},{64,128},{128,192},{192,256},{256,320},{320,384},{384,448},... | collective-permute-start | bytes 3080 | tf_op jit(solution)/shard_map/ppermute | solution.py:23
  314.1 8.8 %collective-permute-start.61 = (f32[4,1,128]{2,1,0:T(1,128)S(1)}, f32[4,1,128]{2,1,0:T(1,128)S(1)}, u32[]{:S(2)}, u32[]{:S(2)}) collective-permute-start(f32[4,1,128]{2,1,0:T(1,128)S(1)} %get-tuple-element.66), channel_id=1, source_target_pairs={{0,1},{1,2},{2,3},{3,4},{4,5},{5,6},{6,7},{7,8},{8,9},{9,10},{10,1... | collective-permute-start | bytes 6152 | tf_op jit(solution)/shard_map/ppermute | solution.py:23
  (22 other events, 358.2 us)
where the time goes:
time: 326 us; the launch traced here: 324 us
  starting transfers between devices  183 us (56%)
  waiting for transfers between devices  91.7 us (28%)
  local copies, waits for them, and re-layouts  31.9 us (10%)
  other arithmetic  15 us (5%)
    ppermute x28, starting transfers between devices, padded_2(): after = lax.ppermute(first, axis, down)  94.7 us
    ppermute x28, waiting for transfers between devices, padded_2(): before = lax.ppermute(last, axis, up)  91.6 us
    ppermute x28, starting transfers between devices, padded_2(): before = lax.ppermute(last, axis, up)  72.6 us
    reshape x3, local copies, waits for them, and re-layouts, coarsen_cells(): field.reshape(nx // 2, 2, ny // 2, 2, nz // 2, 2).mean(axis=(1, 3, 5))  20.5 us
    ppermute x6, starting transfers between devices, from_behind(): return lax.ppermute(block, axis, route)  15.8 us
    reduce_sum x4, other arithmetic, coarsen_cells(): field.reshape(nx // 2, 2, ny // 2, 2, nz // 2, 2).mean(axis=(1, 3, 5))  8.36 us
  transfers between devices with their start and end apart: 62, of which 23 were waited for; matrix products, arithmetic and copies ran while one was open for 14% of the time, Pallas kernels for 0%

commit v1 on v0

v1 whole, which is shorter than its diff:
```python
import jax
import jax.numpy as jnp
from jax import lax
from jax.experimental import pallas as pl
from jax.experimental.pallas import tpu as pltpu
from jax.sharding import PartitionSpec as P

F32 = jnp.float32
BF16 = jnp.bfloat16

U, F, A, BX, BY, BZ = range(6)
PAIRS = ((U, F), (A, BY), (BX, BZ))
H = 4


def iota(shape, dim):
    return lax.broadcasted_iota(jnp.int32, shape, dim)


def call(body, outs, args, scratch=(), flops=1_000_000, nbytes=2_000_000):
    vmem = pl.BlockSpec(memory_space=pltpu.VMEM)
    return pl.pallas_call(
        body,
        out_shape=outs,
        in_specs=[vmem] * len(args),
        out_specs=jax.tree.map(lambda _: vmem, outs),
        scratch_shapes=list(scratch),
        compiler_params=pltpu.CompilerParams(vmem_limit_bytes=48 << 20),
        cost_estimate=pl.CostEstimate(flops=flops, bytes_accessed=nbytes, transcendentals=0),
    )(*args)


def pair_low(first, second):
    return jnp.where(iota(first.shape, 0) < 4, first, pltpu.roll(second, 4, 0))


def pair_high(first, second):
    return jnp.where(iota(first.shape, 0) >= 4, first, pltpu.roll(second, 4, 0))


def pack_body(u, f, a, bx, by, bz, xl, xh, yl, yh):
    fields = (u, f, a, bx, by, bz)
    cut = bx[3].astype(F32)
    for k, ref in enumerate(fields):
        for j in range(H):
            low, high = ref[j].astype(F32), ref[4 + j].astype(F32)
            if j == 3:
                if k == F:
                    low = low + cut * u[4]
                elif k == A:
                    low = low + cut
                elif k == BX:
                    low = jnp.zeros_like(low)
            if j == 0:
                if k == F:
                    high = high + cut * u[3]
                elif k == A:
                    high = high + cut
            xl[k * H + j] = low
            xh[k * H + j] = high
    row = iota(u.shape[1:], 0)
    for p in range(u.shape[0]):
        v = [ref[p].astype(F32) for ref in fields]
        face = v[BY]
        low = list(v)
        low[F] = v[F] + jnp.where(row == 3, face * pltpu.roll(v[U], 7, 0), 0.0)
        low[A] = v[A] + jnp.where(row == 3, face, 0.0)
        low[BY] = jnp.where(row == 3, 0.0, face)
        high = list(v)
        below = pltpu.roll(face, 1, 0)
        high[F] = v[F] + jnp.where(row == 4, below * pltpu.roll(v[U], 1, 0), 0.0)
        high[A] = v[A] + jnp.where(row == 4, below, 0.0)
        for n, (i, j) in enumerate(PAIRS):
            yl[n * 8 + p] = pair_low(low[i], low[j])
            yh[n * 8 + p] = pair_high(high[i], high[j])


def corner_body(xlr, xhr, ycl, ych):
    for p in range(8):
        v = [xhr[k * H + p] if p < 4 else xlr[k * H + p - 4] for k in range(6)]
        for n, (i, j) in enumerate(PAIRS):
            ycl[n * 8 + p] = pair_low(v[i], v[j])
            ych[n * 8 + p] = pair_high(v[i], v[j])


def halves(n):
    row, col = iota((n, n // 2), 0), iota((n, n // 2), 1)
    both = jnp.where(row // 2 == col, 1.0, 0.0).astype(BF16)
    odd = jnp.where(row == 2 * col + 1, 1.0, 0.0).astype(BF16)
    return both, odd


def exact_dot(x, m):
    n = x.shape[0]
    one = x.astype(BF16)
    rest = x - one.astype(F32)
    two = rest.astype(BF16)
    three = (rest - two.astype(F32)).astype(BF16)
    y = jnp.dot(
        jnp.concatenate([one.astype(F32), two.astype(F32), three.astype(F32)], axis=0).astype(BF16),
        m,
        preferred_element_type=F32,
    )
    return (y[2 * n :] + y[n : 2 * n]) + y[:n]


def put(ref, at, x):
    for g in range(x.shape[1] // 128):
        ref[g, at : at + x.shape[0]] = x[:, 128 * g : 128 * g + 128]


def every_other(ref, first, n, width):
    return jnp.concatenate([ref[g, pl.ds(first, n, 2)] for g in range(width // 128)], axis=1)


def below_z(face):
    return jnp.where(iota(face.shape, face.ndim - 1) == 0, 0.0, pltpu.roll(face, 1, face.ndim - 1))


def coarse_body(a, bx, by, bz, xhr, yhr, c1, c2, rows, edge, fine, small):
    nz = a.shape[2]
    both, odd = halves(nz)
    both2, odd2 = halves(nz // 2)

    def even_odd(n):
        return every_other(rows, 0, n, nz), every_other(rows, 1, n, nz)

    def pairs(ref):
        for i in range(4):
            put(rows, 8 * i, ref[2 * i].astype(F32) + ref[2 * i + 1].astype(F32))
        return even_odd(16)

    e, o = pairs(a)
    a_in = e + o
    e, o = pairs(bz)
    bz_in = e + o
    e, o = pairs(by)
    by_in = o
    for i in range(4):
        put(rows, 8 * i, bx[2 * i + 1].astype(F32))
    e, o = even_odd(16)
    bx_in = e + o
    put(rows, 0, xhr[BX * H + 3])
    e, o = even_odd(4)
    edge[0:4] = e + o
    for i in range(4):
        edge[4 + i : 5 + i] = yhr[8 + 2 * i, 3:4] + yhr[8 + 2 * i + 1, 3:4]
    out = exact_dot(jnp.concatenate([a_in, bx_in, by_in, edge[...]], axis=0), both)
    a1, bx1, by1, edges = out[0:16] * 0.125, out[16:32] * 0.25, out[32:48] * 0.25, out[48:56] * 0.25
    bz1 = exact_dot(bz_in, odd) * 0.25
    c1[1] = bx1
    c1[2] = by1
    c1[3] = bz1
    fine[0, 0:8] = edges
    fine[1, 0:4] = edges[0:4]
    fine[1, 4:20] = bx1
    lower_x = fine[1, 0:16]
    fine[2, 1:17] = by1
    lower_y = fine[2, 0:16]
    for i in range(4):
        fine[3, 4 * i : 4 * i + 4] = jnp.broadcast_to(fine[0, 4 + i : 5 + i], (4, nz // 2))
    lower_y = jnp.where(iota(lower_y.shape, 0) % 4 == 0, fine[3, 0:16], lower_y)
    c1[0] = a1 + 0.25 * ((bx1 + lower_x) + (by1 + lower_y) + (bz1 + below_z(bz1)))

    def split(x):
        put(rows, 0, x)
        n = x.shape[0] // 2
        return every_other(rows, 0, n, nz // 2), every_other(rows, 1, n, nz // 2)

    def layers(t):
        small[0:8] = t
        top = small[0:2] + small[2:4]
        bottom = small[4:6] + small[6:8]
        return top, bottom

    e, o = split(a1)
    a_t = layers(e + o)
    e, o = split(bz1)
    bz_t = layers(e + o)
    e, o = split(by1)
    by_t = layers(o)
    e, o = split(bx1)
    small[0:8] = e + o
    bx_t = (small[2:4], small[6:8])
    e, o = split(edges)
    small[0:4] = e + o
    small[8:10] = a_t[0]
    small[10:12] = a_t[1]
    small[12:14] = by_t[0]
    small[14:16] = by_t[1]
    small[16:18] = bx_t[0]
    small[18:20] = bx_t[1]
    small[20:24] = small[0:4]
    small[24:26] = bz_t[0]
    small[26:28] = bz_t[1]
    small[28:32] = small[0:4]
    out = exact_dot(small[8:24], both2)
    out_z = exact_dot(small[24:32], odd2)[0:4] * 0.25
    a2, by2, bx2, edges = out[0:4] * 0.125, out[4:8] * 0.25, out[8:12] * 0.25, out[12:16] * 0.25
    w = nz // 4
    c2[4:8] = bx2
    c2[8:12] = by2
    c2[12:16] = out_z
    small[0:2, 0:w] = edges[0:2]
    small[2:6, 0:w] = bx2
    lower_x = small[0:4, 0:w]
    small[8:12, 0:w] = by2
    small[16:20, 0:w] = edges
    small[24:25, 0:w] = small[18:19, 0:w]
    small[25:26, 0:w] = small[8:9, 0:w]
    small[26:27, 0:w] = small[19:20, 0:w]
    small[27:28, 0:w] = small[10:11, 0:w]
    lower_y = small[24:28, 0:w]
    c2[0:4] = a2 + 0.0625 * ((bx2 + lower_x) + (by2 + lower_y) + (out_z + below_z(out_z)))


def set_weights(weights, w, inverse, source, up_x, low_x, up_y, up_z):
    lane = iota(inverse.shape, 1)
    nz = inverse.shape[1]
    weights[0, w] = source * inverse
    weights[1, w] = up_x * inverse
    weights[2, w] = low_x * inverse
    weights[3, w] = up_y * inverse
    weights[4, w] = pltpu.roll(up_y, 1, 0) * inverse
    weights[5, w] = jnp.where(lane == nz - 1, 0.0, up_z) * inverse
    weights[6, w] = jnp.where(lane == 0, 0.0, pltpu.roll(up_z, 1, 1)) * inverse


def relaxed(weights, held, w):
    here = held[w + 1]
    ny, nz = here.shape
    x = weights[1, w] * held[w + 2] + weights[2, w] * held[w]
    y = weights[3, w] * pltpu.roll(here, ny - 1, 0) + weights[4, w] * pltpu.roll(here, 1, 0)
    z = weights[5, w] * pltpu.roll(here, nz - 1, 1) + weights[6, w] * pltpu.roll(here, 1, 1)
    return ((weights[0, w] + x) + (y + z)), here


def smooth(weights, held, reach):
    count = weights.shape[1]
    spare = (weights.shape[2], weights.shape[3])
    parity = (iota(spare, 0) + iota(spare, 1)) % 2
    for step in range(4):

        def one(w, carry, step=step):
            new, here = relaxed(weights, held, w)
            held[w + 1] = jnp.where((parity + w + step) % 2 == 0, new, here)
            return carry

        first = step
        lax.fori_loop(first, count - first, one, 0)


def fine_body(u, f, a, bx, by, bz, xlr, xhr, ylr, yhr, yclr, ychr, c1, out, p1, win, weights, held, diag, rows):
    own = (u, f, a, bx, by, bz)
    nz = u.shape[2]
    upper = iota((8, nz), 0) >= 4

    for w in range(16):
        for n, pair in enumerate(PAIRS):
            if w < 4:
                below, above = ychr[n * 8 + w], yclr[n * 8 + w]
            elif w < 12:
                below, above = yhr[n * 8 + w - 4], ylr[n * 8 + w - 4]
            else:
                below, above = ychr[n * 8 + w - 8], yclr[n * 8 + w - 8]
            for side, k in enumerate(pair):
                if side:
                    below, above = pltpu.roll(below, 4, 0), pltpu.roll(above, 4, 0)
                if w < 4:
                    mid = xhr[k * H + w]
                elif w < 12:
                    mid = own[k][w - 4].astype(F32)
                else:
                    mid = xlr[k * H + w - 12]
                low = jnp.where(upper, below, 0.0)
                high = jnp.where(upper, 0.0, above)
                if k == U:
                    held[w + 1, 0:8] = low
                    held[w + 1, 8:16] = mid
                    held[w + 1, 16:24] = high
                else:
                    win[k - 1, w + 1, 0:8] = low
                    win[k - 1, w + 1, 8:16] = mid
                    win[k - 1, w + 1, 16:24] = high
    zero = jnp.zeros((24, nz), F32)
    held[0] = zero
    held[17] = zero
    win[BX - 1, 0] = zero

    def prepare(w, carry):
        av, bxv, byv, bzv = win[A - 1, w + 1], win[BX - 1, w + 1], win[BY - 1, w + 1], win[BZ - 1, w + 1]
        low_x = win[BX - 1, w]
        total = av + ((bxv + low_x) + (byv + pltpu.roll(byv, 1, 0)) + (bzv + below_z(bzv)))
        inside = av > 0.0
        inverse = jnp.where(inside, 1.0 / jnp.where(inside, total, 1.0), 0.0)
        set_weights(weights, w, inverse, win[F - 1, w + 1], bxv, low_x, byv, bzv)
        diag[w] = total[8:16]
        return carry

    lax.fori_loop(0, 16, prepare, 0)
    smooth(weights, held, H)
    for i in range(4):
        total = None
        for j in range(2):
            w = 4 + 2 * i + j
            new, here = relaxed(weights, held, w)
            out[w - 4] = here[8:16]
            res = diag[w] * (new[8:16] - here[8:16])
            total = res if total is None else total + res
        put(rows, 8 * i, total)
    both, _ = halves(nz)
    p1[0] = exact_dot(every_other(rows, 0, 16, nz) + every_other(rows, 1, 16, nz), both) * 0.125
    for k in range(4):
        p1[1 + k] = c1[k]


def middle_body(below, here, above, c2, out, p2, win, weights, held, rows):
    nz = below.shape[2]
    zero = jnp.zeros((16, nz), F32)
    for k in range(5):
        for w in range(12):
            win[k, w + 1, 0:4] = jnp.zeros((4, nz), F32)
            win[k, w + 1, 4:8] = below[k, 4 * w : 4 * w + 4]
            win[k, w + 1, 8:12] = here[k, 4 * w : 4 * w + 4]
            win[k, w + 1, 12:16] = above[k, 4 * w : 4 * w + 4]
    win[2, 0] = zero

    def prepare(w, carry):
        total = win[1, w + 1]
        inside = total > 0.0
        inverse = jnp.where(inside, 0.25 / jnp.where(inside, total, 1.0), 0.0)
        set_weights(weights, w, inverse, 4.0 * win[0, w + 1], win[2, w + 1], win[2, w], win[3, w + 1], win[4, w + 1])
        held[w + 1] = zero
        return carry

    lax.fori_loop(0, 12, prepare, 0)
    held[0] = zero
    held[13] = zero
    smooth(weights, held, H)
    for i in range(2):
        total = None
        for j in range(2):
            w = 4 + 2 * i + j
            new, now = relaxed(weights, held, w)
            out[w - 4] = now[8:12]
            res = win[1, w + 1, 8:16] * (new[8:16] - now[8:16])
            total = res if total is None else total + res
        put(rows, 8 * i, total)
    both, _ = halves(nz)
    coarse = exact_dot(every_other(rows, 0, 8, nz) + every_other(rows, 1, 8, nz), both) * 0.125
    p2[0:2] = coarse[0:2]
    p2[2:4] = coarse[4:6]
    p2[4:20] = c2[...]


def coarse_level_body(left, right, down, up, below, here, above, out, win, weights, held):
    nz = left.shape[1]
    win[...] = jnp.zeros(win.shape, F32)
    for k in range(5):
        win[k, 1, 3:5] = left[4 * k + 2 : 4 * k + 4]
        win[k, 8, 3:5] = right[4 * k : 4 * k + 2]
        for i in range(2):
            at = 4 * k + 2 * i
            win[k, 4 + i, 0:1] = down[at + 1 : at + 2]
            win[k, 4 + i, 7:8] = up[at : at + 1]
            for b in range(3):
                win[k, 2 + 2 * b + i, 1:3] = below[b, at : at + 2]
                win[k, 2 + 2 * b + i, 3:5] = here[b, at : at + 2]
                win[k, 2 + 2 * b + i, 5:7] = above[b, at : at + 2]
    held[...] = jnp.zeros(held.shape, F32)
    for w in range(8):
        total = win[1, w + 1]
        inside = total > 0.0
        inverse = jnp.where(inside, 0.0625 / jnp.where(inside, total, 1.0), 0.0)
        set_weights(weights, w, inverse, 16.0 * win[0, w + 1], win[2, w + 1], win[2, w], win[3, w + 1], win[4, w + 1])
    smooth(weights, held, 3)
    for i in range(2):
        out[i] = held[4 + i, 3:5]


def moved(block, axis, by):
    count = lax.axis_size(axis)
    return lax.ppermute(block, axis, [(i, i + by) for i in range(count) if 0 <= i + by < count])


def shape(*dims):
    return jax.ShapeDtypeStruct(dims, F32)


def shards(solution, right_side, alpha, beta_x, beta_y, beta_z):
    own = (solution, right_side, alpha, beta_x, beta_y, beta_z)
    nz = solution.shape[2]
    sent = shape(24, 8, nz)
    xl, xh, yl, yh = call(pack_body, (sent,) * 4, own)
    xlr, xhr = moved(xl, "gx", -1), moved(xh, "gx", 1)
    ylr, yhr = moved(yl, "gy", -1), moved(yh, "gy", 1)
    ycl, ych = call(corner_body, (sent,) * 2, (xlr, xhr))
    yclr, ychr = moved(ycl, "gy", -1), moved(ych, "gy", 1)
    c1, c2 = call(
        coarse_body,
        (shape(4, 16, nz // 2), shape(16, nz // 4)),
        (alpha, beta_x, beta_y, beta_z, xhr, yhr),
        [
            pltpu.VMEM((nz // 128, 32, 128), F32),
            pltpu.VMEM((8, nz), F32),
            pltpu.VMEM((4, 24, nz // 2), F32),
            pltpu.VMEM((32, nz // 2), F32),
        ],
    )
    fine, p1 = call(
        fine_body,
        (shape(8, 8, nz), shape(5, 16, nz // 2)),
        (*own, xlr, xhr, ylr, yhr, yclr, ychr, c1),
        [
            pltpu.VMEM((5, 17, 24, nz), F32),
            pltpu.VMEM((7, 16, 24, nz), F32),
            pltpu.VMEM((18, 24, nz), F32),
            pltpu.VMEM((16, 8, nz), F32),
            pltpu.VMEM((nz // 128, 32, 128), F32),
        ],
        flops=20_000_000,
        nbytes=20_000_000,
    )
    here = jnp.concatenate([moved(p1, "gx", 1), p1, moved(p1, "gx", -1)], axis=1)
    below, above = moved(here, "gy", 1), moved(here, "gy", -1)
    middle, p2 = call(
        middle_body,
        (shape(4, 4, nz // 2), shape(20, nz // 4)),
        (below, here, above, c2),
        [
            pltpu.VMEM((5, 13, 16, nz // 2), F32),
            pltpu.VMEM((7, 12, 16, nz // 2), F32),
            pltpu.VMEM((14, 16, nz // 2), F32),
            pltpu.VMEM((nz // 256, 16, 128), F32),
        ],
    )
    left, right = moved(p2, "gx", 2), moved(p2, "gx", -2)
    down, up = moved(p2, "gy", 2), moved(p2, "gy", -2)
    here = jnp.stack([moved(p2, "gx", 1), p2, moved(p2, "gx", -1)])
    below, above = moved(here, "gy", 1), moved(here, "gy", -1)
    coarse = call(
        coarse_level_body,
        shape(2, 2, nz // 4),
        (left, right, down, up, below, here, above),
        [
            pltpu.VMEM((5, 9, 8, nz // 4), F32),
            pltpu.VMEM((7, 8, 8, nz // 4), F32),
            pltpu.VMEM((10, 8, nz // 4), F32),
        ],
    )
    return (fine, middle, coarse)


def solution(mesh):
    placed = P("gx", "gy", None)
    return jax.shard_map(
        shards,
        mesh=mesh,
        in_specs=(placed,) * 6,
        out_specs=(placed,) * 3,
        check_vma=False,
    )
```

time: 326 us -> 129 us (0.40)
  starting transfers between devices: 183 us -> 79.7 us
  waiting for transfers between devices: 91.7 us -> 26.3 us
  local copies, waits for them, and re-layouts: 31.9 us -> 5.18 us
  Pallas kernels: 0 us -> 16 us
  other arithmetic: 15 us -> 0.01 us
    ppermute x62 -> x18, starting transfers between devices: 183 us -> 79.7 us  [moved(): lax.ppermute(block, axis, [(i, i + by) for i in range(count) if 0 <= i +...]
    ppermute x62 -> x18, waiting for transfers between devices: 91.7 us -> 26.3 us  [moved(): lax.ppermute(block, axis, [(i, i + by) for i in range(count) if 0 <= i +...]
    reshape x6 -> x0, local copies, waits for them, and re-layouts: 21.5 us -> none  [the longest x3 20.5 us: coarsen_cells(): field.reshape(nx // 2, 2, ny // 2, 2, nz // 2, 2).mean(axis=(1, 3, 5))]
    pallas_call x0 -> x6, Pallas kernels: none -> 16 us  [call(): pl.pallas_call(body, out_shape=outs, in_specs=[vmem] * len(args), out_spe...]
    reduce_sum x10 -> x0, other arithmetic: 12.2 us -> none  [the longest x4 8.36 us: coarsen_cells(): field.reshape(nx // 2, 2, ny // 2, 2, nz // 2, 2).mean(axis=(1, 3, 5))]
    slice x47 -> x0, local copies, waits for them, and re-layouts: 8.88 us -> none  [the longest x12 1.96 us: shift_up(): rest = lax.slice_in_dim(field, 1, size, axis=axis)]
    unnamed x18 -> x14, local copies, waits for them, and re-layouts: 0.06 us -> 5.17 us
  transfers between devices with their start and end apart: 62 -> 18, of which waited for: 23 -> 9; matrix products, arithmetic and copies ran while one was open for 14% -> 0% of each run, Pallas kernels for 0% -> 0%
where the time goes in v1:
time: 129 us; the launch traced here: 128 us
  starting transfers between devices  79.7 us (62%)
  waiting for transfers between devices  26.3 us (20%)
  Pallas kernels  16 us (12%)
  local copies, waits for them, and re-layouts  5.18 us (4%)
    ppermute x18, starting transfers between devices, moved(): lax.ppermute(block, axis, [(i, i + by) for i in range(count) if 0 <= i +...  79.7 us
    ppermute x18, waiting for transfers between devices, moved(): lax.ppermute(block, axis, [(i, i + by) for i in range(count) if 0 <= i +...  26.3 us
    pallas_call x6, Pallas kernels, call(): pl.pallas_call(body, out_shape=outs, in_specs=[vmem] * len(args), out_spe...  16 us
    unnamed x14, local copies, waits for them, and re-layouts  5.17 us
  transfers between devices with their start and end apart: 18, of which 9 were waited for; matrix products, arithmetic and copies ran while one was open for 0% of the time, Pallas kernels for 0%

profile of v1, /device:TPU:72, one launch (start us, length us, event | category | flops | bytes accessed | tf_op | source)
XLA Modules:
  0.0 128.1 jit_solution(2694152351758812340)
XLA Ops:
  0.6 0.8 copy-done
  1.5 0.8 copy-done.1
  2.3 0.8 copy-done.2
  3.2 0.8 copy-done.3
  4.0 0.9 copy-done.4
  4.9 0.9 copy-done.5
  5.8 0.2 shard_map.85
  6.0 1.9 %collective-permute-start = (f32[24,8,512]{2,1,0:T(8,128)S(1)}, f32[24,8,512]{2,1,0:T(8,128)S(1)}, u32[]{:S(2)}, u32[]{:S(2)}) collective-permute-start(f32[24,8,512]{2,1,0:T(8,128)S(1)} %get-tuple-element.15), channel_id=1, source_target_pairs={{64,0},{128,64},{192,128},{256,192},{320,256},{384,320},{448,384},... | collective-permute-start | bytes 1179656 | tf_op jit(solution)/shard_map/ppermute | solution.py:383
  7.9 2.4 %collective-permute-start.1 = (f32[24,8,512]{2,1,0:T(8,128)S(1)}, f32[24,8,512]{2,1,0:T(8,128)S(1)}, u32[]{:S(2)}, u32[]{:S(2)}) collective-permute-start(f32[24,8,512]{2,1,0:T(8,128)S(1)} %get-tuple-element.16), channel_id=1, source_target_pairs={{0,64},{64,128},{128,192},{192,256},{256,320},{320,384},{384,448},... | collective-permute-start | bytes 1179656 | tf_op jit(solution)/shard_map/ppermute | solution.py:383
  10.3 17.1 %collective-permute-start.2 = (f32[24,8,512]{2,1,0:T(8,128)S(1)}, f32[24,8,512]{2,1,0:T(8,128)S(1)}, u32[]{:S(2)}, u32[]{:S(2)}) collective-permute-start(f32[24,8,512]{2,1,0:T(8,128)S(1)} %get-tuple-element.17), channel_id=1, source_target_pairs={{1,0},{2,1},{3,2},{4,3},{5,4},{6,5},{7,6},{8,7},{9,8},{10,9},{11,1... | collective-permute-start | bytes 1179656 | tf_op jit(solution)/shard_map/ppermute | solution.py:383
  27.4 1.9 %collective-permute-start.3 = (f32[24,8,512]{2,1,0:T(8,128)S(1)}, f32[24,8,512]{2,1,0:T(8,128)S(1)}, u32[]{:S(2)}, u32[]{:S(2)}) collective-permute-start(f32[24,8,512]{2,1,0:T(8,128)S(1)} %get-tuple-element.18), channel_id=1, source_target_pairs={{0,1},{1,2},{2,3},{3,4},{4,5},{5,6},{6,7},{7,8},{8,9},{9,10},{10,1... | collective-permute-start | bytes 1179656 | tf_op jit(solution)/shard_map/ppermute | solution.py:383
  29.3 0.0 collective-permute-done.xlr
  29.4 0.0 collective-permute-done.1.xhr
  29.4 0.1 shard_map.86
  29.4 7.2 %collective-permute-start.4 = (f32[24,8,512]{2,1,0:T(8,128)S(1)}, f32[24,8,512]{2,1,0:T(8,128)S(1)}, u32[]{:S(2)}, u32[]{:S(2)}) collective-permute-start(f32[24,8,512]{2,1,0:T(8,128)S(1)} %get-tuple-element.19), channel_id=1, source_target_pairs={{1,0},{2,1},{3,2},{4,3},{5,4},{6,5},{7,6},{8,7},{9,8},{10,9},{11,1... | collective-permute-start | bytes 1179656 | tf_op jit(solution)/shard_map/ppermute | solution.py:383
  36.7 1.9 %collective-permute-start.5 = (f32[24,8,512]{2,1,0:T(8,128)S(1)}, f32[24,8,512]{2,1,0:T(8,128)S(1)}, u32[]{:S(2)}, u32[]{:S(2)}) collective-permute-start(f32[24,8,512]{2,1,0:T(8,128)S(1)} %get-tuple-element.20), channel_id=1, source_target_pairs={{0,1},{1,2},{2,3},{3,4},{4,5},{5,6},{6,7},{7,8},{8,9},{9,10},{10,1... | collective-permute-start | bytes 1179656 | tf_op jit(solution)/shard_map/ppermute | solution.py:383
  38.6 5.8 %collective-permute-done.3.yhr = f32[24,8,512]{2,1,0:T(8,128)S(1)} collective-permute-done((f32[24,8,512]{2,1,0:T(8,128)S(1)}, f32[24,8,512]{2,1,0:T(8,128)S(1)}, u32[]{:S(2)}, u32[]{:S(2)}) %collective-permute-start.3) | collective-permute-done | bytes 393248 | tf_op jit(solution)/shard_map/ppermute | solution.py:383
  44.4 0.6 shard_map.87
  45.0 0.0 collective-permute-done.2.ylr
  45.0 0.7 collective-permute-done.4.yclr
  45.7 7.4 %collective-permute-done.5.ychr = f32[24,8,512]{2,1,0:T(8,128)S(1)} collective-permute-done((f32[24,8,512]{2,1,0:T(8,128)S(1)}, f32[24,8,512]{2,1,0:T(8,128)S(1)}, u32[]{:S(2)}, u32[]{:S(2)}) %collective-permute-start.5) | collective-permute-done | bytes 393248 | tf_op jit(solution)/shard_map/ppermute | solution.py:383
  53.1 8.1 %shard_map.88 = (f32[8,8,512]{2,1,0:T(8,128)}, f32[5,16,256]{2,1,0:T(8,128)S(1)}) custom-call(f32[8,8,512]{2,1,0:T(8,128)S(1)} %copy-done.4, f32[8,8,512]{2,1,0:T(8,128)S(1)} %copy-done.5, bf16[8,8,512]{2,1,0:T(8,128)(2,1)S(1)} %copy-done, bf16[8,8,512]{2,1,0:T(8,128)(2,1)S(1)} %copy-done.1, bf16[8,8,512]{2,1,0:T(8,128)(2,1)S(1)} %copy-done.2, ...), custom_call_target="tpu_custom_call" | custom-call | flops 20000000 | bytes 20000000 | tf_op jit(solution)/shard_map/pallas_call | solution.py:22
  61.3 1.9 %collective-permute-start.6 = (f32[5,16,256]{2,1,0:T(8,128)S(1)}, f32[5,16,256]{2,1,0:T(8,128)S(1)}, u32[]{:S(2)}, u32[]{:S(2)}) collective-permute-start(f32[5,16,256]{2,1,0:T(8,128)S(1)} %get-tuple-element.23), channel_id=1, source_target_pairs={{0,64},{64,128},{128,192},{192,256},{256,320},{320,384},{384,448},... | collective-permute-start | bytes 245768 | tf_op jit(solution)/shard_map/ppermute | solution.py:383
  63.2 4.9 %collective-permute-start.7 = (f32[5,16,256]{2,1,0:T(8,128)S(1)}, f32[5,16,256]{2,1,0:T(8,128)S(1)}, u32[]{:S(2)}, u32[]{:S(2)}) collective-permute-start(f32[5,16,256]{2,1,0:T(8,128)S(1)} %get-tuple-element.23), channel_id=1, source_target_pairs={{64,0},{128,64},{192,128},{256,192},{320,256},{384,320},{448,384},... | collective-permute-start | bytes 245768 | tf_op jit(solution)/shard_map/ppermute | solution.py:383
  68.0 0.2 collective-permute-done.6
  68.2 1.8 %collective-permute-done.7 = f32[5,16,256]{2,1,0:T(8,128)S(1)} collective-permute-done((f32[5,16,256]{2,1,0:T(8,128)S(1)}, f32[5,16,256]{2,1,0:T(8,128)S(1)}, u32[]{:S(2)}, u32[]{:S(2)}) %collective-permute-start.7) | collective-permute-done | bytes 81952 | tf_op jit(solution)/shard_map/ppermute | solution.py:383
  70.1 1.9 %collective-permute-start.8 = (f32[5,48,256]{2,1,0:T(8,128)S(1)}, f32[5,48,256]{2,1,0:T(8,128)S(1)}, u32[]{:S(2)}, u32[]{:S(2)}) collective-permute-start(f32[5,48,256]{2,1,0:T(8,128)S(1)} %constant_dynamic-update-slice_fusion.here), channel_id=1, source_target_pairs={{0,1},{1,2},{2,3},{3,4},{4,5},{5,6},{6,7},{7,8},{8,9},{9,10},{10,1... | collective-permute-start | bytes 737288 | tf_op jit(solution)/shard_map/ppermute | solution.py:383
  72.0 7.2 %collective-permute-start.9 = (f32[5,48,256]{2,1,0:T(8,128)S(1)}, f32[5,48,256]{2,1,0:T(8,128)S(1)}, u32[]{:S(2)}, u32[]{:S(2)}) collective-permute-start(f32[5,48,256]{2,1,0:T(8,128)S(1)} %constant_dynamic-update-slice_fusion.here), channel_id=1, source_target_pairs={{1,0},{2,1},{3,2},{4,3},{5,4},{6,5},{7,6},{8,7},{9,8},{10,9},{11,1... | collective-permute-start | bytes 737288 | tf_op jit(solution)/shard_map/ppermute | solution.py:383
  79.3 3.5 %collective-permute-done.8.below = f32[5,48,256]{2,1,0:T(8,128)S(1)} collective-permute-done((f32[5,48,256]{2,1,0:T(8,128)S(1)}, f32[5,48,256]{2,1,0:T(8,128)S(1)}, u32[]{:S(2)}, u32[]{:S(2)}) %collective-permute-start.8) | collective-permute-done | bytes 245792 | tf_op jit(solution)/shard_map/ppermute | solution.py:383
  82.7 1.2 collective-permute-done.9.above
  83.9 4.8 %shard_map.89 = (f32[4,4,256]{2,1,0:T(4,128)}, f32[20,128]{1,0:T(8,128)S(1)}) custom-call(f32[5,48,256]{2,1,0:T(8,128)S(1)} %collective-permute-done.8.below, f32[5,48,256]{2,1,0:T(8,128)S(1)} %constant_dynamic-update-slice_fusion.here, f32[5,48,256]{2,1,0:T(8,128)S(1)} %collective-permute-done.9.above, f32[16,128]{1,0:T(8,128)S(1)} %get-tuple-element.24.c2), custom_call_target="tpu_custom_call" | custom-call | flops 1000000 | bytes 2000000 | tf_op jit(solution)/shard_map/pallas_call | solution.py:22
  88.7 2.9 %collective-permute-start.15 = (f32[20,128]{1,0:T(8,128)S(1)}, f32[20,128]{1,0:T(8,128)S(1)}, u32[]{:S(2)}, u32[]{:S(2)}) collective-permute-start(f32[20,128]{1,0:T(8,128)S(1)} %get-tuple-element.26), channel_id=1, source_target_pairs={{64,0},{128,64},{192,128},{256,192},{320,256},{384,320},{448,384},... | collective-permute-start | bytes 30728 | tf_op jit(solution)/shard_map/ppermute | solution.py:383
  91.6 1.9 %collective-permute-start.14 = (f32[20,128]{1,0:T(8,128)S(1)}, f32[20,128]{1,0:T(8,128)S(1)}, u32[]{:S(2)}, u32[]{:S(2)}) collective-permute-start(f32[20,128]{1,0:T(8,128)S(1)} %get-tuple-element.26), channel_id=1, source_target_pairs={{0,64},{64,128},{128,192},{192,256},{256,320},{320,384},{384,448},... | collective-permute-start | bytes 30728 | tf_op jit(solution)/shard_map/ppermute | solution.py:383
  93.6 0.0 collective-permute-done.15
  93.6 4.3 %collective-permute-done.14 = f32[20,128]{1,0:T(8,128)S(1)} collective-permute-done((f32[20,128]{1,0:T(8,128)S(1)}, f32[20,128]{1,0:T(8,128)S(1)}, u32[]{:S(2)}, u32[]{:S(2)}) %collective-permute-start.14) | collective-permute-done | bytes 10272 | tf_op jit(solution)/shard_map/ppermute | solution.py:383
  97.9 1.9 %collective-permute-start.16 = (f32[3,20,128]{2,1,0:T(8,128)S(1)}, f32[3,20,128]{2,1,0:T(8,128)S(1)}, u32[]{:S(2)}, u32[]{:S(2)}) collective-permute-start(f32[3,20,128]{2,1,0:T(8,128)S(1)} %pad_maximum_fusion.here), channel_id=1, source_target_pairs={{0,1},{1,2},{2,3},{3,4},{4,5},{5,6},{6,7},{7,8},{8,9},{9,10},{10,1... | collective-permute-start | bytes 92168 | tf_op jit(solution)/shard_map/ppermute | solution.py:383
  99.8 7.4 %collective-permute-start.17 = (f32[3,20,128]{2,1,0:T(8,128)S(1)}, f32[3,20,128]{2,1,0:T(8,128)S(1)}, u32[]{:S(2)}, u32[]{:S(2)}) collective-permute-start(f32[3,20,128]{2,1,0:T(8,128)S(1)} %pad_maximum_fusion.here), channel_id=1, source_target_pairs={{1,0},{2,1},{3,2},{4,3},{5,4},{6,5},{7,6},{8,7},{9,8},{10,9},{11,1... | collective-permute-start | bytes 92168 | tf_op jit(solution)/shard_map/ppermute | solution.py:383
  107.2 1.9 %collective-permute-start.10 = (f32[20,128]{1,0:T(8,128)S(1)}, f32[20,128]{1,0:T(8,128)S(1)}, u32[]{:S(2)}, u32[]{:S(2)}) collective-permute-start(f32[20,128]{1,0:T(8,128)S(1)} %get-tuple-element.26), channel_id=1, source_target_pairs={{0,128},{64,192},{128,256},{192,320},{256,384},{320,448},{384,512}... | collective-permute-start | bytes 30728 | tf_op jit(solution)/shard_map/ppermute | solution.py:383
  109.1 5.1 %collective-permute-start.11 = (f32[20,128]{1,0:T(8,128)S(1)}, f32[20,128]{1,0:T(8,128)S(1)}, u32[]{:S(2)}, u32[]{:S(2)}) collective-permute-start(f32[20,128]{1,0:T(8,128)S(1)} %get-tuple-element.26), channel_id=1, source_target_pairs={{128,0},{192,64},{256,128},{320,192},{384,256},{448,320},{512,384}... | collective-permute-start | bytes 30728 | tf_op jit(solution)/shard_map/ppermute | solution.py:383
  114.3 1.9 %collective-permute-start.12 = (f32[20,128]{1,0:T(8,128)S(1)}, f32[20,128]{1,0:T(8,128)S(1)}, u32[]{:S(2)}, u32[]{:S(2)}) collective-permute-start(f32[20,128]{1,0:T(8,128)S(1)} %get-tuple-element.26), channel_id=1, source_target_pairs={{0,2},{1,3},{2,4},{3,5},{4,6},{5,7},{6,8},{7,9},{8,10},{9,11},{10,... | collective-permute-start | bytes 30728 | tf_op jit(solution)/shard_map/ppermute | solution.py:383
  116.2 0.0 collective-permute-done.10.left
  116.2 8.1 %collective-permute-start.13 = (f32[20,128]{1,0:T(8,128)S(1)}, f32[20,128]{1,0:T(8,128)S(1)}, u32[]{:S(2)}, u32[]{:S(2)}) collective-permute-start(f32[20,128]{1,0:T(8,128)S(1)} %get-tuple-element.26), channel_id=1, source_target_pairs={{2,0},{3,1},{4,2},{5,3},{6,4},{7,5},{8,6},{9,7},{10,8},{11,9},{12,... | collective-permute-start | bytes 30728 | tf_op jit(solution)/shard_map/ppermute | solution.py:383
  124.4 0.0 collective-permute-done.11.right
  124.4 0.0 collective-permute-done.12.down
  124.4 1.4 %collective-permute-done.13.up = f32[20,128]{1,0:T(8,128)S(1)} collective-permute-done((f32[20,128]{1,0:T(8,128)S(1)}, f32[20,128]{1,0:T(8,128)S(1)}, u32[]{:S(2)}, u32[]{:S(2)}) %collective-permute-start.13) | collective-permute-done | bytes 10272 | tf_op jit(solution)/shard_map/ppermute | solution.py:383
  125.8 0.0 collective-permute-done.16.below
  125.8 0.0 collective-permute-done.17.above
  125.8 2.3 %shard_map.90 = f32[2,2,128]{2,1,0:T(2,128)} custom-call(f32[20,128]{1,0:T(8,128)S(1)} %collective-permute-done.10.left, f32[20,128]{1,0:T(8,128)S(1)} %collective-permute-done.11.right, f32[20,128]{1,0:T(8,128)S(1)} %collective-permute-done.12.down, f32[20,128]{1,0:T(8,128)S(1)} %collective-permute-done.13.up, ...), custom_call_target="tpu_custom_call" | custom-call | flops 1000000 | bytes 2000000 | tf_op jit(solution)/shard_map/pallas_call | solution.py:22
  (10 shorter events, 0.0 us)
Async XLA Ops:
  0.6 0.8 copy-start
  1.5 0.8 copy-start.1
  2.3 0.8 copy-start.2
  3.2 0.8 copy-start.3
  4.0 0.9 copy-start.4
  4.9 0.9 copy-start.5
  6.0 23.4 %collective-permute-start = (f32[24,8,512]{2,1,0:T(8,128)S(1)}, f32[24,8,512]{2,1,0:T(8,128)S(1)}, u32[]{:S(2)}, u32[]{:S(2)}) collective-permute-start(f32[24,8,512]{2,1,0:T(8,128)S(1)} %get-tuple-element.15), channel_id=1, source_target_pairs={{64,0},{128,64},{192,128},{256,192},{320,256},{384,320},{448,384},... | collective-permute-start | bytes 1179656 | tf_op jit(solution)/shard_map/ppermute | solution.py:383
  7.9 21.5 %collective-permute-start.1 = (f32[24,8,512]{2,1,0:T(8,128)S(1)}, f32[24,8,512]{2,1,0:T(8,128)S(1)}, u32[]{:S(2)}, u32[]{:S(2)}) collective-permute-start(f32[24,8,512]{2,1,0:T(8,128)S(1)} %get-tuple-element.16), channel_id=1, source_target_pairs={{0,64},{64,128},{128,192},{192,256},{256,320},{320,384},{384,448},... | collective-permute-start | bytes 1179656 | tf_op jit(solution)/shard_map/ppermute | solution.py:383
  10.3 34.7 %collective-permute-start.2 = (f32[24,8,512]{2,1,0:T(8,128)S(1)}, f32[24,8,512]{2,1,0:T(8,128)S(1)}, u32[]{:S(2)}, u32[]{:S(2)}) collective-permute-start(f32[24,8,512]{2,1,0:T(8,128)S(1)} %get-tuple-element.17), channel_id=1, source_target_pairs={{1,0},{2,1},{3,2},{4,3},{5,4},{6,5},{7,6},{8,7},{9,8},{10,9},{11,1... | collective-permute-start | bytes 1179656 | tf_op jit(solution)/shard_map/ppermute | solution.py:383
  27.4 17.0 %collective-permute-start.3 = (f32[24,8,512]{2,1,0:T(8,128)S(1)}, f32[24,8,512]{2,1,0:T(8,128)S(1)}, u32[]{:S(2)}, u32[]{:S(2)}) collective-permute-start(f32[24,8,512]{2,1,0:T(8,128)S(1)} %get-tuple-element.18), channel_id=1, source_target_pairs={{0,1},{1,2},{2,3},{3,4},{4,5},{5,6},{6,7},{7,8},{8,9},{9,10},{10,1... | collective-permute-start | bytes 1179656 | tf_op jit(solution)/shard_map/ppermute | solution.py:383
  29.4 16.3 %collective-permute-start.4 = (f32[24,8,512]{2,1,0:T(8,128)S(1)}, f32[24,8,512]{2,1,0:T(8,128)S(1)}, u32[]{:S(2)}, u32[]{:S(2)}) collective-permute-start(f32[24,8,512]{2,1,0:T(8,128)S(1)} %get-tuple-element.19), channel_id=1, source_target_pairs={{1,0},{2,1},{3,2},{4,3},{5,4},{6,5},{7,6},{8,7},{9,8},{10,9},{11,1... | collective-permute-start | bytes 1179656 | tf_op jit(solution)/shard_map/ppermute | solution.py:383
  36.7 16.5 %collective-permute-start.5 = (f32[24,8,512]{2,1,0:T(8,128)S(1)}, f32[24,8,512]{2,1,0:T(8,128)S(1)}, u32[]{:S(2)}, u32[]{:S(2)}) collective-permute-start(f32[24,8,512]{2,1,0:T(8,128)S(1)} %get-tuple-element.20), channel_id=1, source_target_pairs={{0,1},{1,2},{2,3},{3,4},{4,5},{5,6},{6,7},{7,8},{8,9},{9,10},{10,1... | collective-permute-start | bytes 1179656 | tf_op jit(solution)/shard_map/ppermute | solution.py:383
  61.3 7.0 %collective-permute-start.6 = (f32[5,16,256]{2,1,0:T(8,128)S(1)}, f32[5,16,256]{2,1,0:T(8,128)S(1)}, u32[]{:S(2)}, u32[]{:S(2)}) collective-permute-start(f32[5,16,256]{2,1,0:T(8,128)S(1)} %get-tuple-element.23), channel_id=1, source_target_pairs={{0,64},{64,128},{128,192},{192,256},{256,320},{320,384},{384,448},... | collective-permute-start | bytes 245768 | tf_op jit(solution)/shard_map/ppermute | solution.py:383
  63.2 6.9 %collective-permute-start.7 = (f32[5,16,256]{2,1,0:T(8,128)S(1)}, f32[5,16,256]{2,1,0:T(8,128)S(1)}, u32[]{:S(2)}, u32[]{:S(2)}) collective-permute-start(f32[5,16,256]{2,1,0:T(8,128)S(1)} %get-tuple-element.23), channel_id=1, source_target_pairs={{64,0},{128,64},{192,128},{256,192},{320,256},{384,320},{448,384},... | collective-permute-start | bytes 245768 | tf_op jit(solution)/shard_map/ppermute | solution.py:383
  70.1 12.6 %collective-permute-start.8 = (f32[5,48,256]{2,1,0:T(8,128)S(1)}, f32[5,48,256]{2,1,0:T(8,128)S(1)}, u32[]{:S(2)}, u32[]{:S(2)}) collective-permute-start(f32[5,48,256]{2,1,0:T(8,128)S(1)} %constant_dynamic-update-slice_fusion.here), channel_id=1, source_target_pairs={{0,1},{1,2},{2,3},{3,4},{4,5},{5,6},{6,7},{7,8},{8,9},{9,10},{10,1... | collective-permute-start | bytes 737288 | tf_op jit(solution)/shard_map/ppermute | solution.py:383
  72.0 11.9 %collective-permute-start.9 = (f32[5,48,256]{2,1,0:T(8,128)S(1)}, f32[5,48,256]{2,1,0:T(8,128)S(1)}, u32[]{:S(2)}, u32[]{:S(2)}) collective-permute-start(f32[5,48,256]{2,1,0:T(8,128)S(1)} %constant_dynamic-update-slice_fusion.here), channel_id=1, source_target_pairs={{1,0},{2,1},{3,2},{4,3},{5,4},{6,5},{7,6},{8,7},{9,8},{10,9},{11,1... | collective-permute-start | bytes 737288 | tf_op jit(solution)/shard_map/ppermute | solution.py:383
  88.7 4.8 %collective-permute-start.15 = (f32[20,128]{1,0:T(8,128)S(1)}, f32[20,128]{1,0:T(8,128)S(1)}, u32[]{:S(2)}, u32[]{:S(2)}) collective-permute-start(f32[20,128]{1,0:T(8,128)S(1)} %get-tuple-element.26), channel_id=1, source_target_pairs={{64,0},{128,64},{192,128},{256,192},{320,256},{384,320},{448,384},... | collective-permute-start | bytes 30728 | tf_op jit(solution)/shard_map/ppermute | solution.py:383
  91.6 6.2 %collective-permute-start.14 = (f32[20,128]{1,0:T(8,128)S(1)}, f32[20,128]{1,0:T(8,128)S(1)}, u32[]{:S(2)}, u32[]{:S(2)}) collective-permute-start(f32[20,128]{1,0:T(8,128)S(1)} %get-tuple-element.26), channel_id=1, source_target_pairs={{0,64},{64,128},{128,192},{192,256},{256,320},{320,384},{384,448},... | collective-permute-start | bytes 30728 | tf_op jit(solution)/shard_map/ppermute | solution.py:383
  97.9 27.9 %collective-permute-start.16 = (f32[3,20,128]{2,1,0:T(8,128)S(1)}, f32[3,20,128]{2,1,0:T(8,128)S(1)}, u32[]{:S(2)}, u32[]{:S(2)}) collective-permute-start(f32[3,20,128]{2,1,0:T(8,128)S(1)} %pad_maximum_fusion.here), channel_id=1, source_target_pairs={{0,1},{1,2},{2,3},{3,4},{4,5},{5,6},{6,7},{7,8},{8,9},{9,10},{10,1... | collective-permute-start | bytes 92168 | tf_op jit(solution)/shard_map/ppermute | solution.py:383
  99.8 26.0 %collective-permute-start.17 = (f32[3,20,128]{2,1,0:T(8,128)S(1)}, f32[3,20,128]{2,1,0:T(8,128)S(1)}, u32[]{:S(2)}, u32[]{:S(2)}) collective-permute-start(f32[3,20,128]{2,1,0:T(8,128)S(1)} %pad_maximum_fusion.here), channel_id=1, source_target_pairs={{1,0},{2,1},{3,2},{4,3},{5,4},{6,5},{7,6},{8,7},{9,8},{10,9},{11,1... | collective-permute-start | bytes 92168 | tf_op jit(solution)/shard_map/ppermute | solution.py:383
  107.2 9.0 %collective-permute-start.10 = (f32[20,128]{1,0:T(8,128)S(1)}, f32[20,128]{1,0:T(8,128)S(1)}, u32[]{:S(2)}, u32[]{:S(2)}) collective-permute-start(f32[20,128]{1,0:T(8,128)S(1)} %get-tuple-element.26), channel_id=1, source_target_pairs={{0,128},{64,192},{128,256},{192,320},{256,384},{320,448},{384,512}... | collective-permute-start | bytes 30728 | tf_op jit(solution)/shard_map/ppermute | solution.py:383
  109.1 15.2 %collective-permute-start.11 = (f32[20,128]{1,0:T(8,128)S(1)}, f32[20,128]{1,0:T(8,128)S(1)}, u32[]{:S(2)}, u32[]{:S(2)}) collective-permute-start(f32[20,128]{1,0:T(8,128)S(1)} %get-tuple-element.26), channel_id=1, source_target_pairs={{128,0},{192,64},{256,128},{320,192},{384,256},{448,320},{512,384}... | collective-permute-start | bytes 30728 | tf_op jit(solution)/shard_map/ppermute | solution.py:383
  114.3 10.1 %collective-permute-start.12 = (f32[20,128]{1,0:T(8,128)S(1)}, f32[20,128]{1,0:T(8,128)S(1)}, u32[]{:S(2)}, u32[]{:S(2)}) collective-permute-start(f32[20,128]{1,0:T(8,128)S(1)} %get-tuple-element.26), channel_id=1, source_target_pairs={{0,2},{1,3},{2,4},{3,5},{4,6},{5,7},{6,8},{7,9},{8,10},{9,11},{10,... | collective-permute-start | bytes 30728 | tf_op jit(solution)/shard_map/ppermute | solution.py:383
  116.2 9.5 %collective-permute-start.13 = (f32[20,128]{1,0:T(8,128)S(1)}, f32[20,128]{1,0:T(8,128)S(1)}, u32[]{:S(2)}, u32[]{:S(2)}) collective-permute-start(f32[20,128]{1,0:T(8,128)S(1)} %get-tuple-element.26), channel_id=1, source_target_pairs={{2,0},{3,1},{4,2},{5,3},{6,4},{7,5},{8,6},{9,7},{10,8},{11,9},{12,... | collective-permute-start | bytes 30728 | tf_op jit(solution)/shard_map/ppermute | solution.py:383

commit v2 on v1

--- a/solution.py
+++ b/solution.py
@@ -1,3 +1,5 @@
+import functools
+
 import jax
 import jax.numpy as jnp
 from jax import lax
@@ -17,15 +19,15 @@
     return lax.broadcasted_iota(jnp.int32, shape, dim)
 
 
-def call(body, outs, args, scratch=(), flops=1_000_000, nbytes=2_000_000):
+def call(body, outs, args, scratch=(), flops=1_000_000, nbytes=2_000_000, space=pltpu.VMEM, grant=48 << 10):
     vmem = pl.BlockSpec(memory_space=pltpu.VMEM)
     return pl.pallas_call(
         body,
         out_shape=outs,
-        in_specs=[vmem] * len(args),
+        in_specs=[pl.BlockSpec(memory_space=space)] * len(args),
         out_specs=jax.tree.map(lambda _: vmem, outs),
         scratch_shapes=list(scratch),
-        compiler_params=pltpu.CompilerParams(vmem_limit_bytes=48 << 20),
+        compiler_params=pltpu.CompilerParams(vmem_limit_bytes=grant << 10),
         cost_estimate=pl.CostEstimate(flops=flops, bytes_accessed=nbytes, transcendentals=0),
     )(*args)
 
@@ -38,29 +40,36 @@
     return jnp.where(iota(first.shape, 0) >= 4, first, pltpu.roll(second, 4, 0))
 
 
-def pack_body(u, f, a, bx, by, bz, xl, xh, yl, yh):
-    fields = (u, f, a, bx, by, bz)
-    cut = bx[3].astype(F32)
+def pack_body(u, f, a, bx, by, bz, own, xl, xh, yl, yh, uv, fv, av, bxv, byv, bzv, sems):
+    fields = (uv, fv, av, bxv, byv, bzv)
+    copies = [pltpu.make_async_copy(src, dst, sems.at[k]) for k, (src, dst) in enumerate(zip((u, f, a, bx, by, bz), fields))]
+    for copy in copies:
+        copy.start()
+    for copy in copies:
+        copy.wait()
+    cut = bxv[3].astype(F32)
     for k, ref in enumerate(fields):
         for j in range(H):
             low, high = ref[j].astype(F32), ref[4 + j].astype(F32)
+            own[k * 8 + j] = low
+            own[k * 8 + 4 + j] = high
             if j == 3:
                 if k == F:
-                    low = low + cut * u[4]
+                    low = low + cut * uv[4]
                 elif k == A:
                     low = low + cut
                 elif k == BX:
                     low = jnp.zeros_like(low)
             if j == 0:
                 if k == F:
-                    high = high + cut * u[3]
+                    high = high + cut * uv[3]
                 elif k == A:
                     high = high + cut
             xl[k * H + j] = low
             xh[k * H + j] = high
     row = iota(u.shape[1:], 0)
     for p in range(u.shape[0]):
-        v = [ref[p].astype(F32) for ref in fields]
+        v = [own[k * 8 + p] for k in range(6)]
         face = v[BY]
         low = list(v)
         low[F] = v[F] + jnp.where(row == 3, face * pltpu.roll(v[U], 7, 0), 0.0)
@@ -75,9 +84,15 @@
             yh[n * 8 + p] = pair_high(high[i], high[j])
 
 
-def corner_body(xlr, xhr, ycl, ych):
+def beside(count):
+    at = lax.axis_index("gx")
+    return [jnp.where(at >= d, 1.0, 0.0) if s < 0 else jnp.where(at < count - d, 1.0, 0.0) for d in (1, 2) for s in (-1, 1)]
+
+
+def corner_body(count, xlr, xhr, ycl, ych):
+    lower, upper = beside(count)[:2]
     for p in range(8):
-        v = [xhr[k * H + p] if p < 4 else xlr[k * H + p - 4] for k in range(6)]
+        v = [xhr[k * H + p] * lower if p < 4 else xlr[k * H + p - 4] * upper for k in range(6)]
         for n, (i, j) in enumerate(PAIRS):
             ycl[n * 8 + p] = pair_low(v[i], v[j])
             ych[n * 8 + p] = pair_high(v[i], v[j])
@@ -117,30 +132,30 @@
     return jnp.where(iota(face.shape, face.ndim - 1) == 0, 0.0, pltpu.roll(face, 1, face.ndim - 1))
 
 
-def coarse_body(a, bx, by, bz, xhr, yhr, c1, c2, rows, edge, fine, small):
-    nz = a.shape[2]
+def coarse_body(count, own, xhr, yhr, c1, c2, rows, edge, fine, small):
+    nz = own.shape[2]
     both, odd = halves(nz)
     both2, odd2 = halves(nz // 2)
 
     def even_odd(n):
         return every_other(rows, 0, n, nz), every_other(rows, 1, n, nz)
 
-    def pairs(ref):
+    def pairs(k):
         for i in range(4):
-            put(rows, 8 * i, ref[2 * i].astype(F32) + ref[2 * i + 1].astype(F32))
+            put(rows, 8 * i, own[k * 8 + 2 * i] + own[k * 8 + 2 * i + 1])
         return even_odd(16)
 
-    e, o = pairs(a)
+    e, o = pairs(A)
     a_in = e + o
-    e, o = pairs(bz)
+    e, o = pairs(BZ)
     bz_in = e + o
-    e, o = pairs(by)
+    e, o = pairs(BY)
     by_in = o
     for i in range(4):
-        put(rows, 8 * i, bx[2 * i + 1].astype(F32))
+        put(rows, 8 * i, own[BX * 8 + 2 * i + 1])
     e, o = even_odd(16)
     bx_in = e + o
-    put(rows, 0, xhr[BX * H + 3])
+    put(rows, 0, xhr[BX * H + 3] * beside(count)[0])
     e, o = even_odd(4)
     edge[0:4] = e + o
     for i in range(4):
@@ -235,7 +250,7 @@
     return ((weights[0, w] + x) + (y + z)), here
 
 
-def smooth(weights, held, reach):
+def smooth(weights, held, unroll):
     count = weights.shape[1]
     spare = (weights.shape[2], weights.shape[3])
     parity = (iota(spare, 0) + iota(spare, 1)) % 2
@@ -246,14 +261,17 @@
             held[w + 1] = jnp.where((parity + w + step) % 2 == 0, new, here)
             return carry
 
-        first = step
-        lax.fori_loop(first, count - first, one, 0)
-
-
-def fine_body(u, f, a, bx, by, bz, xlr, xhr, ylr, yhr, yclr, ychr, c1, out, p1, win, weights, held, diag, rows):
-    own = (u, f, a, bx, by, bz)
-    nz = u.shape[2]
-    upper = iota((8, nz), 0) >= 4
+        if unroll:
+            for w in range(step, count - step):
+                one(w, 0)
+        else:
+            lax.fori_loop(step, count - step, one, 0, unroll=2)
+
+
+def fine_body(count, own, xlr, xhr, ylr, yhr, yclr, ychr, c1, out, p1, win, weights, held, diag, rows):
+    nz = own.shape[2]
+    first = iota((8, nz), 0) < 4
+    lower, upper = beside(count)[:2]
 
     for w in range(16):
         for n, pair in enumerate(PAIRS):
@@ -265,24 +283,22 @@
                 below, above = ychr[n * 8 + w - 8], yclr[n * 8 + w - 8]
             for side, k in enumerate(pair):
                 if side:
-                    below, above = pltpu.roll(below, 4, 0), pltpu.roll(above, 4, 0)
+                    halo = pltpu.roll(jnp.where(first, below, above), 4, 0)
+                else:
+                    halo = jnp.where(first, above, below)
                 if w < 4:
-                    mid = xhr[k * H + w]
+                    mid = xhr[k * H + w] * lower
                 elif w < 12:
-                    mid = own[k][w - 4].astype(F32)
+                    mid = own[k * 8 + w - 4]
                 else:
-                    mid = xlr[k * H + w - 12]
-                low = jnp.where(upper, below, 0.0)
-                high = jnp.where(upper, 0.0, above)
+                    mid = xlr[k * H + w - 12] * upper
                 if k == U:
-                    held[w + 1, 0:8] = low
-                    held[w + 1, 8:16] = mid
-                    held[w + 1, 16:24] = high
+                    held[w + 1, 0:8] = mid
+                    held[w + 1, 8:16] = halo
                 else:
-                    win[k - 1, w + 1, 0:8] = low
-                    win[k - 1, w + 1, 8:16] = mid
-                    win[k - 1, w + 1, 16:24] = high
-    zero = jnp.zeros((24, nz), F32)
+                    win[k - 1, w + 1, 0:8] = mid
+                    win[k - 1, w + 1, 8:16] = halo
+    zero = jnp.zeros((16, nz), F32)
     held[0] = zero
     held[17] = zero
     win[BX - 1, 0] = zero
@@ -294,18 +310,18 @@
         inside = av > 0.0
         inverse = jnp.where(inside, 1.0 / jnp.where(inside, total, 1.0), 0.0)
         set_weights(weights, w, inverse, win[F - 1, w + 1], bxv, low_x, byv, bzv)
-        diag[w] = total[8:16]
+        diag[w] = total[0:8]
         return carry
 
-    lax.fori_loop(0, 16, prepare, 0)
-    smooth(weights, held, H)
+    lax.fori_loop(0, 16, prepare, 0, unroll=2)
+    smooth(weights, held, False)
     for i in range(4):
         total = None
         for j in range(2):
             w = 4 + 2 * i + j
             new, here = relaxed(weights, held, w)
-            out[w - 4] = here[8:16]
-            res = diag[w] * (new[8:16] - here[8:16])
+            out[w - 4] = here[0:8]
+            res = diag[w] * (new[0:8] - here[0:8])
             total = res if total is None else total + res
         put(rows, 8 * i, total)
     both, _ = halves(nz)
@@ -314,36 +330,40 @@
         p1[1 + k] = c1[k]
 
 
-def middle_body(below, here, above, c2, out, p2, win, weights, held, rows):
-    nz = below.shape[2]
+def middle_body(count, left, here, right, c2, out, p2, win, weights, held, rows):
+    nz = here.shape[3]
+    first = iota((8, nz), 0) < 4
+    lower, upper = beside(count)[:2]
     zero = jnp.zeros((16, nz), F32)
-    for k in range(5):
-        for w in range(12):
-            win[k, w + 1, 0:4] = jnp.zeros((4, nz), F32)
-            win[k, w + 1, 4:8] = below[k, 4 * w : 4 * w + 4]
-            win[k, w + 1, 8:12] = here[k, 4 * w : 4 * w + 4]
-            win[k, w + 1, 12:16] = above[k, 4 * w : 4 * w + 4]
     win[2, 0] = zero
-
-    def prepare(w, carry):
+    for b, (source, there) in enumerate(((left, lower), (here, None), (right, upper))):
+        for k in range(5):
+            for half in range(2):
+                at = slice(8 * half, 8 * half + 8)
+                below, mid, above = source[0, k, at], source[1, k, at], source[2, k, at]
+                if k == 1 and there is not None:
+                    below, mid, above = below * there, mid * there, above * there
+                w = 4 * b + 2 * half + 1
+                win[k, w, 0:8] = jnp.where(first, mid, pltpu.roll(above, 4, 0))
+                win[k, w, 8:16] = jnp.where(first, 0.0, pltpu.roll(below, 4, 0))
+                win[k, w + 1, 0:8] = jnp.where(first, pltpu.roll(mid, 4, 0), above)
+                win[k, w + 1, 8:16] = jnp.where(first, 0.0, below)
+    for w in range(12):
         total = win[1, w + 1]
         inside = total > 0.0
         inverse = jnp.where(inside, 0.25 / jnp.where(inside, total, 1.0), 0.0)
         set_weights(weights, w, inverse, 4.0 * win[0, w + 1], win[2, w + 1], win[2, w], win[3, w + 1], win[4, w + 1])
         held[w + 1] = zero
-        return carry
-
-    lax.fori_loop(0, 12, prepare, 0)
     held[0] = zero
     held[13] = zero
-    smooth(weights, held, H)
+    smooth(weights, held, True)
     for i in range(2):
         total = None
         for j in range(2):
             w = 4 + 2 * i + j
             new, now = relaxed(weights, held, w)
-            out[w - 4] = now[8:12]
-            res = win[1, w + 1, 8:16] * (new[8:16] - now[8:16])
+            out[w - 4] = now[0:4]
+            res = win[1, w + 1, 0:8] * (new[0:8] - now[0:8])
             total = res if total is None else total + res
         put(rows, 8 * i, total)
     both, _ = halves(nz)
@@ -353,34 +373,39 @@
     p2[4:20] = c2[...]
 
 
-def coarse_level_body(left, right, down, up, below, here, above, out, win, weights, held):
-    nz = left.shape[1]
+def coarse_level_body(count, left, mid, right, down, up, out, win, weights, held):
     win[...] = jnp.zeros(win.shape, F32)
+    near = beside(count)
     for k in range(5):
-        win[k, 1, 3:5] = left[4 * k + 2 : 4 * k + 4]
-        win[k, 8, 3:5] = right[4 * k : 4 * k + 2]
+        factor = near if k == 1 else [1.0] * 4
+        win[k, 1, 3:5] = left[3, 4 * k + 2 : 4 * k + 4] * factor[2]
+        win[k, 8, 3:5] = right[3, 4 * k : 4 * k + 2] * factor[3]
         for i in range(2):
             at = 4 * k + 2 * i
             win[k, 4 + i, 0:1] = down[at + 1 : at + 2]
             win[k, 4 + i, 7:8] = up[at : at + 1]
-            for b in range(3):
-                win[k, 2 + 2 * b + i, 1:3] = below[b, at : at + 2]
-                win[k, 2 + 2 * b + i, 3:5] = here[b, at : at + 2]
-                win[k, 2 + 2 * b + i, 5:7] = above[b, at : at + 2]
+            for b, (source, there) in enumerate(((left, factor[0]), (mid, 1.0), (right, factor[1]))):
+                for j in range(3):
+                    win[k, 2 + 2 * b + i, 1 + 2 * j : 3 + 2 * j] = source[j, at : at + 2] * there
     held[...] = jnp.zeros(held.shape, F32)
     for w in range(8):
         total = win[1, w + 1]
         inside = total > 0.0
         inverse = jnp.where(inside, 0.0625 / jnp.where(inside, total, 1.0), 0.0)
         set_weights(weights, w, inverse, 16.0 * win[0, w + 1], win[2, w + 1], win[2, w], win[3, w + 1], win[4, w + 1])
-    smooth(weights, held, 3)
+    smooth(weights, held, True)
     for i in range(2):
         out[i] = held[4 + i, 3:5]
 
 
-def moved(block, axis, by):
-    count = lax.axis_size(axis)
-    return lax.ppermute(block, axis, [(i, i + by) for i in range(count) if 0 <= i + by < count])
+def along_y(block, by):
+    count = lax.axis_size("gy")
+    return lax.ppermute(block, "gy", [(i, i + by) for i in range(count) if 0 <= i + by < count])
+
+
+def round_x(block, by):
+    count = lax.axis_size("gx")
+    return lax.ppermute(block, "gx", [(i, (i + by) % count) for i in range(count)])
 
 
 def shape(*dims):
@@ -388,18 +413,26 @@
 
 
 def shards(solution, right_side, alpha, beta_x, beta_y, beta_z):
-    own = (solution, right_side, alpha, beta_x, beta_y, beta_z)
+    args = (solution, right_side, alpha, beta_x, beta_y, beta_z)
     nz = solution.shape[2]
+    count = lax.axis_size("gx")
     sent = shape(24, 8, nz)
-    xl, xh, yl, yh = call(pack_body, (sent,) * 4, own)
-    xlr, xhr = moved(xl, "gx", -1), moved(xh, "gx", 1)
-    ylr, yhr = moved(yl, "gy", -1), moved(yh, "gy", 1)
-    ycl, ych = call(corner_body, (sent,) * 2, (xlr, xhr))
-    yclr, ychr = moved(ycl, "gy", -1), moved(ych, "gy", 1)
+    own, xl, xh, yl, yh = call(
+        pack_body,
+        (shape(48, 8, nz),) + (sent,) * 4,
+        args,
+        [pltpu.VMEM(x.shape, x.dtype) for x in args] + [pltpu.SemaphoreType.DMA((6,))],
+        space=pltpu.HBM,
+        grant=56 << 10,
+    )
+    xlr, xhr = round_x(xl, -1), round_x(xh, 1)
+    ylr, yhr = along_y(yl, -1), along_y(yh, 1)
+    ycl, ych = call(functools.partial(corner_body, count), (sent,) * 2, (xlr, xhr))
+    yclr, ychr = along_y(ycl, -1), along_y(ych, 1)
     c1, c2 = call(
-        coarse_body,
+        functools.partial(coarse_body, count),
         (shape(4, 16, nz // 2), shape(16, nz // 4)),
-        (alpha, beta_x, beta_y, beta_z, xhr, yhr),
+        (own, xhr, yhr),
         [
             pltpu.VMEM((nz // 128, 32, 128), F32),
             pltpu.VMEM((8, nz), F32),
@@ -408,25 +441,25 @@
         ],
     )
     fine, p1 = call(
-        fine_body,
+        functools.partial(fine_body, count),
         (shape(8, 8, nz), shape(5, 16, nz // 2)),
-        (*own, xlr, xhr, ylr, yhr, yclr, ychr, c1),
+        (own, xlr, xhr, ylr, yhr, yclr, ychr, c1),
         [
-            pltpu.VMEM((5, 17, 24, nz), F32),
-            pltpu.VMEM((7, 16, 24, nz), F32),
-            pltpu.VMEM((18, 24, nz), F32),
+            pltpu.VMEM((5, 17, 16, nz), F32),
+            pltpu.VMEM((7, 16, 16, nz), F32),
+            pltpu.VMEM((18, 16, nz), F32),
             pltpu.VMEM((16, 8, nz), F32),
             pltpu.VMEM((nz // 128, 32, 128), F32),
         ],
         flops=20_000_000,
         nbytes=20_000_000,
     )
-    here = jnp.concatenate([moved(p1, "gx", 1), p1, moved(p1, "gx", -1)], axis=1)
-    below, above = moved(here, "gy", 1), moved(here, "gy", -1)
+    here = jnp.stack([along_y(p1, 1), p1, along_y(p1, -1)])
+    left, right = round_x(here, 1), round_x(here, -1)
     middle, p2 = call(
-        middle_body,
+        functools.partial(middle_body, count),
         (shape(4, 4, nz // 2), shape(20, nz // 4)),
-        (below, here, above, c2),
+        (left, here, right, c2),
         [
             pltpu.VMEM((5, 13, 16, nz // 2), F32),
             pltpu.VMEM((7, 12, 16, nz // 2), F32),
@@ -434,14 +467,15 @@
             pltpu.VMEM((nz // 256, 16, 128), F32),
         ],
     )
-    left, right = moved(p2, "gx", 2), moved(p2, "gx", -2)
-    down, up = moved(p2, "gy", 2), moved(p2, "gy", -2)
-    here = jnp.stack([moved(p2, "gx", 1), p2, moved(p2, "gx", -1)])
-    below, above = moved(here, "gy", 1), moved(here, "gy", -1)
+    before, after = round_x(p2, 1), round_x(p2, -1)
+    below, above = along_y(p2, 1), along_y(p2, -1)
+    down, up = along_y(p2, 2), along_y(p2, -2)
+    left = round_x(jnp.stack([below, p2, above, before]), 1)
+    right = round_x(jnp.stack([below, p2, above, after]), -1)
     coarse = call(
-        coarse_level_body,
+        functools.partial(coarse_level_body, count),
         shape(2, 2, nz // 4),
-        (left, right, down, up, below, here, above),
+        (left, jnp.stack([below, p2, above]), right, down, up),
         [
             pltpu.VMEM((5, 9, 8, nz // 4), F32),
             pltpu.VMEM((7, 8, 8, nz // 4), F32),

time: 129 us -> 99.2 us (0.77)
  the two profiles are of different devices: /device:TPU:72 before, /device:TPU:71 now
where the time goes in v2:
time: 99.2 us; the launch traced here: 98.8 us
  starting transfers between devices  57.4 us (58%)
  waiting for transfers between devices  30.3 us (31%)
  Pallas kernels  10.3 us (10%)
    ppermute x10, starting transfers between devices, along_y(): lax.ppermute(block, 'gy', [(i, i + by) for i in range(count) if 0 <= i +...  47.3 us
    ppermute x10, waiting for transfers between devices, along_y(): lax.ppermute(block, 'gy', [(i, i + by) for i in range(count) if 0 <= i +...  18.9 us
    ppermute x8, waiting for transfers between devices, round_x(): lax.ppermute(block, 'gx', [(i, (i + by) % count) for i in range(count)])  11.4 us
    pallas_call x6, Pallas kernels, call(): pl.pallas_call(body, out_shape=outs, in_specs=[pl.BlockSpec(memory_space=...  10.3 us
    ppermute x8, starting transfers between devices, round_x(): lax.ppermute(block, 'gx', [(i, (i + by) % count) for i in range(count)])  10 us
  transfers between devices with their start and end apart: 18, of which 10 were waited for; matrix products, arithmetic and copies ran while one was open for 0% of the time, Pallas kernels for 1%

profile of v2, /device:TPU:71, one launch (start us, length us, event | category | flops | bytes accessed | tf_op | source)
XLA Modules:
  0.0 98.8 jit_solution(15752661858404444234)
XLA Ops:
  0.6 2.6 %shard_map.85 = (f32[48,8,512]{2,1,0:T(8,128)}, f32[24,8,512]{2,1,0:T(8,128)}, f32[24,8,512]{2,1,0:T(8,128)}, f32[24,8,512]{2,1,0:T(8,128)}, f32[24,8,512]{2,1,0:T(8,128)}) custom-call(f32[8,8,512]{2,1,0:T(8,128)} %u.1, f32[8,8,512]{2,1,0:T(8,128)} %f.1, bf16[8,8,512]{2,1,0:T(8,128)(2,1)} %a.1, bf16[8,8,512]{2,1,0:T(8,128)(2,1)} %bx.1, ...), custom_call_target="tpu_custom_call" | custom-call | flops 1000000 | bytes 2000000 | tf_op jit(solution)/shard_map/pallas_call | solution.py:24
  3.2 0.0 copy-start
  3.2 0.7 collective-permute-start
  3.9 2.3 %collective-permute-start.1 = (f32[24,8,512]{2,1,0:T(8,128)}, f32[24,8,512]{2,1,0:T(8,128)S(1)}, u32[]{:S(2)}, u32[]{:S(2)}) collective-permute-start(f32[24,8,512]{2,1,0:T(8,128)} %get-tuple-element.18), channel_id=1, source_target_pairs={{0,64},{64,128},{128,192},{192,256},{256,320},{320,384},{384,448},... | collective-permute-start | bytes 1179656 | tf_op jit(solution)/shard_map/ppermute | solution.py:408
  6.2 16.8 %collective-permute-start.2 = (f32[24,8,512]{2,1,0:T(8,128)}, f32[24,8,512]{2,1,0:T(8,128)S(1)}, u32[]{:S(2)}, u32[]{:S(2)}) collective-permute-start(f32[24,8,512]{2,1,0:T(8,128)} %get-tuple-element.19), channel_id=1, source_target_pairs={{1,0},{2,1},{3,2},{4,3},{5,4},{6,5},{7,6},{8,7},{9,8},{10,9},{11,1... | collective-permute-start | bytes 1179656 | tf_op jit(solution)/shard_map/ppermute | solution.py:403
  23.0 1.9 %collective-permute-start.3 = (f32[24,8,512]{2,1,0:T(8,128)}, f32[24,8,512]{2,1,0:T(8,128)S(1)}, u32[]{:S(2)}, u32[]{:S(2)}) collective-permute-start(f32[24,8,512]{2,1,0:T(8,128)} %get-tuple-element.20), channel_id=1, source_target_pairs={{0,1},{1,2},{2,3},{3,4},{4,5},{5,6},{6,7},{7,8},{8,9},{9,10},{10,1... | collective-permute-start | bytes 1179656 | tf_op jit(solution)/shard_map/ppermute | solution.py:403
  25.0 0.0 collective-permute-done.xlr
  25.0 0.0 collective-permute-done.1.xhr
  25.0 0.1 shard_map.86
  25.1 6.7 %collective-permute-start.4 = (f32[24,8,512]{2,1,0:T(8,128)S(1)}, f32[24,8,512]{2,1,0:T(8,128)S(1)}, u32[]{:S(2)}, u32[]{:S(2)}) collective-permute-start(f32[24,8,512]{2,1,0:T(8,128)S(1)} %get-tuple-element.21), channel_id=1, source_target_pairs={{1,0},{2,1},{3,2},{4,3},{5,4},{6,5},{7,6},{8,7},{9,8},{10,9},{11,1... | collective-permute-start | bytes 1179656 | tf_op jit(solution)/shard_map/ppermute | solution.py:403
  31.8 1.9 %collective-permute-start.5 = (f32[24,8,512]{2,1,0:T(8,128)S(1)}, f32[24,8,512]{2,1,0:T(8,128)S(1)}, u32[]{:S(2)}, u32[]{:S(2)}) collective-permute-start(f32[24,8,512]{2,1,0:T(8,128)S(1)} %get-tuple-element.22), channel_id=1, source_target_pairs={{0,1},{1,2},{2,3},{3,4},{4,5},{5,6},{6,7},{7,8},{8,9},{9,10},{10,1... | collective-permute-start | bytes 1179656 | tf_op jit(solution)/shard_map/ppermute | solution.py:403
  33.7 4.5 %collective-permute-done.3.yhr = f32[24,8,512]{2,1,0:T(8,128)S(1)} collective-permute-done((f32[24,8,512]{2,1,0:T(8,128)}, f32[24,8,512]{2,1,0:T(8,128)S(1)}, u32[]{:S(2)}, u32[]{:S(2)}) %collective-permute-start.3) | collective-permute-done | bytes 393248 | tf_op jit(solution)/shard_map/ppermute | solution.py:403
  38.2 0.0 copy-done
  38.2 0.5 shard_map.87
  38.8 0.0 collective-permute-done.2.ylr
  38.8 1.1 %collective-permute-done.4.yclr = f32[24,8,512]{2,1,0:T(8,128)S(1)} collective-permute-done((f32[24,8,512]{2,1,0:T(8,128)S(1)}, f32[24,8,512]{2,1,0:T(8,128)S(1)}, u32[]{:S(2)}, u32[]{:S(2)}) %collective-permute-start.4) | collective-permute-done | bytes 393248 | tf_op jit(solution)/shard_map/ppermute | solution.py:403
  39.9 7.4 %collective-permute-done.5.ychr = f32[24,8,512]{2,1,0:T(8,128)S(1)} collective-permute-done((f32[24,8,512]{2,1,0:T(8,128)S(1)}, f32[24,8,512]{2,1,0:T(8,128)S(1)}, u32[]{:S(2)}, u32[]{:S(2)}) %collective-permute-start.5) | collective-permute-done | bytes 393248 | tf_op jit(solution)/shard_map/ppermute | solution.py:403
  47.3 4.8 %shard_map.88 = (f32[8,8,512]{2,1,0:T(8,128)}, f32[5,16,256]{2,1,0:T(8,128)S(1)}) custom-call(f32[48,8,512]{2,1,0:T(8,128)S(1)} %copy-done, f32[24,8,512]{2,1,0:T(8,128)S(1)} %collective-permute-done.xlr, f32[24,8,512]{2,1,0:T(8,128)S(1)} %collective-permute-done.1.xhr, f32[24,8,512]{2,1,0:T(8,128)S(1)} %collective-permute-done.2.ylr, ...), custom_call_target="tpu_custom_call" | custom-call | flops 20000000 | bytes 20000000 | tf_op jit(solution)/shard_map/pallas_call | solution.py:24
  52.1 1.9 %collective-permute-start.7 = (f32[5,16,256]{2,1,0:T(8,128)S(1)}, f32[5,16,256]{2,1,0:T(8,128)S(1)}, u32[]{:S(2)}, u32[]{:S(2)}) collective-permute-start(f32[5,16,256]{2,1,0:T(8,128)S(1)} %get-tuple-element.25), channel_id=1, source_target_pairs={{1,0},{2,1},{3,2},{4,3},{5,4},{6,5},{7,6},{8,7},{9,8},{10,9},{11,1... | collective-permute-start | bytes 245768 | tf_op jit(solution)/shard_map/ppermute | solution.py:403
  54.0 3.4 %collective-permute-start.6 = (f32[5,16,256]{2,1,0:T(8,128)S(1)}, f32[5,16,256]{2,1,0:T(8,128)S(1)}, u32[]{:S(2)}, u32[]{:S(2)}) collective-permute-start(f32[5,16,256]{2,1,0:T(8,128)S(1)} %get-tuple-element.25), channel_id=1, source_target_pairs={{0,1},{1,2},{2,3},{3,4},{4,5},{5,6},{6,7},{7,8},{8,9},{9,10},{10,1... | collective-permute-start | bytes 245768 | tf_op jit(solution)/shard_map/ppermute | solution.py:403
  57.4 0.4 collective-permute-done.7
  57.8 5.2 %collective-permute-done.6 = f32[5,16,256]{2,1,0:T(8,128)S(1)} collective-permute-done((f32[5,16,256]{2,1,0:T(8,128)S(1)}, f32[5,16,256]{2,1,0:T(8,128)S(1)}, u32[]{:S(2)}, u32[]{:S(2)}) %collective-permute-start.6) | collective-permute-done | bytes 81952 | tf_op jit(solution)/shard_map/ppermute | solution.py:403
  63.1 2.9 %collective-permute-start.8 = (f32[3,5,16,256]{3,2,1,0:T(8,128)S(1)}, f32[3,5,16,256]{3,2,1,0:T(8,128)S(1)}, u32[]{:S(2)}, u32[]{:S(2)}) collective-permute-start(f32[3,5,16,256]{3,2,1,0:T(8,128)S(1)} %pad_maximum_fusion.here), channel_id=1, source_target_pairs={{0,64},{64,128},{128,192},{192,256},{256,320},{320,384},{384,448},... | collective-permute-start | bytes 737288 | tf_op jit(solution)/shard_map/ppermute | solution.py:408
  66.0 0.0 collective-permute-start.9
  66.0 3.1 %collective-permute-done.8.left = f32[3,5,16,256]{3,2,1,0:T(8,128)S(1)} collective-permute-done((f32[3,5,16,256]{3,2,1,0:T(8,128)S(1)}, f32[3,5,16,256]{3,2,1,0:T(8,128)S(1)}, u32[]{:S(2)}, u32[]{:S(2)}) %collective-permute-start.8) | collective-permute-done | bytes 245792 | tf_op jit(solution)/shard_map/ppermute | solution.py:408
  69.1 3.7 %collective-permute-done.9.right = f32[3,5,16,256]{3,2,1,0:T(8,128)S(1)} collective-permute-done((f32[3,5,16,256]{3,2,1,0:T(8,128)S(1)}, f32[3,5,16,256]{3,2,1,0:T(8,128)S(1)}, u32[]{:S(2)}, u32[]{:S(2)}) %collective-permute-start.9) | collective-permute-done | bytes 245792 | tf_op jit(solution)/shard_map/ppermute | solution.py:408
  72.8 1.4 %shard_map.89 = (f32[4,4,256]{2,1,0:T(4,128)}, f32[20,128]{1,0:T(8,128)S(1)}) custom-call(f32[3,5,16,256]{3,2,1,0:T(8,128)S(1)} %collective-permute-done.8.left, f32[3,5,16,256]{3,2,1,0:T(8,128)S(1)} %pad_maximum_fusion.here, f32[3,5,16,256]{3,2,1,0:T(8,128)S(1)} %collective-permute-done.9.right, f32[16,128]{1,0:T(8,128)S(1)} %get-tuple-element.26.c2), custom_call_target="tpu_custom_call" | custom-call | flops 1000000 | bytes 2000000 | tf_op jit(solution)/shard_map/pallas_call | solution.py:24
  74.2 0.0 collective-permute-start.14
  74.2 1.9 %collective-permute-start.11 = (f32[20,128]{1,0:T(8,128)S(1)}, f32[20,128]{1,0:T(8,128)S(1)}, u32[]{:S(2)}, u32[]{:S(2)}) collective-permute-start(f32[20,128]{1,0:T(8,128)S(1)} %get-tuple-element.28), channel_id=1, source_target_pairs={{1,0},{2,1},{3,2},{4,3},{5,4},{6,5},{7,6},{8,7},{9,8},{10,9},{11,1... | collective-permute-start | bytes 30728 | tf_op jit(solution)/shard_map/ppermute | solution.py:403
  76.1 3.4 %collective-permute-start.10 = (f32[20,128]{1,0:T(8,128)S(1)}, f32[20,128]{1,0:T(8,128)S(1)}, u32[]{:S(2)}, u32[]{:S(2)}) collective-permute-start(f32[20,128]{1,0:T(8,128)S(1)} %get-tuple-element.28), channel_id=1, source_target_pairs={{0,1},{1,2},{2,3},{3,4},{4,5},{5,6},{6,7},{7,8},{8,9},{9,10},{10,1... | collective-permute-start | bytes 30728 | tf_op jit(solution)/shard_map/ppermute | solution.py:403
  79.5 3.5 %collective-permute-start.12 = (f32[20,128]{1,0:T(8,128)S(1)}, f32[20,128]{1,0:T(8,128)S(1)}, u32[]{:S(2)}, u32[]{:S(2)}) collective-permute-start(f32[20,128]{1,0:T(8,128)S(1)} %get-tuple-element.28), channel_id=1, source_target_pairs={{0,64},{64,128},{128,192},{192,256},{256,320},{320,384},{384,448},... | collective-permute-start | bytes 30728 | tf_op jit(solution)/shard_map/ppermute | solution.py:408
  83.0 1.9 %collective-permute-start.16 = (f32[20,128]{1,0:T(8,128)S(1)}, f32[20,128]{1,0:T(8,128)S(1)}, u32[]{:S(2)}, u32[]{:S(2)}) collective-permute-start(f32[20,128]{1,0:T(8,128)S(1)} %get-tuple-element.28), channel_id=1, source_target_pairs={{0,2},{1,3},{2,4},{3,5},{4,6},{5,7},{6,8},{7,9},{8,10},{9,11},{10,... | collective-permute-start | bytes 30728 | tf_op jit(solution)/shard_map/ppermute | solution.py:403
  84.9 0.0 collective-permute-done.14
  85.0 7.6 %collective-permute-start.17 = (f32[20,128]{1,0:T(8,128)S(1)}, f32[20,128]{1,0:T(8,128)S(1)}, u32[]{:S(2)}, u32[]{:S(2)}) collective-permute-start(f32[20,128]{1,0:T(8,128)S(1)} %get-tuple-element.28), channel_id=1, source_target_pairs={{2,0},{3,1},{4,2},{5,3},{6,4},{7,5},{8,6},{9,7},{10,8},{11,9},{12,... | collective-permute-start | bytes 30728 | tf_op jit(solution)/shard_map/ppermute | solution.py:403
  92.5 0.0 collective-permute-done.11
  92.6 0.0 collective-permute-done.10
  92.6 0.0 collective-permute-done.12
  92.6 0.6 collective-permute-start.13
  93.2 0.0 collective-permute-start.15
  93.2 0.0 collective-permute-done.16.down
  93.2 0.1 collective-permute-done.17.up
  93.4 1.0 %collective-permute-done.13.left = f32[4,20,128]{2,1,0:T(8,128)S(1)} collective-permute-done((f32[4,20,128]{2,1,0:T(8,128)S(1)}, f32[4,20,128]{2,1,0:T(8,128)S(1)}, u32[]{:S(2)}, u32[]{:S(2)}) %collective-permute-start.13) | collective-permute-done | bytes 40992 | tf_op jit(solution)/shard_map/ppermute | solution.py:408
  94.4 3.5 %collective-permute-done.15.right = f32[4,20,128]{2,1,0:T(8,128)S(1)} collective-permute-done((f32[4,20,128]{2,1,0:T(8,128)S(1)}, f32[4,20,128]{2,1,0:T(8,128)S(1)}, u32[]{:S(2)}, u32[]{:S(2)}) %collective-permute-start.15) | collective-permute-done | bytes 40992 | tf_op jit(solution)/shard_map/ppermute | solution.py:408
  97.9 0.9 shard_map.90
  (3 shorter events, 0.0 us)
Async XLA Ops:
  3.2 35.0 %copy-start = (f32[48,8,512]{2,1,0:T(8,128)S(1)}, f32[48,8,512]{2,1,0:T(8,128)}, u32[]{:S(2)}) copy-start(f32[48,8,512]{2,1,0:T(8,128)} %get-tuple-element.16.own) | copy-start | bytes 2359300
  3.2 21.7 %collective-permute-start = (f32[24,8,512]{2,1,0:T(8,128)}, f32[24,8,512]{2,1,0:T(8,128)S(1)}, u32[]{:S(2)}, u32[]{:S(2)}) collective-permute-start(f32[24,8,512]{2,1,0:T(8,128)} %get-tuple-element.17), channel_id=1, source_target_pairs={{0,960},{64,0},{128,64},{192,128},{256,192},{320,256},{384,320},{4... | collective-permute-start | bytes 1179656 | tf_op jit(solution)/shard_map/ppermute | solution.py:408
  3.9 21.1 %collective-permute-start.1 = (f32[24,8,512]{2,1,0:T(8,128)}, f32[24,8,512]{2,1,0:T(8,128)S(1)}, u32[]{:S(2)}, u32[]{:S(2)}) collective-permute-start(f32[24,8,512]{2,1,0:T(8,128)} %get-tuple-element.18), channel_id=1, source_target_pairs={{0,64},{64,128},{128,192},{192,256},{256,320},{320,384},{384,448},... | collective-permute-start | bytes 1179656 | tf_op jit(solution)/shard_map/ppermute | solution.py:408
  6.2 32.5 %collective-permute-start.2 = (f32[24,8,512]{2,1,0:T(8,128)}, f32[24,8,512]{2,1,0:T(8,128)S(1)}, u32[]{:S(2)}, u32[]{:S(2)}) collective-permute-start(f32[24,8,512]{2,1,0:T(8,128)} %get-tuple-element.19), channel_id=1, source_target_pairs={{1,0},{2,1},{3,2},{4,3},{5,4},{6,5},{7,6},{8,7},{9,8},{10,9},{11,1... | collective-permute-start | bytes 1179656 | tf_op jit(solution)/shard_map/ppermute | solution.py:403
  23.0 15.2 %collective-permute-start.3 = (f32[24,8,512]{2,1,0:T(8,128)}, f32[24,8,512]{2,1,0:T(8,128)S(1)}, u32[]{:S(2)}, u32[]{:S(2)}) collective-permute-start(f32[24,8,512]{2,1,0:T(8,128)} %get-tuple-element.20), channel_id=1, source_target_pairs={{0,1},{1,2},{2,3},{3,4},{4,5},{5,6},{6,7},{7,8},{8,9},{9,10},{10,1... | collective-permute-start | bytes 1179656 | tf_op jit(solution)/shard_map/ppermute | solution.py:403
  25.1 14.8 %collective-permute-start.4 = (f32[24,8,512]{2,1,0:T(8,128)S(1)}, f32[24,8,512]{2,1,0:T(8,128)S(1)}, u32[]{:S(2)}, u32[]{:S(2)}) collective-permute-start(f32[24,8,512]{2,1,0:T(8,128)S(1)} %get-tuple-element.21), channel_id=1, source_target_pairs={{1,0},{2,1},{3,2},{4,3},{5,4},{6,5},{7,6},{8,7},{9,8},{10,9},{11,1... | collective-permute-start | bytes 1179656 | tf_op jit(solution)/shard_map/ppermute | solution.py:403
  31.8 15.5 %collective-permute-start.5 = (f32[24,8,512]{2,1,0:T(8,128)S(1)}, f32[24,8,512]{2,1,0:T(8,128)S(1)}, u32[]{:S(2)}, u32[]{:S(2)}) collective-permute-start(f32[24,8,512]{2,1,0:T(8,128)S(1)} %get-tuple-element.22), channel_id=1, source_target_pairs={{0,1},{1,2},{2,3},{3,4},{4,5},{5,6},{6,7},{7,8},{8,9},{9,10},{10,1... | collective-permute-start | bytes 1179656 | tf_op jit(solution)/shard_map/ppermute | solution.py:403
  52.1 5.7 %collective-permute-start.7 = (f32[5,16,256]{2,1,0:T(8,128)S(1)}, f32[5,16,256]{2,1,0:T(8,128)S(1)}, u32[]{:S(2)}, u32[]{:S(2)}) collective-permute-start(f32[5,16,256]{2,1,0:T(8,128)S(1)} %get-tuple-element.25), channel_id=1, source_target_pairs={{1,0},{2,1},{3,2},{4,3},{5,4},{6,5},{7,6},{8,7},{9,8},{10,9},{11,1... | collective-permute-start | bytes 245768 | tf_op jit(solution)/shard_map/ppermute | solution.py:403
  54.0 9.0 %collective-permute-start.6 = (f32[5,16,256]{2,1,0:T(8,128)S(1)}, f32[5,16,256]{2,1,0:T(8,128)S(1)}, u32[]{:S(2)}, u32[]{:S(2)}) collective-permute-start(f32[5,16,256]{2,1,0:T(8,128)S(1)} %get-tuple-element.25), channel_id=1, source_target_pairs={{0,1},{1,2},{2,3},{3,4},{4,5},{5,6},{6,7},{7,8},{8,9},{9,10},{10,1... | collective-permute-start | bytes 245768 | tf_op jit(solution)/shard_map/ppermute | solution.py:403
  63.1 6.0 %collective-permute-start.8 = (f32[3,5,16,256]{3,2,1,0:T(8,128)S(1)}, f32[3,5,16,256]{3,2,1,0:T(8,128)S(1)}, u32[]{:S(2)}, u32[]{:S(2)}) collective-permute-start(f32[3,5,16,256]{3,2,1,0:T(8,128)S(1)} %pad_maximum_fusion.here), channel_id=1, source_target_pairs={{0,64},{64,128},{128,192},{192,256},{256,320},{320,384},{384,448},... | collective-permute-start | bytes 737288 | tf_op jit(solution)/shard_map/ppermute | solution.py:408
  66.0 6.8 %collective-permute-start.9 = (f32[3,5,16,256]{3,2,1,0:T(8,128)S(1)}, f32[3,5,16,256]{3,2,1,0:T(8,128)S(1)}, u32[]{:S(2)}, u32[]{:S(2)}) collective-permute-start(f32[3,5,16,256]{3,2,1,0:T(8,128)S(1)} %pad_maximum_fusion.here), channel_id=1, source_target_pairs={{0,960},{64,0},{128,64},{192,128},{256,192},{320,256},{384,320},{4... | collective-permute-start | bytes 737288 | tf_op jit(solution)/shard_map/ppermute | solution.py:408
  74.2 10.7 %collective-permute-start.14 = (f32[20,128]{1,0:T(8,128)S(1)}, f32[20,128]{1,0:T(8,128)S(1)}, u32[]{:S(2)}, u32[]{:S(2)}) collective-permute-start(f32[20,128]{1,0:T(8,128)S(1)} %get-tuple-element.28), channel_id=1, source_target_pairs={{0,960},{64,0},{128,64},{192,128},{256,192},{320,256},{384,320},{4... | collective-permute-start | bytes 30728 | tf_op jit(solution)/shard_map/ppermute | solution.py:408
  74.2 18.3 %collective-permute-start.11 = (f32[20,128]{1,0:T(8,128)S(1)}, f32[20,128]{1,0:T(8,128)S(1)}, u32[]{:S(2)}, u32[]{:S(2)}) collective-permute-start(f32[20,128]{1,0:T(8,128)S(1)} %get-tuple-element.28), channel_id=1, source_target_pairs={{1,0},{2,1},{3,2},{4,3},{5,4},{6,5},{7,6},{8,7},{9,8},{10,9},{11,1... | collective-permute-start | bytes 30728 | tf_op jit(solution)/shard_map/ppermute | solution.py:403
  76.1 16.4 %collective-permute-start.10 = (f32[20,128]{1,0:T(8,128)S(1)}, f32[20,128]{1,0:T(8,128)S(1)}, u32[]{:S(2)}, u32[]{:S(2)}) collective-permute-start(f32[20,128]{1,0:T(8,128)S(1)} %get-tuple-element.28), channel_id=1, source_target_pairs={{0,1},{1,2},{2,3},{3,4},{4,5},{5,6},{6,7},{7,8},{8,9},{9,10},{10,1... | collective-permute-start | bytes 30728 | tf_op jit(solution)/shard_map/ppermute | solution.py:403
  79.5 13.1 %collective-permute-start.12 = (f32[20,128]{1,0:T(8,128)S(1)}, f32[20,128]{1,0:T(8,128)S(1)}, u32[]{:S(2)}, u32[]{:S(2)}) collective-permute-start(f32[20,128]{1,0:T(8,128)S(1)} %get-tuple-element.28), channel_id=1, source_target_pairs={{0,64},{64,128},{128,192},{192,256},{256,320},{320,384},{384,448},... | collective-permute-start | bytes 30728 | tf_op jit(solution)/shard_map/ppermute | solution.py:408
  83.0 10.2 %collective-permute-start.16 = (f32[20,128]{1,0:T(8,128)S(1)}, f32[20,128]{1,0:T(8,128)S(1)}, u32[]{:S(2)}, u32[]{:S(2)}) collective-permute-start(f32[20,128]{1,0:T(8,128)S(1)} %get-tuple-element.28), channel_id=1, source_target_pairs={{0,2},{1,3},{2,4},{3,5},{4,6},{5,7},{6,8},{7,9},{8,10},{9,11},{10,... | collective-permute-start | bytes 30728 | tf_op jit(solution)/shard_map/ppermute | solution.py:403
  85.0 8.4 %collective-permute-start.17 = (f32[20,128]{1,0:T(8,128)S(1)}, f32[20,128]{1,0:T(8,128)S(1)}, u32[]{:S(2)}, u32[]{:S(2)}) collective-permute-start(f32[20,128]{1,0:T(8,128)S(1)} %get-tuple-element.28), channel_id=1, source_target_pairs={{2,0},{3,1},{4,2},{5,3},{6,4},{7,5},{8,6},{9,7},{10,8},{11,9},{12,... | collective-permute-start | bytes 30728 | tf_op jit(solution)/shard_map/ppermute | solution.py:403
  92.6 1.8 %collective-permute-start.13 = (f32[4,20,128]{2,1,0:T(8,128)S(1)}, f32[4,20,128]{2,1,0:T(8,128)S(1)}, u32[]{:S(2)}, u32[]{:S(2)}) collective-permute-start(f32[4,20,128]{2,1,0:T(8,128)S(1)} %get-tuple-element.30), channel_id=1, source_target_pairs={{0,64},{64,128},{128,192},{192,256},{256,320},{320,384},{384,448},... | collective-permute-start | bytes 122888 | tf_op jit(solution)/shard_map/ppermute | solution.py:408
  93.2 4.7 %collective-permute-start.15 = (f32[4,20,128]{2,1,0:T(8,128)S(1)}, f32[4,20,128]{2,1,0:T(8,128)S(1)}, u32[]{:S(2)}, u32[]{:S(2)}) collective-permute-start(f32[4,20,128]{2,1,0:T(8,128)S(1)} %get-tuple-element.29), channel_id=1, source_target_pairs={{0,960},{64,0},{128,64},{192,128},{256,192},{320,256},{384,320},{4... | collective-permute-start | bytes 122888 | tf_op jit(solution)/shard_map/ppermute | solution.py:408

commit v3 on v2

--- a/solution.py
+++ b/solution.py
@@ -89,13 +89,47 @@
     return [jnp.where(at >= d, 1.0, 0.0) if s < 0 else jnp.where(at < count - d, 1.0, 0.0) for d in (1, 2) for s in (-1, 1)]
 
 
-def corner_body(count, xlr, xhr, ycl, ych):
-    lower, upper = beside(count)[:2]
-    for p in range(8):
-        v = [xhr[k * H + p] * lower if p < 4 else xlr[k * H + p - 4] * upper for k in range(6)]
-        for n, (i, j) in enumerate(PAIRS):
-            ycl[n * 8 + p] = pair_low(v[i], v[j])
-            ych[n * 8 + p] = pair_high(v[i], v[j])
+CORNER = (
+    [(1, (k,)) for k in range(6)]
+    + [(2, (U,)), (2, (BY,)), (2, (BX,)), (2, (F, A)), (2, (BZ,))]
+    + [(3, (U, BY)), (3, (F, A)), (3, (BX, BZ)), (4, (U, BY)), (4, (BX,))]
+)
+
+
+def nearest(shape):
+    row = iota(shape, 0)
+    return (row < 2) | (row >= 6)
+
+
+def halo_rows(k, p, ylr, yhr):
+    n, side = next((n, pair.index(k)) for n, pair in enumerate(PAIRS) if k in pair)
+    above, below = ylr[n * 8 + p], yhr[n * 8 + p]
+    first = iota(above.shape, 0) < 4
+    if side:
+        return pltpu.roll(jnp.where(first, below, above), 4, 0)
+    return jnp.where(first, above, below)
+
+
+def corner_body(ylr, yhr, xcl, xch):
+    near = nearest(ylr.shape[1:])
+    for out, plane in ((xcl, lambda d: d - 1), (xch, lambda d: 8 - d)):
+        for t, (d, fields) in enumerate(CORNER):
+            tile = halo_rows(fields[0], plane(d), ylr, yhr)
+            if len(fields) == 2:
+                tile = jnp.where(near, tile, pltpu.roll(halo_rows(fields[1], plane(d), ylr, yhr), 4, 0))
+            out[t] = tile
+
+
+def corner_rows(k, d, tiles):
+    for t, (distance, fields) in enumerate(CORNER):
+        if distance == d and k in fields:
+            tile = tiles[t]
+            if len(fields) == 1:
+                return tile
+            if fields[1] == k:
+                tile = pltpu.roll(tile, 4, 0)
+            return jnp.where(nearest(tile.shape), tile, 0.0)
+    return jnp.zeros(tiles.shape[1:], F32)
 
 
 def halves(n):
@@ -268,36 +302,26 @@
             lax.fori_loop(step, count - step, one, 0, unroll=2)
 
 
-def fine_body(count, own, xlr, xhr, ylr, yhr, yclr, ychr, c1, out, p1, win, weights, held, diag, rows):
+def fine_body(count, own, xlr, xhr, ylr, yhr, xclr, xchr, c1, out, p1, win, weights, held, diag, rows):
     nz = own.shape[2]
-    first = iota((8, nz), 0) < 4
     lower, upper = beside(count)[:2]
 
     for w in range(16):
-        for n, pair in enumerate(PAIRS):
+        for k in range(6):
             if w < 4:
-                below, above = ychr[n * 8 + w], yclr[n * 8 + w]
+                mid, halo, there = xhr[k * H + w], corner_rows(k, 4 - w, xchr), lower
             elif w < 12:
-                below, above = yhr[n * 8 + w - 4], ylr[n * 8 + w - 4]
+                mid, halo, there = own[k * 8 + w - 4], halo_rows(k, w - 4, ylr, yhr), None
             else:
-                below, above = ychr[n * 8 + w - 8], yclr[n * 8 + w - 8]
-            for side, k in enumerate(pair):
-                if side:
-                    halo = pltpu.roll(jnp.where(first, below, above), 4, 0)
-                else:
-                    halo = jnp.where(first, above, below)
-                if w < 4:
-                    mid = xhr[k * H + w] * lower
-                elif w < 12:
-                    mid = own[k * 8 + w - 4]
-                else:
-                    mid = xlr[k * H + w - 12] * upper
-                if k == U:
-                    held[w + 1, 0:8] = mid
-                    held[w + 1, 8:16] = halo
-                else:
-                    win[k - 1, w + 1, 0:8] = mid
-                    win[k - 1, w + 1, 8:16] = halo
+                mid, halo, there = xlr[k * H + w - 12], corner_rows(k, w - 11, xclr), upper
+            if there is not None and k in (U, A, BX):
+                mid, halo = mid * there, halo * there
+            if k == U:
+                held[w + 1, 0:8] = mid
+                held[w + 1, 8:16] = halo
+            else:
+                win[k - 1, w + 1, 0:8] = mid
+                win[k - 1, w + 1, 8:16] = halo
     zero = jnp.zeros((16, nz), F32)
     held[0] = zero
     held[17] = zero
@@ -425,10 +449,10 @@
         space=pltpu.HBM,
         grant=56 << 10,
     )
+    ylr, yhr = along_y(yl, -1), along_y(yh, 1)
     xlr, xhr = round_x(xl, -1), round_x(xh, 1)
-    ylr, yhr = along_y(yl, -1), along_y(yh, 1)
-    ycl, ych = call(functools.partial(corner_body, count), (sent,) * 2, (xlr, xhr))
-    yclr, ychr = along_y(ycl, -1), along_y(ych, 1)
+    xcl, xch = call(corner_body, (shape(len(CORNER), 8, nz),) * 2, (ylr, yhr))
+    xclr, xchr = round_x(xcl, -1), round_x(xch, 1)
     c1, c2 = call(
         functools.partial(coarse_body, count),
         (shape(4, 16, nz // 2), shape(16, nz // 4)),
@@ -443,7 +467,7 @@
     fine, p1 = call(
         functools.partial(fine_body, count),
         (shape(8, 8, nz), shape(5, 16, nz // 2)),
-        (own, xlr, xhr, ylr, yhr, yclr, ychr, c1),
+        (own, xlr, xhr, ylr, yhr, xclr, xchr, c1),
         [
             pltpu.VMEM((5, 17, 16, nz), F32),
             pltpu.VMEM((7, 16, 16, nz), F32),

time: 99.2 us -> 96.2 us (0.970)
  starting transfers between devices: 57.4 us -> 53.6 us
    ppermute x10 -> x8, starting transfers between devices: 47.3 us -> 38.9 us  [along_y(): lax.ppermute(block, 'gy', [(i, i + by) for i in range(count) if 0 <= i +...]
    ppermute x8 -> x10, starting transfers between devices: 10 us -> 14.7 us  [round_x(): lax.ppermute(block, 'gx', [(i, (i + by) % count) for i in range(count)])]
    ppermute x8 -> x10, waiting for transfers between devices: 11.4 us -> 14.9 us  [round_x(): lax.ppermute(block, 'gx', [(i, (i + by) % count) for i in range(count)])]
    ppermute x10 -> x8, waiting for transfers between devices: 18.9 us -> 16.2 us  [along_y(): lax.ppermute(block, 'gy', [(i, i + by) for i in range(count) if 0 <= i +...]
where the time goes in v3:
time: 96.2 us; the launch traced here: 95.8 us
  starting transfers between devices  53.6 us (56%)
  waiting for transfers between devices  31 us (32%)
  Pallas kernels  10.3 us (11%)
    ppermute x8, starting transfers between devices, along_y(): lax.ppermute(block, 'gy', [(i, i + by) for i in range(count) if 0 <= i +...  38.9 us
    ppermute x8, waiting for transfers between devices, along_y(): lax.ppermute(block, 'gy', [(i, i + by) for i in range(count) if 0 <= i +...  16.2 us
    ppermute x10, waiting for transfers between devices, round_x(): lax.ppermute(block, 'gx', [(i, (i + by) % count) for i in range(count)])  14.9 us
    ppermute x10, starting transfers between devices, round_x(): lax.ppermute(block, 'gx', [(i, (i + by) % count) for i in range(count)])  14.7 us
    pallas_call x6, Pallas kernels, call(): pl.pallas_call(body, out_shape=outs, in_specs=[pl.BlockSpec(memory_space=...  10.3 us
  transfers between devices with their start and end apart: 18, of which 10 were waited for; matrix products, arithmetic and copies ran while one was open for 0% of the time, Pallas kernels for 1%

profile of v3, /device:TPU:71, one launch (start us, length us, event | category | flops | bytes accessed | tf_op | source)
XLA Modules:
  0.0 95.8 jit_solution(5440064811302354202)
XLA Ops:
  0.6 2.6 %shard_map.85 = (f32[48,8,512]{2,1,0:T(8,128)}, f32[24,8,512]{2,1,0:T(8,128)}, f32[24,8,512]{2,1,0:T(8,128)}, f32[24,8,512]{2,1,0:T(8,128)}, f32[24,8,512]{2,1,0:T(8,128)}) custom-call(f32[8,8,512]{2,1,0:T(8,128)} %u.1, f32[8,8,512]{2,1,0:T(8,128)} %f.1, bf16[8,8,512]{2,1,0:T(8,128)(2,1)} %a.1, bf16[8,8,512]{2,1,0:T(8,128)(2,1)} %bx.1, ...), custom_call_target="tpu_custom_call" | custom-call | flops 1000000 | bytes 2000000 | tf_op jit(solution)/shard_map/pallas_call | solution.py:24
  3.2 0.0 copy-start
  3.2 16.9 %collective-permute-start.2 = (f32[24,8,512]{2,1,0:T(8,128)}, f32[24,8,512]{2,1,0:T(8,128)S(1)}, u32[]{:S(2)}, u32[]{:S(2)}) collective-permute-start(f32[24,8,512]{2,1,0:T(8,128)} %get-tuple-element.19), channel_id=1, source_target_pairs={{1,0},{2,1},{3,2},{4,3},{5,4},{6,5},{7,6},{8,7},{9,8},{10,9},{11,1... | collective-permute-start | bytes 1179656 | tf_op jit(solution)/shard_map/ppermute | solution.py:427
  20.2 1.9 %collective-permute-start.3 = (f32[24,8,512]{2,1,0:T(8,128)}, f32[24,8,512]{2,1,0:T(8,128)S(1)}, u32[]{:S(2)}, u32[]{:S(2)}) collective-permute-start(f32[24,8,512]{2,1,0:T(8,128)} %get-tuple-element.20), channel_id=1, source_target_pairs={{0,1},{1,2},{2,3},{3,4},{4,5},{5,6},{6,7},{7,8},{8,9},{9,10},{10,1... | collective-permute-start | bytes 1179656 | tf_op jit(solution)/shard_map/ppermute | solution.py:427
  22.1 3.3 %collective-permute-start.1 = (f32[24,8,512]{2,1,0:T(8,128)}, f32[24,8,512]{2,1,0:T(8,128)S(1)}, u32[]{:S(2)}, u32[]{:S(2)}) collective-permute-start(f32[24,8,512]{2,1,0:T(8,128)} %get-tuple-element.18), channel_id=1, source_target_pairs={{0,64},{64,128},{128,192},{192,256},{256,320},{320,384},{384,448},... | collective-permute-start | bytes 1179656 | tf_op jit(solution)/shard_map/ppermute | solution.py:432
  25.4 0.0 collective-permute-start
  25.4 2.9 %collective-permute-done.2.ylr = f32[24,8,512]{2,1,0:T(8,128)S(1)} collective-permute-done((f32[24,8,512]{2,1,0:T(8,128)}, f32[24,8,512]{2,1,0:T(8,128)S(1)}, u32[]{:S(2)}, u32[]{:S(2)}) %collective-permute-start.2) | collective-permute-done | bytes 393248 | tf_op jit(solution)/shard_map/ppermute | solution.py:427
  28.2 7.0 %collective-permute-done.3.yhr = f32[24,8,512]{2,1,0:T(8,128)S(1)} collective-permute-done((f32[24,8,512]{2,1,0:T(8,128)}, f32[24,8,512]{2,1,0:T(8,128)S(1)}, u32[]{:S(2)}, u32[]{:S(2)}) %collective-permute-start.3) | collective-permute-done | bytes 393248 | tf_op jit(solution)/shard_map/ppermute | solution.py:427
  35.3 1.9 %collective-permute-start.4 = (f32[16,8,512]{2,1,0:T(8,128)S(1)}, f32[16,8,512]{2,1,0:T(8,128)S(1)}, u32[]{:S(2)}, u32[]{:S(2)}) collective-permute-start(f32[16,8,512]{2,1,0:T(8,128)S(1)} %get-tuple-element.21), channel_id=1, source_target_pairs={{0,960},{64,0},{128,64},{192,128},{256,192},{320,256},{384,320},{4... | collective-permute-start | bytes 786440 | tf_op jit(solution)/shard_map/ppermute | solution.py:432
  37.2 2.3 %collective-permute-start.5 = (f32[16,8,512]{2,1,0:T(8,128)S(1)}, f32[16,8,512]{2,1,0:T(8,128)S(1)}, u32[]{:S(2)}, u32[]{:S(2)}) collective-permute-start(f32[16,8,512]{2,1,0:T(8,128)S(1)} %get-tuple-element.22), channel_id=1, source_target_pairs={{0,64},{64,128},{128,192},{192,256},{256,320},{320,384},{384,448},... | collective-permute-start | bytes 786440 | tf_op jit(solution)/shard_map/ppermute | solution.py:432
  39.5 0.0 collective-permute-done.1.xhr
  39.5 0.0 copy-done
  39.5 0.5 shard_map.87
  40.1 0.0 collective-permute-done.xlr
  40.1 3.5 %collective-permute-done.4.xclr = f32[16,8,512]{2,1,0:T(8,128)S(1)} collective-permute-done((f32[16,8,512]{2,1,0:T(8,128)S(1)}, f32[16,8,512]{2,1,0:T(8,128)S(1)}, u32[]{:S(2)}, u32[]{:S(2)}) %collective-permute-start.4) | collective-permute-done | bytes 262176 | tf_op jit(solution)/shard_map/ppermute | solution.py:432
  43.5 0.0 collective-permute-done.5.xchr
  43.6 4.8 %shard_map.88 = (f32[8,8,512]{2,1,0:T(8,128)}, f32[5,16,256]{2,1,0:T(8,128)S(1)}) custom-call(f32[48,8,512]{2,1,0:T(8,128)S(1)} %copy-done, f32[24,8,512]{2,1,0:T(8,128)S(1)} %collective-permute-done.xlr, f32[24,8,512]{2,1,0:T(8,128)S(1)} %collective-permute-done.1.xhr, f32[24,8,512]{2,1,0:T(8,128)S(1)} %collective-permute-done.2.ylr, ...), custom_call_target="tpu_custom_call" | custom-call | flops 20000000 | bytes 20000000 | tf_op jit(solution)/shard_map/pallas_call | solution.py:24
  48.4 1.9 %collective-permute-start.7 = (f32[5,16,256]{2,1,0:T(8,128)S(1)}, f32[5,16,256]{2,1,0:T(8,128)S(1)}, u32[]{:S(2)}, u32[]{:S(2)}) collective-permute-start(f32[5,16,256]{2,1,0:T(8,128)S(1)} %get-tuple-element.25), channel_id=1, source_target_pairs={{1,0},{2,1},{3,2},{4,3},{5,4},{6,5},{7,6},{8,7},{9,8},{10,9},{11,1... | collective-permute-start | bytes 245768 | tf_op jit(solution)/shard_map/ppermute | solution.py:427
  50.3 3.4 %collective-permute-start.6 = (f32[5,16,256]{2,1,0:T(8,128)S(1)}, f32[5,16,256]{2,1,0:T(8,128)S(1)}, u32[]{:S(2)}, u32[]{:S(2)}) collective-permute-start(f32[5,16,256]{2,1,0:T(8,128)S(1)} %get-tuple-element.25), channel_id=1, source_target_pairs={{0,1},{1,2},{2,3},{3,4},{4,5},{5,6},{6,7},{7,8},{8,9},{9,10},{10,1... | collective-permute-start | bytes 245768 | tf_op jit(solution)/shard_map/ppermute | solution.py:427
  53.6 0.9 collective-permute-done.7
  54.5 5.2 %collective-permute-done.6 = f32[5,16,256]{2,1,0:T(8,128)S(1)} collective-permute-done((f32[5,16,256]{2,1,0:T(8,128)S(1)}, f32[5,16,256]{2,1,0:T(8,128)S(1)}, u32[]{:S(2)}, u32[]{:S(2)}) %collective-permute-start.6) | collective-permute-done | bytes 81952 | tf_op jit(solution)/shard_map/ppermute | solution.py:427
  59.8 3.1 %collective-permute-start.8 = (f32[3,5,16,256]{3,2,1,0:T(8,128)S(1)}, f32[3,5,16,256]{3,2,1,0:T(8,128)S(1)}, u32[]{:S(2)}, u32[]{:S(2)}) collective-permute-start(f32[3,5,16,256]{3,2,1,0:T(8,128)S(1)} %pad_maximum_fusion.here), channel_id=1, source_target_pairs={{0,64},{64,128},{128,192},{192,256},{256,320},{320,384},{384,448},... | collective-permute-start | bytes 737288 | tf_op jit(solution)/shard_map/ppermute | solution.py:432
  62.9 0.0 collective-permute-start.9
  62.9 3.1 %collective-permute-done.8.left = f32[3,5,16,256]{3,2,1,0:T(8,128)S(1)} collective-permute-done((f32[3,5,16,256]{3,2,1,0:T(8,128)S(1)}, f32[3,5,16,256]{3,2,1,0:T(8,128)S(1)}, u32[]{:S(2)}, u32[]{:S(2)}) %collective-permute-start.8) | collective-permute-done | bytes 245792 | tf_op jit(solution)/shard_map/ppermute | solution.py:432
  66.1 3.7 %collective-permute-done.9.right = f32[3,5,16,256]{3,2,1,0:T(8,128)S(1)} collective-permute-done((f32[3,5,16,256]{3,2,1,0:T(8,128)S(1)}, f32[3,5,16,256]{3,2,1,0:T(8,128)S(1)}, u32[]{:S(2)}, u32[]{:S(2)}) %collective-permute-start.9) | collective-permute-done | bytes 245792 | tf_op jit(solution)/shard_map/ppermute | solution.py:432
  69.8 1.4 %shard_map.89 = (f32[4,4,256]{2,1,0:T(4,128)}, f32[20,128]{1,0:T(8,128)S(1)}) custom-call(f32[3,5,16,256]{3,2,1,0:T(8,128)S(1)} %collective-permute-done.8.left, f32[3,5,16,256]{3,2,1,0:T(8,128)S(1)} %pad_maximum_fusion.here, f32[3,5,16,256]{3,2,1,0:T(8,128)S(1)} %collective-permute-done.9.right, f32[16,128]{1,0:T(8,128)S(1)} %get-tuple-element.26.c2), custom_call_target="tpu_custom_call" | custom-call | flops 1000000 | bytes 2000000 | tf_op jit(solution)/shard_map/pallas_call | solution.py:24
  71.2 0.0 collective-permute-start.14
  71.2 1.9 %collective-permute-start.11 = (f32[20,128]{1,0:T(8,128)S(1)}, f32[20,128]{1,0:T(8,128)S(1)}, u32[]{:S(2)}, u32[]{:S(2)}) collective-permute-start(f32[20,128]{1,0:T(8,128)S(1)} %get-tuple-element.28), channel_id=1, source_target_pairs={{1,0},{2,1},{3,2},{4,3},{5,4},{6,5},{7,6},{8,7},{9,8},{10,9},{11,1... | collective-permute-start | bytes 30728 | tf_op jit(solution)/shard_map/ppermute | solution.py:427
  73.1 3.4 %collective-permute-start.10 = (f32[20,128]{1,0:T(8,128)S(1)}, f32[20,128]{1,0:T(8,128)S(1)}, u32[]{:S(2)}, u32[]{:S(2)}) collective-permute-start(f32[20,128]{1,0:T(8,128)S(1)} %get-tuple-element.28), channel_id=1, source_target_pairs={{0,1},{1,2},{2,3},{3,4},{4,5},{5,6},{6,7},{7,8},{8,9},{9,10},{10,1... | collective-permute-start | bytes 30728 | tf_op jit(solution)/shard_map/ppermute | solution.py:427
  76.5 3.5 %collective-permute-start.12 = (f32[20,128]{1,0:T(8,128)S(1)}, f32[20,128]{1,0:T(8,128)S(1)}, u32[]{:S(2)}, u32[]{:S(2)}) collective-permute-start(f32[20,128]{1,0:T(8,128)S(1)} %get-tuple-element.28), channel_id=1, source_target_pairs={{0,64},{64,128},{128,192},{192,256},{256,320},{320,384},{384,448},... | collective-permute-start | bytes 30728 | tf_op jit(solution)/shard_map/ppermute | solution.py:432
  80.0 1.9 %collective-permute-start.16 = (f32[20,128]{1,0:T(8,128)S(1)}, f32[20,128]{1,0:T(8,128)S(1)}, u32[]{:S(2)}, u32[]{:S(2)}) collective-permute-start(f32[20,128]{1,0:T(8,128)S(1)} %get-tuple-element.28), channel_id=1, source_target_pairs={{0,2},{1,3},{2,4},{3,5},{4,6},{5,7},{6,8},{7,9},{8,10},{9,11},{10,... | collective-permute-start | bytes 30728 | tf_op jit(solution)/shard_map/ppermute | solution.py:427
  81.9 0.0 collective-permute-done.14
  81.9 7.6 %collective-permute-start.17 = (f32[20,128]{1,0:T(8,128)S(1)}, f32[20,128]{1,0:T(8,128)S(1)}, u32[]{:S(2)}, u32[]{:S(2)}) collective-permute-start(f32[20,128]{1,0:T(8,128)S(1)} %get-tuple-element.28), channel_id=1, source_target_pairs={{2,0},{3,1},{4,2},{5,3},{6,4},{7,5},{8,6},{9,7},{10,8},{11,9},{12,... | collective-permute-start | bytes 30728 | tf_op jit(solution)/shard_map/ppermute | solution.py:427
  89.5 0.0 collective-permute-done.11
  89.5 0.0 collective-permute-done.10
  89.5 0.0 collective-permute-done.12
  89.6 0.6 collective-permute-start.13
  90.2 0.0 collective-permute-start.15
  90.2 0.0 collective-permute-done.16.down
  90.2 0.1 collective-permute-done.17.up
  90.3 1.0 %collective-permute-done.13.left = f32[4,20,128]{2,1,0:T(8,128)S(1)} collective-permute-done((f32[4,20,128]{2,1,0:T(8,128)S(1)}, f32[4,20,128]{2,1,0:T(8,128)S(1)}, u32[]{:S(2)}, u32[]{:S(2)}) %collective-permute-start.13) | collective-permute-done | bytes 40992 | tf_op jit(solution)/shard_map/ppermute | solution.py:432
  91.3 3.5 %collective-permute-done.15.right = f32[4,20,128]{2,1,0:T(8,128)S(1)} collective-permute-done((f32[4,20,128]{2,1,0:T(8,128)S(1)}, f32[4,20,128]{2,1,0:T(8,128)S(1)}, u32[]{:S(2)}, u32[]{:S(2)}) %collective-permute-start.15) | collective-permute-done | bytes 40992 | tf_op jit(solution)/shard_map/ppermute | solution.py:432
  94.9 0.9 shard_map.90
  (4 shorter events, 0.1 us)
Async XLA Ops:
  3.2 36.3 %copy-start = (f32[48,8,512]{2,1,0:T(8,128)S(1)}, f32[48,8,512]{2,1,0:T(8,128)}, u32[]{:S(2)}) copy-start(f32[48,8,512]{2,1,0:T(8,128)} %get-tuple-element.16.own) | copy-start | bytes 2359300
  3.2 25.0 %collective-permute-start.2 = (f32[24,8,512]{2,1,0:T(8,128)}, f32[24,8,512]{2,1,0:T(8,128)S(1)}, u32[]{:S(2)}, u32[]{:S(2)}) collective-permute-start(f32[24,8,512]{2,1,0:T(8,128)} %get-tuple-element.19), channel_id=1, source_target_pairs={{1,0},{2,1},{3,2},{4,3},{5,4},{6,5},{7,6},{8,7},{9,8},{10,9},{11,1... | collective-permute-start | bytes 1179656 | tf_op jit(solution)/shard_map/ppermute | solution.py:427
  20.2 15.1 %collective-permute-start.3 = (f32[24,8,512]{2,1,0:T(8,128)}, f32[24,8,512]{2,1,0:T(8,128)S(1)}, u32[]{:S(2)}, u32[]{:S(2)}) collective-permute-start(f32[24,8,512]{2,1,0:T(8,128)} %get-tuple-element.20), channel_id=1, source_target_pairs={{0,1},{1,2},{2,3},{3,4},{4,5},{5,6},{6,7},{7,8},{8,9},{9,10},{10,1... | collective-permute-start | bytes 1179656 | tf_op jit(solution)/shard_map/ppermute | solution.py:427
  22.1 17.4 %collective-permute-start.1 = (f32[24,8,512]{2,1,0:T(8,128)}, f32[24,8,512]{2,1,0:T(8,128)S(1)}, u32[]{:S(2)}, u32[]{:S(2)}) collective-permute-start(f32[24,8,512]{2,1,0:T(8,128)} %get-tuple-element.18), channel_id=1, source_target_pairs={{0,64},{64,128},{128,192},{192,256},{256,320},{320,384},{384,448},... | collective-permute-start | bytes 1179656 | tf_op jit(solution)/shard_map/ppermute | solution.py:432
  25.4 14.7 %collective-permute-start = (f32[24,8,512]{2,1,0:T(8,128)}, f32[24,8,512]{2,1,0:T(8,128)S(1)}, u32[]{:S(2)}, u32[]{:S(2)}) collective-permute-start(f32[24,8,512]{2,1,0:T(8,128)} %get-tuple-element.17), channel_id=1, source_target_pairs={{0,960},{64,0},{128,64},{192,128},{256,192},{320,256},{384,320},{4... | collective-permute-start | bytes 1179656 | tf_op jit(solution)/shard_map/ppermute | solution.py:432
  35.3 8.2 %collective-permute-start.4 = (f32[16,8,512]{2,1,0:T(8,128)S(1)}, f32[16,8,512]{2,1,0:T(8,128)S(1)}, u32[]{:S(2)}, u32[]{:S(2)}) collective-permute-start(f32[16,8,512]{2,1,0:T(8,128)S(1)} %get-tuple-element.21), channel_id=1, source_target_pairs={{0,960},{64,0},{128,64},{192,128},{256,192},{320,256},{384,320},{4... | collective-permute-start | bytes 786440 | tf_op jit(solution)/shard_map/ppermute | solution.py:432
  37.2 6.4 %collective-permute-start.5 = (f32[16,8,512]{2,1,0:T(8,128)S(1)}, f32[16,8,512]{2,1,0:T(8,128)S(1)}, u32[]{:S(2)}, u32[]{:S(2)}) collective-permute-start(f32[16,8,512]{2,1,0:T(8,128)S(1)} %get-tuple-element.22), channel_id=1, source_target_pairs={{0,64},{64,128},{128,192},{192,256},{256,320},{320,384},{384,448},... | collective-permute-start | bytes 786440 | tf_op jit(solution)/shard_map/ppermute | solution.py:432
  48.4 6.2 %collective-permute-start.7 = (f32[5,16,256]{2,1,0:T(8,128)S(1)}, f32[5,16,256]{2,1,0:T(8,128)S(1)}, u32[]{:S(2)}, u32[]{:S(2)}) collective-permute-start(f32[5,16,256]{2,1,0:T(8,128)S(1)} %get-tuple-element.25), channel_id=1, source_target_pairs={{1,0},{2,1},{3,2},{4,3},{5,4},{6,5},{7,6},{8,7},{9,8},{10,9},{11,1... | collective-permute-start | bytes 245768 | tf_op jit(solution)/shard_map/ppermute | solution.py:427
  50.3 9.5 %collective-permute-start.6 = (f32[5,16,256]{2,1,0:T(8,128)S(1)}, f32[5,16,256]{2,1,0:T(8,128)S(1)}, u32[]{:S(2)}, u32[]{:S(2)}) collective-permute-start(f32[5,16,256]{2,1,0:T(8,128)S(1)} %get-tuple-element.25), channel_id=1, source_target_pairs={{0,1},{1,2},{2,3},{3,4},{4,5},{5,6},{6,7},{7,8},{8,9},{9,10},{10,1... | collective-permute-start | bytes 245768 | tf_op jit(solution)/shard_map/ppermute | solution.py:427
  59.8 6.3 %collective-permute-start.8 = (f32[3,5,16,256]{3,2,1,0:T(8,128)S(1)}, f32[3,5,16,256]{3,2,1,0:T(8,128)S(1)}, u32[]{:S(2)}, u32[]{:S(2)}) collective-permute-start(f32[3,5,16,256]{3,2,1,0:T(8,128)S(1)} %pad_maximum_fusion.here), channel_id=1, source_target_pairs={{0,64},{64,128},{128,192},{192,256},{256,320},{320,384},{384,448},... | collective-permute-start | bytes 737288 | tf_op jit(solution)/shard_map/ppermute | solution.py:432
  62.9 6.8 %collective-permute-start.9 = (f32[3,5,16,256]{3,2,1,0:T(8,128)S(1)}, f32[3,5,16,256]{3,2,1,0:T(8,128)S(1)}, u32[]{:S(2)}, u32[]{:S(2)}) collective-permute-start(f32[3,5,16,256]{3,2,1,0:T(8,128)S(1)} %pad_maximum_fusion.here), channel_id=1, source_target_pairs={{0,960},{64,0},{128,64},{192,128},{256,192},{320,256},{384,320},{4... | collective-permute-start | bytes 737288 | tf_op jit(solution)/shard_map/ppermute | solution.py:432
  71.2 10.7 %collective-permute-start.14 = (f32[20,128]{1,0:T(8,128)S(1)}, f32[20,128]{1,0:T(8,128)S(1)}, u32[]{:S(2)}, u32[]{:S(2)}) collective-permute-start(f32[20,128]{1,0:T(8,128)S(1)} %get-tuple-element.28), channel_id=1, source_target_pairs={{0,960},{64,0},{128,64},{192,128},{256,192},{320,256},{384,320},{4... | collective-permute-start | bytes 30728 | tf_op jit(solution)/shard_map/ppermute | solution.py:432
  71.2 18.3 %collective-permute-start.11 = (f32[20,128]{1,0:T(8,128)S(1)}, f32[20,128]{1,0:T(8,128)S(1)}, u32[]{:S(2)}, u32[]{:S(2)}) collective-permute-start(f32[20,128]{1,0:T(8,128)S(1)} %get-tuple-element.28), channel_id=1, source_target_pairs={{1,0},{2,1},{3,2},{4,3},{5,4},{6,5},{7,6},{8,7},{9,8},{10,9},{11,1... | collective-permute-start | bytes 30728 | tf_op jit(solution)/shard_map/ppermute | solution.py:427
  73.1 16.4 %collective-permute-start.10 = (f32[20,128]{1,0:T(8,128)S(1)}, f32[20,128]{1,0:T(8,128)S(1)}, u32[]{:S(2)}, u32[]{:S(2)}) collective-permute-start(f32[20,128]{1,0:T(8,128)S(1)} %get-tuple-element.28), channel_id=1, source_target_pairs={{0,1},{1,2},{2,3},{3,4},{4,5},{5,6},{6,7},{7,8},{8,9},{9,10},{10,1... | collective-permute-start | bytes 30728 | tf_op jit(solution)/shard_map/ppermute | solution.py:427
  76.5 13.1 %collective-permute-start.12 = (f32[20,128]{1,0:T(8,128)S(1)}, f32[20,128]{1,0:T(8,128)S(1)}, u32[]{:S(2)}, u32[]{:S(2)}) collective-permute-start(f32[20,128]{1,0:T(8,128)S(1)} %get-tuple-element.28), channel_id=1, source_target_pairs={{0,64},{64,128},{128,192},{192,256},{256,320},{320,384},{384,448},... | collective-permute-start | bytes 30728 | tf_op jit(solution)/shard_map/ppermute | solution.py:432
  80.0 10.2 %collective-permute-start.16 = (f32[20,128]{1,0:T(8,128)S(1)}, f32[20,128]{1,0:T(8,128)S(1)}, u32[]{:S(2)}, u32[]{:S(2)}) collective-permute-start(f32[20,128]{1,0:T(8,128)S(1)} %get-tuple-element.28), channel_id=1, source_target_pairs={{0,2},{1,3},{2,4},{3,5},{4,6},{5,7},{6,8},{7,9},{8,10},{9,11},{10,... | collective-permute-start | bytes 30728 | tf_op jit(solution)/shard_map/ppermute | solution.py:427
  81.9 8.4 %collective-permute-start.17 = (f32[20,128]{1,0:T(8,128)S(1)}, f32[20,128]{1,0:T(8,128)S(1)}, u32[]{:S(2)}, u32[]{:S(2)}) collective-permute-start(f32[20,128]{1,0:T(8,128)S(1)} %get-tuple-element.28), channel_id=1, source_target_pairs={{2,0},{3,1},{4,2},{5,3},{6,4},{7,5},{8,6},{9,7},{10,8},{11,9},{12,... | collective-permute-start | bytes 30728 | tf_op jit(solution)/shard_map/ppermute | solution.py:427
  89.6 1.8 %collective-permute-start.13 = (f32[4,20,128]{2,1,0:T(8,128)S(1)}, f32[4,20,128]{2,1,0:T(8,128)S(1)}, u32[]{:S(2)}, u32[]{:S(2)}) collective-permute-start(f32[4,20,128]{2,1,0:T(8,128)S(1)} %get-tuple-element.30), channel_id=1, source_target_pairs={{0,64},{64,128},{128,192},{192,256},{256,320},{320,384},{384,448},... | collective-permute-start | bytes 122888 | tf_op jit(solution)/shard_map/ppermute | solution.py:432
  90.2 4.7 %collective-permute-start.15 = (f32[4,20,128]{2,1,0:T(8,128)S(1)}, f32[4,20,128]{2,1,0:T(8,128)S(1)}, u32[]{:S(2)}, u32[]{:S(2)}) collective-permute-start(f32[4,20,128]{2,1,0:T(8,128)S(1)} %get-tuple-element.29), channel_id=1, source_target_pairs={{0,960},{64,0},{128,64},{192,128},{256,192},{320,256},{384,320},{4... | collective-permute-start | bytes 122888 | tf_op jit(solution)/shard_map/ppermute | solution.py:432

commit v4 on v3

--- a/solution.py
+++ b/solution.py
@@ -284,22 +284,18 @@
     return ((weights[0, w] + x) + (y + z)), here
 
 
-def smooth(weights, held, unroll):
+def coloured(shape):
+    parity = (iota(shape, 0) + iota(shape, 1)) % 2
+    return [parity == 0, parity == 1]
+
+
+def smooth(weights, held, first):
     count = weights.shape[1]
-    spare = (weights.shape[2], weights.shape[3])
-    parity = (iota(spare, 0) + iota(spare, 1)) % 2
-    for step in range(4):
-
-        def one(w, carry, step=step):
+    colours = coloured((weights.shape[2], weights.shape[3]))
+    for step in range(first, 4):
+        for w in range(step, count - step):
             new, here = relaxed(weights, held, w)
-            held[w + 1] = jnp.where((parity + w + step) % 2 == 0, new, here)
-            return carry
-
-        if unroll:
-            for w in range(step, count - step):
-                one(w, 0)
-        else:
-            lax.fori_loop(step, count - step, one, 0, unroll=2)
+            held[w + 1] = jnp.where(colours[(w + step) % 2], new, here)
 
 
 def fine_body(count, own, xlr, xhr, ylr, yhr, xclr, xchr, c1, out, p1, win, weights, held, diag, rows):
@@ -327,7 +323,7 @@
     held[17] = zero
     win[BX - 1, 0] = zero
 
-    def prepare(w, carry):
+    for w in range(16):
         av, bxv, byv, bzv = win[A - 1, w + 1], win[BX - 1, w + 1], win[BY - 1, w + 1], win[BZ - 1, w + 1]
         low_x = win[BX - 1, w]
         total = av + ((bxv + low_x) + (byv + pltpu.roll(byv, 1, 0)) + (bzv + below_z(bzv)))
@@ -335,10 +331,7 @@
         inverse = jnp.where(inside, 1.0 / jnp.where(inside, total, 1.0), 0.0)
         set_weights(weights, w, inverse, win[F - 1, w + 1], bxv, low_x, byv, bzv)
         diag[w] = total[0:8]
-        return carry
-
-    lax.fori_loop(0, 16, prepare, 0, unroll=2)
-    smooth(weights, held, False)
+    smooth(weights, held, 0)
     for i in range(4):
         total = None
         for j in range(2):
@@ -360,6 +353,7 @@
     lower, upper = beside(count)[:2]
     zero = jnp.zeros((16, nz), F32)
     win[2, 0] = zero
+    colours = coloured((16, nz))
     for b, (source, there) in enumerate(((left, lower), (here, None), (right, upper))):
         for k in range(5):
             for half in range(2):
@@ -377,10 +371,10 @@
         inside = total > 0.0
         inverse = jnp.where(inside, 0.25 / jnp.where(inside, total, 1.0), 0.0)
         set_weights(weights, w, inverse, 4.0 * win[0, w + 1], win[2, w + 1], win[2, w], win[3, w + 1], win[4, w + 1])
-        held[w + 1] = zero
+        held[w + 1] = jnp.where(colours[w % 2], weights[0, w], 0.0)
     held[0] = zero
     held[13] = zero
-    smooth(weights, held, True)
+    smooth(weights, held, 1)
     for i in range(2):
         total = None
         for j in range(2):
@@ -411,13 +405,16 @@
             for b, (source, there) in enumerate(((left, factor[0]), (mid, 1.0), (right, factor[1]))):
                 for j in range(3):
                     win[k, 2 + 2 * b + i, 1 + 2 * j : 3 + 2 * j] = source[j, at : at + 2] * there
-    held[...] = jnp.zeros(held.shape, F32)
+    held[0] = jnp.zeros(held.shape[1:], F32)
+    held[9] = jnp.zeros(held.shape[1:], F32)
+    colours = coloured(held.shape[1:])
     for w in range(8):
         total = win[1, w + 1]
         inside = total > 0.0
         inverse = jnp.where(inside, 0.0625 / jnp.where(inside, total, 1.0), 0.0)
         set_weights(weights, w, inverse, 16.0 * win[0, w + 1], win[2, w + 1], win[2, w], win[3, w + 1], win[4, w + 1])
-    smooth(weights, held, True)
+        held[w + 1] = jnp.where(colours[w % 2], weights[0, w], 0.0)
+    smooth(weights, held, 1)
     for i in range(2):
         out[i] = held[4 + i, 3:5]
 
@@ -444,10 +441,9 @@
     own, xl, xh, yl, yh = call(
         pack_body,
         (shape(48, 8, nz),) + (sent,) * 4,
-        args,
+        tuple(pltpu.with_memory_space_constraint(x, pltpu.HBM) for x in args),
         [pltpu.VMEM(x.shape, x.dtype) for x in args] + [pltpu.SemaphoreType.DMA((6,))],
         space=pltpu.HBM,
-        grant=56 << 10,
     )
     ylr, yhr = along_y(yl, -1), along_y(yh, 1)
     xlr, xhr = round_x(xl, -1), round_x(xh, 1)

time: 96.2 us -> 91.6 us (0.952)
  Pallas kernels: 10.3 us -> 6.06 us
    pallas_call x6, Pallas kernels: 10.3 us -> 6.06 us  [call(): pl.pallas_call(body, out_shape=outs, in_specs=[pl.BlockSpec(memory_space=...]
where the time goes in v4:
time: 91.6 us; the launch traced here: 91.2 us
  starting transfers between devices  53.5 us (58%)
  waiting for transfers between devices  30.8 us (34%)
  Pallas kernels  6.06 us (7%)
    ppermute x8, starting transfers between devices, along_y(): lax.ppermute(block, 'gy', [(i, i + by) for i in range(count) if 0 <= i +...  38.8 us
    ppermute x8, waiting for transfers between devices, along_y(): lax.ppermute(block, 'gy', [(i, i + by) for i in range(count) if 0 <= i +...  16 us
    ppermute x10, waiting for transfers between devices, round_x(): lax.ppermute(block, 'gx', [(i, (i + by) % count) for i in range(count)])  14.9 us
    ppermute x10, starting transfers between devices, round_x(): lax.ppermute(block, 'gx', [(i, (i + by) % count) for i in range(count)])  14.7 us
    pallas_call x6, Pallas kernels, call(): pl.pallas_call(body, out_shape=outs, in_specs=[pl.BlockSpec(memory_space=...  6.06 us
  transfers between devices with their start and end apart: 18, of which 10 were waited for; matrix products, arithmetic and copies ran while one was open for 0% of the time, Pallas kernels for 1%

profile of v4, /device:TPU:71, one launch (start us, length us, event | category | flops | bytes accessed | tf_op | source)
XLA Modules:
  0.0 91.2 jit_solution(9574043429040030473)
XLA Ops:
  0.6 1.3 %shard_map.85 = (f32[48,8,512]{2,1,0:T(8,128)S(1)}, f32[24,8,512]{2,1,0:T(8,128)S(1)}, f32[24,8,512]{2,1,0:T(8,128)S(1)}, f32[24,8,512]{2,1,0:T(8,128)S(1)}, f32[24,8,512]{2,1,0:T(8,128)S(1)}) custom-call(f32[8,8,512]{2,1,0:T(8,128)} %u.1, f32[8,8,512]{2,1,0:T(8,128)} %f.1, bf16[8,8,512]{2,1,0:T(8,128)(2,1)} %a.1, bf16[8,8,512]{2,1,0:T(8,128)(2,1)} %bx.1, ...), custom_call_target="tpu_custom_call" | custom-call | flops 1000000 | bytes 2000000 | tf_op jit(solution)/shard_map/pallas_call | solution.py:24
  2.0 16.8 %collective-permute-start.2 = (f32[24,8,512]{2,1,0:T(8,128)S(1)}, f32[24,8,512]{2,1,0:T(8,128)S(1)}, u32[]{:S(2)}, u32[]{:S(2)}) collective-permute-start(f32[24,8,512]{2,1,0:T(8,128)S(1)} %get-tuple-element.19), channel_id=1, source_target_pairs={{1,0},{2,1},{3,2},{4,3},{5,4},{6,5},{7,6},{8,7},{9,8},{10,9},{11,1... | collective-permute-start | bytes 1179656 | tf_op jit(solution)/shard_map/ppermute | solution.py:424
  18.8 1.9 %collective-permute-start.3 = (f32[24,8,512]{2,1,0:T(8,128)S(1)}, f32[24,8,512]{2,1,0:T(8,128)S(1)}, u32[]{:S(2)}, u32[]{:S(2)}) collective-permute-start(f32[24,8,512]{2,1,0:T(8,128)S(1)} %get-tuple-element.20), channel_id=1, source_target_pairs={{0,1},{1,2},{2,3},{3,4},{4,5},{5,6},{6,7},{7,8},{8,9},{9,10},{10,1... | collective-permute-start | bytes 1179656 | tf_op jit(solution)/shard_map/ppermute | solution.py:424
  20.7 3.3 %collective-permute-start.1 = (f32[24,8,512]{2,1,0:T(8,128)S(1)}, f32[24,8,512]{2,1,0:T(8,128)S(1)}, u32[]{:S(2)}, u32[]{:S(2)}) collective-permute-start(f32[24,8,512]{2,1,0:T(8,128)S(1)} %get-tuple-element.18), channel_id=1, source_target_pairs={{0,64},{64,128},{128,192},{192,256},{256,320},{320,384},{384,448},... | collective-permute-start | bytes 1179656 | tf_op jit(solution)/shard_map/ppermute | solution.py:429
  24.0 0.0 collective-permute-start
  24.0 2.6 %collective-permute-done.2.ylr = f32[24,8,512]{2,1,0:T(8,128)S(1)} collective-permute-done((f32[24,8,512]{2,1,0:T(8,128)S(1)}, f32[24,8,512]{2,1,0:T(8,128)S(1)}, u32[]{:S(2)}, u32[]{:S(2)}) %collective-permute-start.2) | collective-permute-done | bytes 393248 | tf_op jit(solution)/shard_map/ppermute | solution.py:424
  26.5 7.1 %collective-permute-done.3.yhr = f32[24,8,512]{2,1,0:T(8,128)S(1)} collective-permute-done((f32[24,8,512]{2,1,0:T(8,128)S(1)}, f32[24,8,512]{2,1,0:T(8,128)S(1)}, u32[]{:S(2)}, u32[]{:S(2)}) %collective-permute-start.3) | collective-permute-done | bytes 393248 | tf_op jit(solution)/shard_map/ppermute | solution.py:424
  33.7 1.9 %collective-permute-start.4 = (f32[16,8,512]{2,1,0:T(8,128)S(1)}, f32[16,8,512]{2,1,0:T(8,128)S(1)}, u32[]{:S(2)}, u32[]{:S(2)}) collective-permute-start(f32[16,8,512]{2,1,0:T(8,128)S(1)} %get-tuple-element.21), channel_id=1, source_target_pairs={{0,960},{64,0},{128,64},{192,128},{256,192},{320,256},{384,320},{4... | collective-permute-start | bytes 786440 | tf_op jit(solution)/shard_map/ppermute | solution.py:429
  35.6 2.3 %collective-permute-start.5 = (f32[16,8,512]{2,1,0:T(8,128)S(1)}, f32[16,8,512]{2,1,0:T(8,128)S(1)}, u32[]{:S(2)}, u32[]{:S(2)}) collective-permute-start(f32[16,8,512]{2,1,0:T(8,128)S(1)} %get-tuple-element.22), channel_id=1, source_target_pairs={{0,64},{64,128},{128,192},{192,256},{256,320},{320,384},{384,448},... | collective-permute-start | bytes 786440 | tf_op jit(solution)/shard_map/ppermute | solution.py:429
  37.9 0.0 collective-permute-done.1.xhr
  37.9 0.5 shard_map.87
  38.5 0.0 collective-permute-done.xlr
  38.5 3.5 %collective-permute-done.4.xclr = f32[16,8,512]{2,1,0:T(8,128)S(1)} collective-permute-done((f32[16,8,512]{2,1,0:T(8,128)S(1)}, f32[16,8,512]{2,1,0:T(8,128)S(1)}, u32[]{:S(2)}, u32[]{:S(2)}) %collective-permute-start.4) | collective-permute-done | bytes 262176 | tf_op jit(solution)/shard_map/ppermute | solution.py:429
  41.9 0.0 collective-permute-done.5.xchr
  41.9 2.2 %shard_map.88 = (f32[8,8,512]{2,1,0:T(8,128)}, f32[5,16,256]{2,1,0:T(8,128)S(1)}) custom-call(f32[48,8,512]{2,1,0:T(8,128)S(1)} %get-tuple-element.16.own, f32[24,8,512]{2,1,0:T(8,128)S(1)} %collective-permute-done.xlr, f32[24,8,512]{2,1,0:T(8,128)S(1)} %collective-permute-done.1.xhr, f32[24,8,512]{2,1,0:T(8,128)S(1)} %collective-permute-done.2.ylr, ...), custom_call_target="tpu_custom_call" | custom-call | flops 20000000 | bytes 20000000 | tf_op jit(solution)/shard_map/pallas_call | solution.py:24
  44.2 1.9 %collective-permute-start.7 = (f32[5,16,256]{2,1,0:T(8,128)S(1)}, f32[5,16,256]{2,1,0:T(8,128)S(1)}, u32[]{:S(2)}, u32[]{:S(2)}) collective-permute-start(f32[5,16,256]{2,1,0:T(8,128)S(1)} %get-tuple-element.25), channel_id=1, source_target_pairs={{1,0},{2,1},{3,2},{4,3},{5,4},{6,5},{7,6},{8,7},{9,8},{10,9},{11,1... | collective-permute-start | bytes 245768 | tf_op jit(solution)/shard_map/ppermute | solution.py:424
  46.1 3.4 %collective-permute-start.6 = (f32[5,16,256]{2,1,0:T(8,128)S(1)}, f32[5,16,256]{2,1,0:T(8,128)S(1)}, u32[]{:S(2)}, u32[]{:S(2)}) collective-permute-start(f32[5,16,256]{2,1,0:T(8,128)S(1)} %get-tuple-element.25), channel_id=1, source_target_pairs={{0,1},{1,2},{2,3},{3,4},{4,5},{5,6},{6,7},{7,8},{8,9},{9,10},{10,1... | collective-permute-start | bytes 245768 | tf_op jit(solution)/shard_map/ppermute | solution.py:424
  49.5 0.9 collective-permute-done.7
  50.3 5.2 %collective-permute-done.6 = f32[5,16,256]{2,1,0:T(8,128)S(1)} collective-permute-done((f32[5,16,256]{2,1,0:T(8,128)S(1)}, f32[5,16,256]{2,1,0:T(8,128)S(1)}, u32[]{:S(2)}, u32[]{:S(2)}) %collective-permute-start.6) | collective-permute-done | bytes 81952 | tf_op jit(solution)/shard_map/ppermute | solution.py:424
  55.6 3.1 %collective-permute-start.8 = (f32[3,5,16,256]{3,2,1,0:T(8,128)S(1)}, f32[3,5,16,256]{3,2,1,0:T(8,128)S(1)}, u32[]{:S(2)}, u32[]{:S(2)}) collective-permute-start(f32[3,5,16,256]{3,2,1,0:T(8,128)S(1)} %pad_maximum_fusion.here), channel_id=1, source_target_pairs={{0,64},{64,128},{128,192},{192,256},{256,320},{320,384},{384,448},... | collective-permute-start | bytes 737288 | tf_op jit(solution)/shard_map/ppermute | solution.py:429
  58.7 0.0 collective-permute-start.9
  58.7 3.1 %collective-permute-done.8.left = f32[3,5,16,256]{3,2,1,0:T(8,128)S(1)} collective-permute-done((f32[3,5,16,256]{3,2,1,0:T(8,128)S(1)}, f32[3,5,16,256]{3,2,1,0:T(8,128)S(1)}, u32[]{:S(2)}, u32[]{:S(2)}) %collective-permute-start.8) | collective-permute-done | bytes 245792 | tf_op jit(solution)/shard_map/ppermute | solution.py:429
  61.9 3.7 %collective-permute-done.9.right = f32[3,5,16,256]{3,2,1,0:T(8,128)S(1)} collective-permute-done((f32[3,5,16,256]{3,2,1,0:T(8,128)S(1)}, f32[3,5,16,256]{3,2,1,0:T(8,128)S(1)}, u32[]{:S(2)}, u32[]{:S(2)}) %collective-permute-start.9) | collective-permute-done | bytes 245792 | tf_op jit(solution)/shard_map/ppermute | solution.py:429
  65.6 1.1 %shard_map.89 = (f32[4,4,256]{2,1,0:T(4,128)}, f32[20,128]{1,0:T(8,128)S(1)}) custom-call(f32[3,5,16,256]{3,2,1,0:T(8,128)S(1)} %collective-permute-done.8.left, f32[3,5,16,256]{3,2,1,0:T(8,128)S(1)} %pad_maximum_fusion.here, f32[3,5,16,256]{3,2,1,0:T(8,128)S(1)} %collective-permute-done.9.right, f32[16,128]{1,0:T(8,128)S(1)} %get-tuple-element.26.c2), custom_call_target="tpu_custom_call" | custom-call | flops 1000000 | bytes 2000000 | tf_op jit(solution)/shard_map/pallas_call | solution.py:24
  66.6 0.0 collective-permute-start.14
  66.6 1.9 %collective-permute-start.11 = (f32[20,128]{1,0:T(8,128)S(1)}, f32[20,128]{1,0:T(8,128)S(1)}, u32[]{:S(2)}, u32[]{:S(2)}) collective-permute-start(f32[20,128]{1,0:T(8,128)S(1)} %get-tuple-element.28), channel_id=1, source_target_pairs={{1,0},{2,1},{3,2},{4,3},{5,4},{6,5},{7,6},{8,7},{9,8},{10,9},{11,1... | collective-permute-start | bytes 30728 | tf_op jit(solution)/shard_map/ppermute | solution.py:424
  68.6 3.4 %collective-permute-start.10 = (f32[20,128]{1,0:T(8,128)S(1)}, f32[20,128]{1,0:T(8,128)S(1)}, u32[]{:S(2)}, u32[]{:S(2)}) collective-permute-start(f32[20,128]{1,0:T(8,128)S(1)} %get-tuple-element.28), channel_id=1, source_target_pairs={{0,1},{1,2},{2,3},{3,4},{4,5},{5,6},{6,7},{7,8},{8,9},{9,10},{10,1... | collective-permute-start | bytes 30728 | tf_op jit(solution)/shard_map/ppermute | solution.py:424
  71.9 3.5 %collective-permute-start.12 = (f32[20,128]{1,0:T(8,128)S(1)}, f32[20,128]{1,0:T(8,128)S(1)}, u32[]{:S(2)}, u32[]{:S(2)}) collective-permute-start(f32[20,128]{1,0:T(8,128)S(1)} %get-tuple-element.28), channel_id=1, source_target_pairs={{0,64},{64,128},{128,192},{192,256},{256,320},{320,384},{384,448},... | collective-permute-start | bytes 30728 | tf_op jit(solution)/shard_map/ppermute | solution.py:429
  75.5 1.9 %collective-permute-start.16 = (f32[20,128]{1,0:T(8,128)S(1)}, f32[20,128]{1,0:T(8,128)S(1)}, u32[]{:S(2)}, u32[]{:S(2)}) collective-permute-start(f32[20,128]{1,0:T(8,128)S(1)} %get-tuple-element.28), channel_id=1, source_target_pairs={{0,2},{1,3},{2,4},{3,5},{4,6},{5,7},{6,8},{7,9},{8,10},{9,11},{10,... | collective-permute-start | bytes 30728 | tf_op jit(solution)/shard_map/ppermute | solution.py:424
  77.4 0.0 collective-permute-done.14
  77.4 7.6 %collective-permute-start.17 = (f32[20,128]{1,0:T(8,128)S(1)}, f32[20,128]{1,0:T(8,128)S(1)}, u32[]{:S(2)}, u32[]{:S(2)}) collective-permute-start(f32[20,128]{1,0:T(8,128)S(1)} %get-tuple-element.28), channel_id=1, source_target_pairs={{2,0},{3,1},{4,2},{5,3},{6,4},{7,5},{8,6},{9,7},{10,8},{11,9},{12,... | collective-permute-start | bytes 30728 | tf_op jit(solution)/shard_map/ppermute | solution.py:424
  85.0 0.0 collective-permute-done.11
  85.0 0.0 collective-permute-done.10
  85.0 0.0 collective-permute-done.12
  85.0 0.6 collective-permute-start.13
  85.6 0.0 collective-permute-start.15
  85.6 0.0 collective-permute-done.16.down
  85.6 0.1 collective-permute-done.17.up
  85.8 1.0 %collective-permute-done.13.left = f32[4,20,128]{2,1,0:T(8,128)S(1)} collective-permute-done((f32[4,20,128]{2,1,0:T(8,128)S(1)}, f32[4,20,128]{2,1,0:T(8,128)S(1)}, u32[]{:S(2)}, u32[]{:S(2)}) %collective-permute-start.13) | collective-permute-done | bytes 40992 | tf_op jit(solution)/shard_map/ppermute | solution.py:429
  86.8 3.5 %collective-permute-done.15.right = f32[4,20,128]{2,1,0:T(8,128)S(1)} collective-permute-done((f32[4,20,128]{2,1,0:T(8,128)S(1)}, f32[4,20,128]{2,1,0:T(8,128)S(1)}, u32[]{:S(2)}, u32[]{:S(2)}) %collective-permute-start.15) | collective-permute-done | bytes 40992 | tf_op jit(solution)/shard_map/ppermute | solution.py:429
  90.3 0.9 shard_map.90
  (4 shorter events, 0.1 us)
Async XLA Ops:
  2.0 24.6 %collective-permute-start.2 = (f32[24,8,512]{2,1,0:T(8,128)S(1)}, f32[24,8,512]{2,1,0:T(8,128)S(1)}, u32[]{:S(2)}, u32[]{:S(2)}) collective-permute-start(f32[24,8,512]{2,1,0:T(8,128)S(1)} %get-tuple-element.19), channel_id=1, source_target_pairs={{1,0},{2,1},{3,2},{4,3},{5,4},{6,5},{7,6},{8,7},{9,8},{10,9},{11,1... | collective-permute-start | bytes 1179656 | tf_op jit(solution)/shard_map/ppermute | solution.py:424
  18.8 14.9 %collective-permute-start.3 = (f32[24,8,512]{2,1,0:T(8,128)S(1)}, f32[24,8,512]{2,1,0:T(8,128)S(1)}, u32[]{:S(2)}, u32[]{:S(2)}) collective-permute-start(f32[24,8,512]{2,1,0:T(8,128)S(1)} %get-tuple-element.20), channel_id=1, source_target_pairs={{0,1},{1,2},{2,3},{3,4},{4,5},{5,6},{6,7},{7,8},{8,9},{9,10},{10,1... | collective-permute-start | bytes 1179656 | tf_op jit(solution)/shard_map/ppermute | solution.py:424
  20.7 17.2 %collective-permute-start.1 = (f32[24,8,512]{2,1,0:T(8,128)S(1)}, f32[24,8,512]{2,1,0:T(8,128)S(1)}, u32[]{:S(2)}, u32[]{:S(2)}) collective-permute-start(f32[24,8,512]{2,1,0:T(8,128)S(1)} %get-tuple-element.18), channel_id=1, source_target_pairs={{0,64},{64,128},{128,192},{192,256},{256,320},{320,384},{384,448},... | collective-permute-start | bytes 1179656 | tf_op jit(solution)/shard_map/ppermute | solution.py:429
  24.0 14.5 %collective-permute-start = (f32[24,8,512]{2,1,0:T(8,128)S(1)}, f32[24,8,512]{2,1,0:T(8,128)S(1)}, u32[]{:S(2)}, u32[]{:S(2)}) collective-permute-start(f32[24,8,512]{2,1,0:T(8,128)S(1)} %get-tuple-element.17), channel_id=1, source_target_pairs={{0,960},{64,0},{128,64},{192,128},{256,192},{320,256},{384,320},{4... | collective-permute-start | bytes 1179656 | tf_op jit(solution)/shard_map/ppermute | solution.py:429
  33.7 8.2 %collective-permute-start.4 = (f32[16,8,512]{2,1,0:T(8,128)S(1)}, f32[16,8,512]{2,1,0:T(8,128)S(1)}, u32[]{:S(2)}, u32[]{:S(2)}) collective-permute-start(f32[16,8,512]{2,1,0:T(8,128)S(1)} %get-tuple-element.21), channel_id=1, source_target_pairs={{0,960},{64,0},{128,64},{192,128},{256,192},{320,256},{384,320},{4... | collective-permute-start | bytes 786440 | tf_op jit(solution)/shard_map/ppermute | solution.py:429
  35.6 6.4 %collective-permute-start.5 = (f32[16,8,512]{2,1,0:T(8,128)S(1)}, f32[16,8,512]{2,1,0:T(8,128)S(1)}, u32[]{:S(2)}, u32[]{:S(2)}) collective-permute-start(f32[16,8,512]{2,1,0:T(8,128)S(1)} %get-tuple-element.22), channel_id=1, source_target_pairs={{0,64},{64,128},{128,192},{192,256},{256,320},{320,384},{384,448},... | collective-permute-start | bytes 786440 | tf_op jit(solution)/shard_map/ppermute | solution.py:429
  44.2 6.2 %collective-permute-start.7 = (f32[5,16,256]{2,1,0:T(8,128)S(1)}, f32[5,16,256]{2,1,0:T(8,128)S(1)}, u32[]{:S(2)}, u32[]{:S(2)}) collective-permute-start(f32[5,16,256]{2,1,0:T(8,128)S(1)} %get-tuple-element.25), channel_id=1, source_target_pairs={{1,0},{2,1},{3,2},{4,3},{5,4},{6,5},{7,6},{8,7},{9,8},{10,9},{11,1... | collective-permute-start | bytes 245768 | tf_op jit(solution)/shard_map/ppermute | solution.py:424
  46.1 9.5 %collective-permute-start.6 = (f32[5,16,256]{2,1,0:T(8,128)S(1)}, f32[5,16,256]{2,1,0:T(8,128)S(1)}, u32[]{:S(2)}, u32[]{:S(2)}) collective-permute-start(f32[5,16,256]{2,1,0:T(8,128)S(1)} %get-tuple-element.25), channel_id=1, source_target_pairs={{0,1},{1,2},{2,3},{3,4},{4,5},{5,6},{6,7},{7,8},{8,9},{9,10},{10,1... | collective-permute-start | bytes 245768 | tf_op jit(solution)/shard_map/ppermute | solution.py:424
  55.6 6.3 %collective-permute-start.8 = (f32[3,5,16,256]{3,2,1,0:T(8,128)S(1)}, f32[3,5,16,256]{3,2,1,0:T(8,128)S(1)}, u32[]{:S(2)}, u32[]{:S(2)}) collective-permute-start(f32[3,5,16,256]{3,2,1,0:T(8,128)S(1)} %pad_maximum_fusion.here), channel_id=1, source_target_pairs={{0,64},{64,128},{128,192},{192,256},{256,320},{320,384},{384,448},... | collective-permute-start | bytes 737288 | tf_op jit(solution)/shard_map/ppermute | solution.py:429
  58.7 6.8 %collective-permute-start.9 = (f32[3,5,16,256]{3,2,1,0:T(8,128)S(1)}, f32[3,5,16,256]{3,2,1,0:T(8,128)S(1)}, u32[]{:S(2)}, u32[]{:S(2)}) collective-permute-start(f32[3,5,16,256]{3,2,1,0:T(8,128)S(1)} %pad_maximum_fusion.here), channel_id=1, source_target_pairs={{0,960},{64,0},{128,64},{192,128},{256,192},{320,256},{384,320},{4... | collective-permute-start | bytes 737288 | tf_op jit(solution)/shard_map/ppermute | solution.py:429
  66.6 10.7 %collective-permute-start.14 = (f32[20,128]{1,0:T(8,128)S(1)}, f32[20,128]{1,0:T(8,128)S(1)}, u32[]{:S(2)}, u32[]{:S(2)}) collective-permute-start(f32[20,128]{1,0:T(8,128)S(1)} %get-tuple-element.28), channel_id=1, source_target_pairs={{0,960},{64,0},{128,64},{192,128},{256,192},{320,256},{384,320},{4... | collective-permute-start | bytes 30728 | tf_op jit(solution)/shard_map/ppermute | solution.py:429
  66.6 18.3 %collective-permute-start.11 = (f32[20,128]{1,0:T(8,128)S(1)}, f32[20,128]{1,0:T(8,128)S(1)}, u32[]{:S(2)}, u32[]{:S(2)}) collective-permute-start(f32[20,128]{1,0:T(8,128)S(1)} %get-tuple-element.28), channel_id=1, source_target_pairs={{1,0},{2,1},{3,2},{4,3},{5,4},{6,5},{7,6},{8,7},{9,8},{10,9},{11,1... | collective-permute-start | bytes 30728 | tf_op jit(solution)/shard_map/ppermute | solution.py:424
  68.6 16.4 %collective-permute-start.10 = (f32[20,128]{1,0:T(8,128)S(1)}, f32[20,128]{1,0:T(8,128)S(1)}, u32[]{:S(2)}, u32[]{:S(2)}) collective-permute-start(f32[20,128]{1,0:T(8,128)S(1)} %get-tuple-element.28), channel_id=1, source_target_pairs={{0,1},{1,2},{2,3},{3,4},{4,5},{5,6},{6,7},{7,8},{8,9},{9,10},{10,1... | collective-permute-start | bytes 30728 | tf_op jit(solution)/shard_map/ppermute | solution.py:424
  71.9 13.1 %collective-permute-start.12 = (f32[20,128]{1,0:T(8,128)S(1)}, f32[20,128]{1,0:T(8,128)S(1)}, u32[]{:S(2)}, u32[]{:S(2)}) collective-permute-start(f32[20,128]{1,0:T(8,128)S(1)} %get-tuple-element.28), channel_id=1, source_target_pairs={{0,64},{64,128},{128,192},{192,256},{256,320},{320,384},{384,448},... | collective-permute-start | bytes 30728 | tf_op jit(solution)/shard_map/ppermute | solution.py:429
  75.5 10.2 %collective-permute-start.16 = (f32[20,128]{1,0:T(8,128)S(1)}, f32[20,128]{1,0:T(8,128)S(1)}, u32[]{:S(2)}, u32[]{:S(2)}) collective-permute-start(f32[20,128]{1,0:T(8,128)S(1)} %get-tuple-element.28), channel_id=1, source_target_pairs={{0,2},{1,3},{2,4},{3,5},{4,6},{5,7},{6,8},{7,9},{8,10},{9,11},{10,... | collective-permute-start | bytes 30728 | tf_op jit(solution)/shard_map/ppermute | solution.py:424
  77.4 8.4 %collective-permute-start.17 = (f32[20,128]{1,0:T(8,128)S(1)}, f32[20,128]{1,0:T(8,128)S(1)}, u32[]{:S(2)}, u32[]{:S(2)}) collective-permute-start(f32[20,128]{1,0:T(8,128)S(1)} %get-tuple-element.28), channel_id=1, source_target_pairs={{2,0},{3,1},{4,2},{5,3},{6,4},{7,5},{8,6},{9,7},{10,8},{11,9},{12,... | collective-permute-start | bytes 30728 | tf_op jit(solution)/shard_map/ppermute | solution.py:424
  85.0 1.8 %collective-permute-start.13 = (f32[4,20,128]{2,1,0:T(8,128)S(1)}, f32[4,20,128]{2,1,0:T(8,128)S(1)}, u32[]{:S(2)}, u32[]{:S(2)}) collective-permute-start(f32[4,20,128]{2,1,0:T(8,128)S(1)} %get-tuple-element.30), channel_id=1, source_target_pairs={{0,64},{64,128},{128,192},{192,256},{256,320},{320,384},{384,448},... | collective-permute-start | bytes 122888 | tf_op jit(solution)/shard_map/ppermute | solution.py:429
  85.6 4.7 %collective-permute-start.15 = (f32[4,20,128]{2,1,0:T(8,128)S(1)}, f32[4,20,128]{2,1,0:T(8,128)S(1)}, u32[]{:S(2)}, u32[]{:S(2)}) collective-permute-start(f32[4,20,128]{2,1,0:T(8,128)S(1)} %get-tuple-element.29), channel_id=1, source_target_pairs={{0,960},{64,0},{128,64},{192,128},{256,192},{320,256},{384,320},{4... | collective-permute-start | bytes 122888 | tf_op jit(solution)/shard_map/ppermute | solution.py:429

commit v5 on v4

--- a/solution.py
+++ b/solution.py
@@ -40,7 +40,7 @@
     return jnp.where(iota(first.shape, 0) >= 4, first, pltpu.roll(second, 4, 0))
 
 
-def pack_body(u, f, a, bx, by, bz, own, xl, xh, yl, yh, uv, fv, av, bxv, byv, bzv, sems):
+def pack_body(u, f, a, bx, by, bz, own, yh, yl, xl, xh, uv, fv, av, bxv, byv, bzv, sems):
     fields = (uv, fv, av, bxv, byv, bzv)
     copies = [pltpu.make_async_copy(src, dst, sems.at[k]) for k, (src, dst) in enumerate(zip((u, f, a, bx, by, bz), fields))]
     for copy in copies:
@@ -110,7 +110,7 @@
     return jnp.where(first, above, below)
 
 
-def corner_body(ylr, yhr, xcl, xch):
+def corner_body(yhr, ylr, xcl, xch):
     near = nearest(ylr.shape[1:])
     for out, plane in ((xcl, lambda d: d - 1), (xch, lambda d: 8 - d)):
         for t, (d, fields) in enumerate(CORNER):
@@ -298,7 +298,7 @@
             held[w + 1] = jnp.where(colours[(w + step) % 2], new, here)
 
 
-def fine_body(count, own, xlr, xhr, ylr, yhr, xclr, xchr, c1, out, p1, win, weights, held, diag, rows):
+def fine_body(count, own, xlr, xhr, yhr, ylr, xclr, xchr, c1, out, p1, win, weights, held, diag, rows):
     nz = own.shape[2]
     lower, upper = beside(count)[:2]
 
@@ -358,7 +358,7 @@
         for k in range(5):
             for half in range(2):
                 at = slice(8 * half, 8 * half + 8)
-                below, mid, above = source[0, k, at], source[1, k, at], source[2, k, at]
+                above, mid, below = source[0, k, at], source[1, k, at], source[2, k, at]
                 if k == 1 and there is not None:
                     below, mid, above = below * there, mid * there, above * there
                 w = 4 * b + 2 * half + 1
@@ -404,7 +404,7 @@
             win[k, 4 + i, 7:8] = up[at : at + 1]
             for b, (source, there) in enumerate(((left, factor[0]), (mid, 1.0), (right, factor[1]))):
                 for j in range(3):
-                    win[k, 2 + 2 * b + i, 1 + 2 * j : 3 + 2 * j] = source[j, at : at + 2] * there
+                    win[k, 2 + 2 * b + i, 1 + 2 * j : 3 + 2 * j] = source[2 - j, at : at + 2] * there
     held[0] = jnp.zeros(held.shape[1:], F32)
     held[9] = jnp.zeros(held.shape[1:], F32)
     colours = coloured(held.shape[1:])
@@ -438,16 +438,16 @@
     nz = solution.shape[2]
     count = lax.axis_size("gx")
     sent = shape(24, 8, nz)
-    own, xl, xh, yl, yh = call(
+    own, yh, yl, xl, xh = call(
         pack_body,
         (shape(48, 8, nz),) + (sent,) * 4,
         tuple(pltpu.with_memory_space_constraint(x, pltpu.HBM) for x in args),
         [pltpu.VMEM(x.shape, x.dtype) for x in args] + [pltpu.SemaphoreType.DMA((6,))],
         space=pltpu.HBM,
     )
-    ylr, yhr = along_y(yl, -1), along_y(yh, 1)
+    yhr, ylr = along_y(yh, 1), along_y(yl, -1)
     xlr, xhr = round_x(xl, -1), round_x(xh, 1)
-    xcl, xch = call(corner_body, (shape(len(CORNER), 8, nz),) * 2, (ylr, yhr))
+    xcl, xch = call(corner_body, (shape(len(CORNER), 8, nz),) * 2, (yhr, ylr))
     xclr, xchr = round_x(xcl, -1), round_x(xch, 1)
     c1, c2 = call(
         functools.partial(coarse_body, count),
@@ -463,7 +463,7 @@
     fine, p1 = call(
         functools.partial(fine_body, count),
         (shape(8, 8, nz), shape(5, 16, nz // 2)),
-        (own, xlr, xhr, ylr, yhr, xclr, xchr, c1),
+        (own, xlr, xhr, yhr, ylr, xclr, xchr, c1),
         [
             pltpu.VMEM((5, 17, 16, nz), F32),
             pltpu.VMEM((7, 16, 16, nz), F32),
@@ -474,7 +474,8 @@
         flops=20_000_000,
         nbytes=20_000_000,
     )
-    here = jnp.stack([along_y(p1, 1), p1, along_y(p1, -1)])
+    above, below = along_y(p1, -1), along_y(p1, 1)
+    here = jnp.stack([above, p1, below])
     left, right = round_x(here, 1), round_x(here, -1)
     middle, p2 = call(
         functools.partial(middle_body, count),
@@ -488,14 +489,14 @@
         ],
     )
     before, after = round_x(p2, 1), round_x(p2, -1)
-    below, above = along_y(p2, 1), along_y(p2, -1)
+    above, below = along_y(p2, -1), along_y(p2, 1)
     down, up = along_y(p2, 2), along_y(p2, -2)
-    left = round_x(jnp.stack([below, p2, above, before]), 1)
-    right = round_x(jnp.stack([below, p2, above, after]), -1)
+    left = round_x(jnp.stack([above, p2, below, before]), 1)
+    right = round_x(jnp.stack([above, p2, below, after]), -1)
     coarse = call(
         functools.partial(coarse_level_body, count),
         shape(2, 2, nz // 4),
-        (left, jnp.stack([below, p2, above]), right, down, up),
+        (left, jnp.stack([above, p2, below]), right, down, up),
         [
             pltpu.VMEM((5, 9, 8, nz // 4), F32),
             pltpu.VMEM((7, 8, 8, nz // 4), F32),

time: 91.6 us -> 89.8 us (0.980)
  waiting for transfers between devices: 30.8 us -> 21.8 us
  starting transfers between devices: 53.5 us -> 60.9 us
    ppermute x8, waiting for transfers between devices: 16 us -> 6.87 us  [along_y(): lax.ppermute(block, 'gy', [(i, i + by) for i in range(count) if 0 <= i +...]
    ppermute x8, starting transfers between devices: 38.8 us -> 46.8 us  [along_y(): lax.ppermute(block, 'gy', [(i, i + by) for i in range(count) if 0 <= i +...]
where the time goes in v5:
time: 89.8 us; the launch traced here: 89.5 us
  starting transfers between devices  60.9 us (68%)
  waiting for transfers between devices  21.8 us (24%)
  Pallas kernels  6.06 us (7%)
    ppermute x8, starting transfers between devices, along_y(): lax.ppermute(block, 'gy', [(i, i + by) for i in range(count) if 0 <= i +...  46.8 us
    ppermute x10, waiting for transfers between devices, round_x(): lax.ppermute(block, 'gx', [(i, (i + by) % count) for i in range(count)])  14.9 us
    ppermute x10, starting transfers between devices, round_x(): lax.ppermute(block, 'gx', [(i, (i + by) % count) for i in range(count)])  14.1 us
    ppermute x8, waiting for transfers between devices, along_y(): lax.ppermute(block, 'gy', [(i, i + by) for i in range(count) if 0 <= i +...  6.87 us
    pallas_call x6, Pallas kernels, call(): pl.pallas_call(body, out_shape=outs, in_specs=[pl.BlockSpec(memory_space=...  6.06 us
  transfers between devices with their start and end apart: 18, of which 10 were waited for; matrix products, arithmetic and copies ran while one was open for 0% of the time, Pallas kernels for 1%

profile of v5, /device:TPU:71, one launch (start us, length us, event | category | flops | bytes accessed | tf_op | source)
XLA Modules:
  0.0 89.5 jit_solution(8489015432641594562)
XLA Ops:
  0.6 1.3 %shard_map.85 = (f32[48,8,512]{2,1,0:T(8,128)S(1)}, f32[24,8,512]{2,1,0:T(8,128)S(1)}, f32[24,8,512]{2,1,0:T(8,128)S(1)}, f32[24,8,512]{2,1,0:T(8,128)S(1)}, f32[24,8,512]{2,1,0:T(8,128)S(1)}) custom-call(f32[8,8,512]{2,1,0:T(8,128)} %u.1, f32[8,8,512]{2,1,0:T(8,128)} %f.1, bf16[8,8,512]{2,1,0:T(8,128)(2,1)} %a.1, bf16[8,8,512]{2,1,0:T(8,128)(2,1)} %bx.1, ...), custom_call_target="tpu_custom_call" | custom-call | flops 1000000 | bytes 2000000 | tf_op jit(solution)/shard_map/pallas_call | solution.py:24
  2.0 4.9 %collective-permute-start.2 = (f32[24,8,512]{2,1,0:T(8,128)S(1)}, f32[24,8,512]{2,1,0:T(8,128)S(1)}, u32[]{:S(2)}, u32[]{:S(2)}) collective-permute-start(f32[24,8,512]{2,1,0:T(8,128)S(1)} %get-tuple-element.19), channel_id=1, source_target_pairs={{0,1},{1,2},{2,3},{3,4},{4,5},{5,6},{6,7},{7,8},{8,9},{9,10},{10,1... | collective-permute-start | bytes 1179656 | tf_op jit(solution)/shard_map/ppermute | solution.py:424
  6.9 13.8 %collective-permute-start.3 = (f32[24,8,512]{2,1,0:T(8,128)S(1)}, f32[24,8,512]{2,1,0:T(8,128)S(1)}, u32[]{:S(2)}, u32[]{:S(2)}) collective-permute-start(f32[24,8,512]{2,1,0:T(8,128)S(1)} %get-tuple-element.20), channel_id=1, source_target_pairs={{1,0},{2,1},{3,2},{4,3},{5,4},{6,5},{7,6},{8,7},{9,8},{10,9},{11,1... | collective-permute-start | bytes 1179656 | tf_op jit(solution)/shard_map/ppermute | solution.py:424
  20.7 3.3 %collective-permute-start.1 = (f32[24,8,512]{2,1,0:T(8,128)S(1)}, f32[24,8,512]{2,1,0:T(8,128)S(1)}, u32[]{:S(2)}, u32[]{:S(2)}) collective-permute-start(f32[24,8,512]{2,1,0:T(8,128)S(1)} %get-tuple-element.18), channel_id=1, source_target_pairs={{0,64},{64,128},{128,192},{192,256},{256,320},{320,384},{384,448},... | collective-permute-start | bytes 1179656 | tf_op jit(solution)/shard_map/ppermute | solution.py:429
  24.0 0.0 collective-permute-start
  24.0 3.6 %collective-permute-done.2.yhr = f32[24,8,512]{2,1,0:T(8,128)S(1)} collective-permute-done((f32[24,8,512]{2,1,0:T(8,128)S(1)}, f32[24,8,512]{2,1,0:T(8,128)S(1)}, u32[]{:S(2)}, u32[]{:S(2)}) %collective-permute-start.2) | collective-permute-done | bytes 393248 | tf_op jit(solution)/shard_map/ppermute | solution.py:424
  27.6 0.9 collective-permute-done.3.ylr
  28.5 1.6 %collective-permute-start.4 = (f32[16,8,512]{2,1,0:T(8,128)S(1)}, f32[16,8,512]{2,1,0:T(8,128)S(1)}, u32[]{:S(2)}, u32[]{:S(2)}) collective-permute-start(f32[16,8,512]{2,1,0:T(8,128)S(1)} %get-tuple-element.21), channel_id=1, source_target_pairs={{0,960},{64,0},{128,64},{192,128},{256,192},{320,256},{384,320},{4... | collective-permute-start | bytes 786440 | tf_op jit(solution)/shard_map/ppermute | solution.py:429
  30.1 2.3 %collective-permute-start.5 = (f32[16,8,512]{2,1,0:T(8,128)S(1)}, f32[16,8,512]{2,1,0:T(8,128)S(1)}, u32[]{:S(2)}, u32[]{:S(2)}) collective-permute-start(f32[16,8,512]{2,1,0:T(8,128)S(1)} %get-tuple-element.22), channel_id=1, source_target_pairs={{0,64},{64,128},{128,192},{192,256},{256,320},{320,384},{384,448},... | collective-permute-start | bytes 786440 | tf_op jit(solution)/shard_map/ppermute | solution.py:429
  32.4 0.0 collective-permute-done.1.xhr
  32.4 0.5 shard_map.87
  33.0 0.0 collective-permute-done.xlr
  33.0 3.5 %collective-permute-done.4.xclr = f32[16,8,512]{2,1,0:T(8,128)S(1)} collective-permute-done((f32[16,8,512]{2,1,0:T(8,128)S(1)}, f32[16,8,512]{2,1,0:T(8,128)S(1)}, u32[]{:S(2)}, u32[]{:S(2)}) %collective-permute-start.4) | collective-permute-done | bytes 262176 | tf_op jit(solution)/shard_map/ppermute | solution.py:429
  36.4 0.0 collective-permute-done.5.xchr
  36.4 2.2 %shard_map.88 = (f32[8,8,512]{2,1,0:T(8,128)}, f32[5,16,256]{2,1,0:T(8,128)S(1)}) custom-call(f32[48,8,512]{2,1,0:T(8,128)S(1)} %get-tuple-element.16.own, f32[24,8,512]{2,1,0:T(8,128)S(1)} %collective-permute-done.xlr, f32[24,8,512]{2,1,0:T(8,128)S(1)} %collective-permute-done.1.xhr, f32[24,8,512]{2,1,0:T(8,128)S(1)} %collective-permute-done.2.yhr, ...), custom_call_target="tpu_custom_call" | custom-call | flops 20000000 | bytes 20000000 | tf_op jit(solution)/shard_map/pallas_call | solution.py:24
  38.7 1.9 %collective-permute-start.7 = (f32[5,16,256]{2,1,0:T(8,128)S(1)}, f32[5,16,256]{2,1,0:T(8,128)S(1)}, u32[]{:S(2)}, u32[]{:S(2)}) collective-permute-start(f32[5,16,256]{2,1,0:T(8,128)S(1)} %get-tuple-element.25), channel_id=1, source_target_pairs={{0,1},{1,2},{2,3},{3,4},{4,5},{5,6},{6,7},{7,8},{8,9},{9,10},{10,1... | collective-permute-start | bytes 245768 | tf_op jit(solution)/shard_map/ppermute | solution.py:424
  40.6 7.4 %collective-permute-start.6 = (f32[5,16,256]{2,1,0:T(8,128)S(1)}, f32[5,16,256]{2,1,0:T(8,128)S(1)}, u32[]{:S(2)}, u32[]{:S(2)}) collective-permute-start(f32[5,16,256]{2,1,0:T(8,128)S(1)} %get-tuple-element.25), channel_id=1, source_target_pairs={{1,0},{2,1},{3,2},{4,3},{5,4},{6,5},{7,6},{8,7},{9,8},{10,9},{11,1... | collective-permute-start | bytes 245768 | tf_op jit(solution)/shard_map/ppermute | solution.py:424
  48.0 0.4 collective-permute-done.7
  48.4 1.8 %collective-permute-done.6 = f32[5,16,256]{2,1,0:T(8,128)S(1)} collective-permute-done((f32[5,16,256]{2,1,0:T(8,128)S(1)}, f32[5,16,256]{2,1,0:T(8,128)S(1)}, u32[]{:S(2)}, u32[]{:S(2)}) %collective-permute-start.6) | collective-permute-done | bytes 81952 | tf_op jit(solution)/shard_map/ppermute | solution.py:424
  50.3 3.1 %collective-permute-start.8 = (f32[3,5,16,256]{3,2,1,0:T(8,128)S(1)}, f32[3,5,16,256]{3,2,1,0:T(8,128)S(1)}, u32[]{:S(2)}, u32[]{:S(2)}) collective-permute-start(f32[3,5,16,256]{3,2,1,0:T(8,128)S(1)} %pad_maximum_fusion.here), channel_id=1, source_target_pairs={{0,64},{64,128},{128,192},{192,256},{256,320},{320,384},{384,448},... | collective-permute-start | bytes 737288 | tf_op jit(solution)/shard_map/ppermute | solution.py:429
  53.3 0.0 collective-permute-start.9
  53.3 3.1 %collective-permute-done.8.left = f32[3,5,16,256]{3,2,1,0:T(8,128)S(1)} collective-permute-done((f32[3,5,16,256]{3,2,1,0:T(8,128)S(1)}, f32[3,5,16,256]{3,2,1,0:T(8,128)S(1)}, u32[]{:S(2)}, u32[]{:S(2)}) %collective-permute-start.8) | collective-permute-done | bytes 245792 | tf_op jit(solution)/shard_map/ppermute | solution.py:429
  56.5 3.7 %collective-permute-done.9.right = f32[3,5,16,256]{3,2,1,0:T(8,128)S(1)} collective-permute-done((f32[3,5,16,256]{3,2,1,0:T(8,128)S(1)}, f32[3,5,16,256]{3,2,1,0:T(8,128)S(1)}, u32[]{:S(2)}, u32[]{:S(2)}) %collective-permute-start.9) | collective-permute-done | bytes 245792 | tf_op jit(solution)/shard_map/ppermute | solution.py:429
  60.2 1.1 %shard_map.89 = (f32[4,4,256]{2,1,0:T(4,128)}, f32[20,128]{1,0:T(8,128)S(1)}) custom-call(f32[3,5,16,256]{3,2,1,0:T(8,128)S(1)} %collective-permute-done.8.left, f32[3,5,16,256]{3,2,1,0:T(8,128)S(1)} %pad_maximum_fusion.here, f32[3,5,16,256]{3,2,1,0:T(8,128)S(1)} %collective-permute-done.9.right, f32[16,128]{1,0:T(8,128)S(1)} %get-tuple-element.26.c2), custom_call_target="tpu_custom_call" | custom-call | flops 1000000 | bytes 2000000 | tf_op jit(solution)/shard_map/pallas_call | solution.py:24
  61.2 0.0 collective-permute-start.14
  61.2 1.9 %collective-permute-start.11 = (f32[20,128]{1,0:T(8,128)S(1)}, f32[20,128]{1,0:T(8,128)S(1)}, u32[]{:S(2)}, u32[]{:S(2)}) collective-permute-start(f32[20,128]{1,0:T(8,128)S(1)} %get-tuple-element.28), channel_id=1, source_target_pairs={{0,1},{1,2},{2,3},{3,4},{4,5},{5,6},{6,7},{7,8},{8,9},{9,10},{10,1... | collective-permute-start | bytes 30728 | tf_op jit(solution)/shard_map/ppermute | solution.py:424
  63.2 7.3 %collective-permute-start.10 = (f32[20,128]{1,0:T(8,128)S(1)}, f32[20,128]{1,0:T(8,128)S(1)}, u32[]{:S(2)}, u32[]{:S(2)}) collective-permute-start(f32[20,128]{1,0:T(8,128)S(1)} %get-tuple-element.28), channel_id=1, source_target_pairs={{1,0},{2,1},{3,2},{4,3},{5,4},{6,5},{7,6},{8,7},{9,8},{10,9},{11,1... | collective-permute-start | bytes 30728 | tf_op jit(solution)/shard_map/ppermute | solution.py:424
  70.5 3.2 %collective-permute-start.12 = (f32[20,128]{1,0:T(8,128)S(1)}, f32[20,128]{1,0:T(8,128)S(1)}, u32[]{:S(2)}, u32[]{:S(2)}) collective-permute-start(f32[20,128]{1,0:T(8,128)S(1)} %get-tuple-element.28), channel_id=1, source_target_pairs={{0,64},{64,128},{128,192},{192,256},{256,320},{320,384},{384,448},... | collective-permute-start | bytes 30728 | tf_op jit(solution)/shard_map/ppermute | solution.py:429
  73.7 1.9 %collective-permute-start.16 = (f32[20,128]{1,0:T(8,128)S(1)}, f32[20,128]{1,0:T(8,128)S(1)}, u32[]{:S(2)}, u32[]{:S(2)}) collective-permute-start(f32[20,128]{1,0:T(8,128)S(1)} %get-tuple-element.28), channel_id=1, source_target_pairs={{0,2},{1,3},{2,4},{3,5},{4,6},{5,7},{6,8},{7,9},{8,10},{9,11},{10,... | collective-permute-start | bytes 30728 | tf_op jit(solution)/shard_map/ppermute | solution.py:424
  75.7 0.0 collective-permute-done.14
  75.7 7.6 %collective-permute-start.17 = (f32[20,128]{1,0:T(8,128)S(1)}, f32[20,128]{1,0:T(8,128)S(1)}, u32[]{:S(2)}, u32[]{:S(2)}) collective-permute-start(f32[20,128]{1,0:T(8,128)S(1)} %get-tuple-element.28), channel_id=1, source_target_pairs={{2,0},{3,1},{4,2},{5,3},{6,4},{7,5},{8,6},{9,7},{10,8},{11,9},{12,... | collective-permute-start | bytes 30728 | tf_op jit(solution)/shard_map/ppermute | solution.py:424
  83.2 0.0 collective-permute-done.11
  83.3 0.0 collective-permute-done.10
  83.3 0.0 collective-permute-done.12
  83.3 0.6 collective-permute-start.13
  83.9 0.0 collective-permute-start.15
  83.9 0.0 collective-permute-done.16.down
  83.9 0.1 collective-permute-done.17.up
  84.1 1.0 %collective-permute-done.13.left = f32[4,20,128]{2,1,0:T(8,128)S(1)} collective-permute-done((f32[4,20,128]{2,1,0:T(8,128)S(1)}, f32[4,20,128]{2,1,0:T(8,128)S(1)}, u32[]{:S(2)}, u32[]{:S(2)}) %collective-permute-start.13) | collective-permute-done | bytes 40992 | tf_op jit(solution)/shard_map/ppermute | solution.py:429
  85.1 3.5 %collective-permute-done.15.right = f32[4,20,128]{2,1,0:T(8,128)S(1)} collective-permute-done((f32[4,20,128]{2,1,0:T(8,128)S(1)}, f32[4,20,128]{2,1,0:T(8,128)S(1)}, u32[]{:S(2)}, u32[]{:S(2)}) %collective-permute-start.15) | collective-permute-done | bytes 40992 | tf_op jit(solution)/shard_map/ppermute | solution.py:429
  88.6 0.9 shard_map.90
  (4 shorter events, 0.1 us)
Async XLA Ops:
  2.0 25.6 %collective-permute-start.2 = (f32[24,8,512]{2,1,0:T(8,128)S(1)}, f32[24,8,512]{2,1,0:T(8,128)S(1)}, u32[]{:S(2)}, u32[]{:S(2)}) collective-permute-start(f32[24,8,512]{2,1,0:T(8,128)S(1)} %get-tuple-element.19), channel_id=1, source_target_pairs={{0,1},{1,2},{2,3},{3,4},{4,5},{5,6},{6,7},{7,8},{8,9},{9,10},{10,1... | collective-permute-start | bytes 1179656 | tf_op jit(solution)/shard_map/ppermute | solution.py:424
  6.9 21.6 %collective-permute-start.3 = (f32[24,8,512]{2,1,0:T(8,128)S(1)}, f32[24,8,512]{2,1,0:T(8,128)S(1)}, u32[]{:S(2)}, u32[]{:S(2)}) collective-permute-start(f32[24,8,512]{2,1,0:T(8,128)S(1)} %get-tuple-element.20), channel_id=1, source_target_pairs={{1,0},{2,1},{3,2},{4,3},{5,4},{6,5},{7,6},{8,7},{9,8},{10,9},{11,1... | collective-permute-start | bytes 1179656 | tf_op jit(solution)/shard_map/ppermute | solution.py:424
  20.7 11.7 %collective-permute-start.1 = (f32[24,8,512]{2,1,0:T(8,128)S(1)}, f32[24,8,512]{2,1,0:T(8,128)S(1)}, u32[]{:S(2)}, u32[]{:S(2)}) collective-permute-start(f32[24,8,512]{2,1,0:T(8,128)S(1)} %get-tuple-element.18), channel_id=1, source_target_pairs={{0,64},{64,128},{128,192},{192,256},{256,320},{320,384},{384,448},... | collective-permute-start | bytes 1179656 | tf_op jit(solution)/shard_map/ppermute | solution.py:429
  24.0 9.0 %collective-permute-start = (f32[24,8,512]{2,1,0:T(8,128)S(1)}, f32[24,8,512]{2,1,0:T(8,128)S(1)}, u32[]{:S(2)}, u32[]{:S(2)}) collective-permute-start(f32[24,8,512]{2,1,0:T(8,128)S(1)} %get-tuple-element.17), channel_id=1, source_target_pairs={{0,960},{64,0},{128,64},{192,128},{256,192},{320,256},{384,320},{4... | collective-permute-start | bytes 1179656 | tf_op jit(solution)/shard_map/ppermute | solution.py:429
  28.5 7.9 %collective-permute-start.4 = (f32[16,8,512]{2,1,0:T(8,128)S(1)}, f32[16,8,512]{2,1,0:T(8,128)S(1)}, u32[]{:S(2)}, u32[]{:S(2)}) collective-permute-start(f32[16,8,512]{2,1,0:T(8,128)S(1)} %get-tuple-element.21), channel_id=1, source_target_pairs={{0,960},{64,0},{128,64},{192,128},{256,192},{320,256},{384,320},{4... | collective-permute-start | bytes 786440 | tf_op jit(solution)/shard_map/ppermute | solution.py:429
  30.1 6.4 %collective-permute-start.5 = (f32[16,8,512]{2,1,0:T(8,128)S(1)}, f32[16,8,512]{2,1,0:T(8,128)S(1)}, u32[]{:S(2)}, u32[]{:S(2)}) collective-permute-start(f32[16,8,512]{2,1,0:T(8,128)S(1)} %get-tuple-element.22), channel_id=1, source_target_pairs={{0,64},{64,128},{128,192},{192,256},{256,320},{320,384},{384,448},... | collective-permute-start | bytes 786440 | tf_op jit(solution)/shard_map/ppermute | solution.py:429
  38.7 9.8 %collective-permute-start.7 = (f32[5,16,256]{2,1,0:T(8,128)S(1)}, f32[5,16,256]{2,1,0:T(8,128)S(1)}, u32[]{:S(2)}, u32[]{:S(2)}) collective-permute-start(f32[5,16,256]{2,1,0:T(8,128)S(1)} %get-tuple-element.25), channel_id=1, source_target_pairs={{0,1},{1,2},{2,3},{3,4},{4,5},{5,6},{6,7},{7,8},{8,9},{9,10},{10,1... | collective-permute-start | bytes 245768 | tf_op jit(solution)/shard_map/ppermute | solution.py:424
  40.6 9.7 %collective-permute-start.6 = (f32[5,16,256]{2,1,0:T(8,128)S(1)}, f32[5,16,256]{2,1,0:T(8,128)S(1)}, u32[]{:S(2)}, u32[]{:S(2)}) collective-permute-start(f32[5,16,256]{2,1,0:T(8,128)S(1)} %get-tuple-element.25), channel_id=1, source_target_pairs={{1,0},{2,1},{3,2},{4,3},{5,4},{6,5},{7,6},{8,7},{9,8},{10,9},{11,1... | collective-permute-start | bytes 245768 | tf_op jit(solution)/shard_map/ppermute | solution.py:424
  50.3 6.2 %collective-permute-start.8 = (f32[3,5,16,256]{3,2,1,0:T(8,128)S(1)}, f32[3,5,16,256]{3,2,1,0:T(8,128)S(1)}, u32[]{:S(2)}, u32[]{:S(2)}) collective-permute-start(f32[3,5,16,256]{3,2,1,0:T(8,128)S(1)} %pad_maximum_fusion.here), channel_id=1, source_target_pairs={{0,64},{64,128},{128,192},{192,256},{256,320},{320,384},{384,448},... | collective-permute-start | bytes 737288 | tf_op jit(solution)/shard_map/ppermute | solution.py:429
  53.3 6.8 %collective-permute-start.9 = (f32[3,5,16,256]{3,2,1,0:T(8,128)S(1)}, f32[3,5,16,256]{3,2,1,0:T(8,128)S(1)}, u32[]{:S(2)}, u32[]{:S(2)}) collective-permute-start(f32[3,5,16,256]{3,2,1,0:T(8,128)S(1)} %pad_maximum_fusion.here), channel_id=1, source_target_pairs={{0,960},{64,0},{128,64},{192,128},{256,192},{320,256},{384,320},{4... | collective-permute-start | bytes 737288 | tf_op jit(solution)/shard_map/ppermute | solution.py:429
  61.2 14.4 %collective-permute-start.14 = (f32[20,128]{1,0:T(8,128)S(1)}, f32[20,128]{1,0:T(8,128)S(1)}, u32[]{:S(2)}, u32[]{:S(2)}) collective-permute-start(f32[20,128]{1,0:T(8,128)S(1)} %get-tuple-element.28), channel_id=1, source_target_pairs={{0,960},{64,0},{128,64},{192,128},{256,192},{320,256},{384,320},{4... | collective-permute-start | bytes 30728 | tf_op jit(solution)/shard_map/ppermute | solution.py:429
  61.2 22.0 %collective-permute-start.11 = (f32[20,128]{1,0:T(8,128)S(1)}, f32[20,128]{1,0:T(8,128)S(1)}, u32[]{:S(2)}, u32[]{:S(2)}) collective-permute-start(f32[20,128]{1,0:T(8,128)S(1)} %get-tuple-element.28), channel_id=1, source_target_pairs={{0,1},{1,2},{2,3},{3,4},{4,5},{5,6},{6,7},{7,8},{8,9},{9,10},{10,1... | collective-permute-start | bytes 30728 | tf_op jit(solution)/shard_map/ppermute | solution.py:424
  63.2 20.1 %collective-permute-start.10 = (f32[20,128]{1,0:T(8,128)S(1)}, f32[20,128]{1,0:T(8,128)S(1)}, u32[]{:S(2)}, u32[]{:S(2)}) collective-permute-start(f32[20,128]{1,0:T(8,128)S(1)} %get-tuple-element.28), channel_id=1, source_target_pairs={{1,0},{2,1},{3,2},{4,3},{5,4},{6,5},{7,6},{8,7},{9,8},{10,9},{11,1... | collective-permute-start | bytes 30728 | tf_op jit(solution)/shard_map/ppermute | solution.py:424
  70.5 12.8 %collective-permute-start.12 = (f32[20,128]{1,0:T(8,128)S(1)}, f32[20,128]{1,0:T(8,128)S(1)}, u32[]{:S(2)}, u32[]{:S(2)}) collective-permute-start(f32[20,128]{1,0:T(8,128)S(1)} %get-tuple-element.28), channel_id=1, source_target_pairs={{0,64},{64,128},{128,192},{192,256},{256,320},{320,384},{384,448},... | collective-permute-start | bytes 30728 | tf_op jit(solution)/shard_map/ppermute | solution.py:429
  73.7 10.2 %collective-permute-start.16 = (f32[20,128]{1,0:T(8,128)S(1)}, f32[20,128]{1,0:T(8,128)S(1)}, u32[]{:S(2)}, u32[]{:S(2)}) collective-permute-start(f32[20,128]{1,0:T(8,128)S(1)} %get-tuple-element.28), channel_id=1, source_target_pairs={{0,2},{1,3},{2,4},{3,5},{4,6},{5,7},{6,8},{7,9},{8,10},{9,11},{10,... | collective-permute-start | bytes 30728 | tf_op jit(solution)/shard_map/ppermute | solution.py:424
  75.7 8.4 %collective-permute-start.17 = (f32[20,128]{1,0:T(8,128)S(1)}, f32[20,128]{1,0:T(8,128)S(1)}, u32[]{:S(2)}, u32[]{:S(2)}) collective-permute-start(f32[20,128]{1,0:T(8,128)S(1)} %get-tuple-element.28), channel_id=1, source_target_pairs={{2,0},{3,1},{4,2},{5,3},{6,4},{7,5},{8,6},{9,7},{10,8},{11,9},{12,... | collective-permute-start | bytes 30728 | tf_op jit(solution)/shard_map/ppermute | solution.py:424
  83.3 1.8 %collective-permute-start.13 = (f32[4,20,128]{2,1,0:T(8,128)S(1)}, f32[4,20,128]{2,1,0:T(8,128)S(1)}, u32[]{:S(2)}, u32[]{:S(2)}) collective-permute-start(f32[4,20,128]{2,1,0:T(8,128)S(1)} %get-tuple-element.30), channel_id=1, source_target_pairs={{0,64},{64,128},{128,192},{192,256},{256,320},{320,384},{384,448},... | collective-permute-start | bytes 122888 | tf_op jit(solution)/shard_map/ppermute | solution.py:429
  83.9 4.7 %collective-permute-start.15 = (f32[4,20,128]{2,1,0:T(8,128)S(1)}, f32[4,20,128]{2,1,0:T(8,128)S(1)}, u32[]{:S(2)}, u32[]{:S(2)}) collective-permute-start(f32[4,20,128]{2,1,0:T(8,128)S(1)} %get-tuple-element.29), channel_id=1, source_target_pairs={{0,960},{64,0},{128,64},{192,128},{256,192},{320,256},{384,320},{4... | collective-permute-start | bytes 122888 | tf_op jit(solution)/shard_map/ppermute | solution.py:429

commit v6 on v5

--- a/solution.py
+++ b/solution.py
@@ -404,7 +404,7 @@
             win[k, 4 + i, 7:8] = up[at : at + 1]
             for b, (source, there) in enumerate(((left, factor[0]), (mid, 1.0), (right, factor[1]))):
                 for j in range(3):
-                    win[k, 2 + 2 * b + i, 1 + 2 * j : 3 + 2 * j] = source[2 - j, at : at + 2] * there
+                    win[k, 2 + 2 * b + i, 1 + 2 * j : 3 + 2 * j] = source[j, at : at + 2] * there
     held[0] = jnp.zeros(held.shape[1:], F32)
     held[9] = jnp.zeros(held.shape[1:], F32)
     colours = coloured(held.shape[1:])
@@ -491,12 +491,12 @@
     before, after = round_x(p2, 1), round_x(p2, -1)
     above, below = along_y(p2, -1), along_y(p2, 1)
     down, up = along_y(p2, 2), along_y(p2, -2)
-    left = round_x(jnp.stack([above, p2, below, before]), 1)
-    right = round_x(jnp.stack([above, p2, below, after]), -1)
+    left = round_x(jnp.stack([below, p2, above, before]), 1)
+    right = round_x(jnp.stack([below, p2, above, after]), -1)
     coarse = call(
         functools.partial(coarse_level_body, count),
         shape(2, 2, nz // 4),
-        (left, jnp.stack([above, p2, below]), right, down, up),
+        (left, jnp.stack([below, p2, above]), right, down, up),
         [
             pltpu.VMEM((5, 9, 8, nz // 4), F32),
             pltpu.VMEM((7, 8, 8, nz // 4), F32),

time: 89.8 us -> 89.8 us (level)
  no operation moved by 1% of the time
where the time goes in v6:
time: 89.8 us; the launch traced here: 89.5 us
  starting transfers between devices  60.9 us (68%)
  waiting for transfers between devices  21.8 us (24%)
  Pallas kernels  6.06 us (7%)
    ppermute x8, starting transfers between devices, along_y(): lax.ppermute(block, 'gy', [(i, i + by) for i in range(count) if 0 <= i +...  46.8 us
    ppermute x10, waiting for transfers between devices, round_x(): lax.ppermute(block, 'gx', [(i, (i + by) % count) for i in range(count)])  14.9 us
    ppermute x10, starting transfers between devices, round_x(): lax.ppermute(block, 'gx', [(i, (i + by) % count) for i in range(count)])  14.1 us
    ppermute x8, waiting for transfers between devices, along_y(): lax.ppermute(block, 'gy', [(i, i + by) for i in range(count) if 0 <= i +...  6.87 us
    pallas_call x6, Pallas kernels, call(): pl.pallas_call(body, out_shape=outs, in_specs=[pl.BlockSpec(memory_space=...  6.06 us
  transfers between devices with their start and end apart: 18, of which 10 were waited for; matrix products, arithmetic and copies ran while one was open for 0% of the time, Pallas kernels for 1%

profile of v6, /device:TPU:71, one launch (start us, length us, event | category | flops | bytes accessed | tf_op | source)
XLA Modules:
  0.0 89.5 jit_solution(15176368174489853225)
XLA Ops:
  0.6 1.3 %shard_map.85 = (f32[48,8,512]{2,1,0:T(8,128)S(1)}, f32[24,8,512]{2,1,0:T(8,128)S(1)}, f32[24,8,512]{2,1,0:T(8,128)S(1)}, f32[24,8,512]{2,1,0:T(8,128)S(1)}, f32[24,8,512]{2,1,0:T(8,128)S(1)}) custom-call(f32[8,8,512]{2,1,0:T(8,128)} %u.1, f32[8,8,512]{2,1,0:T(8,128)} %f.1, bf16[8,8,512]{2,1,0:T(8,128)(2,1)} %a.1, bf16[8,8,512]{2,1,0:T(8,128)(2,1)} %bx.1, ...), custom_call_target="tpu_custom_call" | custom-call | flops 1000000 | bytes 2000000 | tf_op jit(solution)/shard_map/pallas_call | solution.py:24
  2.0 4.9 %collective-permute-start.2 = (f32[24,8,512]{2,1,0:T(8,128)S(1)}, f32[24,8,512]{2,1,0:T(8,128)S(1)}, u32[]{:S(2)}, u32[]{:S(2)}) collective-permute-start(f32[24,8,512]{2,1,0:T(8,128)S(1)} %get-tuple-element.19), channel_id=1, source_target_pairs={{0,1},{1,2},{2,3},{3,4},{4,5},{5,6},{6,7},{7,8},{8,9},{9,10},{10,1... | collective-permute-start | bytes 1179656 | tf_op jit(solution)/shard_map/ppermute | solution.py:424
  6.9 13.8 %collective-permute-start.3 = (f32[24,8,512]{2,1,0:T(8,128)S(1)}, f32[24,8,512]{2,1,0:T(8,128)S(1)}, u32[]{:S(2)}, u32[]{:S(2)}) collective-permute-start(f32[24,8,512]{2,1,0:T(8,128)S(1)} %get-tuple-element.20), channel_id=1, source_target_pairs={{1,0},{2,1},{3,2},{4,3},{5,4},{6,5},{7,6},{8,7},{9,8},{10,9},{11,1... | collective-permute-start | bytes 1179656 | tf_op jit(solution)/shard_map/ppermute | solution.py:424
  20.7 3.3 %collective-permute-start.1 = (f32[24,8,512]{2,1,0:T(8,128)S(1)}, f32[24,8,512]{2,1,0:T(8,128)S(1)}, u32[]{:S(2)}, u32[]{:S(2)}) collective-permute-start(f32[24,8,512]{2,1,0:T(8,128)S(1)} %get-tuple-element.18), channel_id=1, source_target_pairs={{0,64},{64,128},{128,192},{192,256},{256,320},{320,384},{384,448},... | collective-permute-start | bytes 1179656 | tf_op jit(solution)/shard_map/ppermute | solution.py:429
  24.0 0.0 collective-permute-start
  24.0 3.6 %collective-permute-done.2.yhr = f32[24,8,512]{2,1,0:T(8,128)S(1)} collective-permute-done((f32[24,8,512]{2,1,0:T(8,128)S(1)}, f32[24,8,512]{2,1,0:T(8,128)S(1)}, u32[]{:S(2)}, u32[]{:S(2)}) %collective-permute-start.2) | collective-permute-done | bytes 393248 | tf_op jit(solution)/shard_map/ppermute | solution.py:424
  27.6 0.9 collective-permute-done.3.ylr
  28.5 1.6 %collective-permute-start.4 = (f32[16,8,512]{2,1,0:T(8,128)S(1)}, f32[16,8,512]{2,1,0:T(8,128)S(1)}, u32[]{:S(2)}, u32[]{:S(2)}) collective-permute-start(f32[16,8,512]{2,1,0:T(8,128)S(1)} %get-tuple-element.21), channel_id=1, source_target_pairs={{0,960},{64,0},{128,64},{192,128},{256,192},{320,256},{384,320},{4... | collective-permute-start | bytes 786440 | tf_op jit(solution)/shard_map/ppermute | solution.py:429
  30.1 2.3 %collective-permute-start.5 = (f32[16,8,512]{2,1,0:T(8,128)S(1)}, f32[16,8,512]{2,1,0:T(8,128)S(1)}, u32[]{:S(2)}, u32[]{:S(2)}) collective-permute-start(f32[16,8,512]{2,1,0:T(8,128)S(1)} %get-tuple-element.22), channel_id=1, source_target_pairs={{0,64},{64,128},{128,192},{192,256},{256,320},{320,384},{384,448},... | collective-permute-start | bytes 786440 | tf_op jit(solution)/shard_map/ppermute | solution.py:429
  32.4 0.0 collective-permute-done.1.xhr
  32.4 0.5 shard_map.87
  33.0 0.0 collective-permute-done.xlr
  33.0 3.5 %collective-permute-done.4.xclr = f32[16,8,512]{2,1,0:T(8,128)S(1)} collective-permute-done((f32[16,8,512]{2,1,0:T(8,128)S(1)}, f32[16,8,512]{2,1,0:T(8,128)S(1)}, u32[]{:S(2)}, u32[]{:S(2)}) %collective-permute-start.4) | collective-permute-done | bytes 262176 | tf_op jit(solution)/shard_map/ppermute | solution.py:429
  36.4 0.0 collective-permute-done.5.xchr
  36.4 2.2 %shard_map.88 = (f32[8,8,512]{2,1,0:T(8,128)}, f32[5,16,256]{2,1,0:T(8,128)S(1)}) custom-call(f32[48,8,512]{2,1,0:T(8,128)S(1)} %get-tuple-element.16.own, f32[24,8,512]{2,1,0:T(8,128)S(1)} %collective-permute-done.xlr, f32[24,8,512]{2,1,0:T(8,128)S(1)} %collective-permute-done.1.xhr, f32[24,8,512]{2,1,0:T(8,128)S(1)} %collective-permute-done.2.yhr, ...), custom_call_target="tpu_custom_call" | custom-call | flops 20000000 | bytes 20000000 | tf_op jit(solution)/shard_map/pallas_call | solution.py:24
  38.7 1.9 %collective-permute-start.7 = (f32[5,16,256]{2,1,0:T(8,128)S(1)}, f32[5,16,256]{2,1,0:T(8,128)S(1)}, u32[]{:S(2)}, u32[]{:S(2)}) collective-permute-start(f32[5,16,256]{2,1,0:T(8,128)S(1)} %get-tuple-element.25), channel_id=1, source_target_pairs={{0,1},{1,2},{2,3},{3,4},{4,5},{5,6},{6,7},{7,8},{8,9},{9,10},{10,1... | collective-permute-start | bytes 245768 | tf_op jit(solution)/shard_map/ppermute | solution.py:424
  40.6 7.4 %collective-permute-start.6 = (f32[5,16,256]{2,1,0:T(8,128)S(1)}, f32[5,16,256]{2,1,0:T(8,128)S(1)}, u32[]{:S(2)}, u32[]{:S(2)}) collective-permute-start(f32[5,16,256]{2,1,0:T(8,128)S(1)} %get-tuple-element.25), channel_id=1, source_target_pairs={{1,0},{2,1},{3,2},{4,3},{5,4},{6,5},{7,6},{8,7},{9,8},{10,9},{11,1... | collective-permute-start | bytes 245768 | tf_op jit(solution)/shard_map/ppermute | solution.py:424
  48.0 0.4 collective-permute-done.7
  48.4 1.8 %collective-permute-done.6 = f32[5,16,256]{2,1,0:T(8,128)S(1)} collective-permute-done((f32[5,16,256]{2,1,0:T(8,128)S(1)}, f32[5,16,256]{2,1,0:T(8,128)S(1)}, u32[]{:S(2)}, u32[]{:S(2)}) %collective-permute-start.6) | collective-permute-done | bytes 81952 | tf_op jit(solution)/shard_map/ppermute | solution.py:424
  50.3 3.1 %collective-permute-start.8 = (f32[3,5,16,256]{3,2,1,0:T(8,128)S(1)}, f32[3,5,16,256]{3,2,1,0:T(8,128)S(1)}, u32[]{:S(2)}, u32[]{:S(2)}) collective-permute-start(f32[3,5,16,256]{3,2,1,0:T(8,128)S(1)} %pad_maximum_fusion.here), channel_id=1, source_target_pairs={{0,64},{64,128},{128,192},{192,256},{256,320},{320,384},{384,448},... | collective-permute-start | bytes 737288 | tf_op jit(solution)/shard_map/ppermute | solution.py:429
  53.3 0.0 collective-permute-start.9
  53.3 3.1 %collective-permute-done.8.left = f32[3,5,16,256]{3,2,1,0:T(8,128)S(1)} collective-permute-done((f32[3,5,16,256]{3,2,1,0:T(8,128)S(1)}, f32[3,5,16,256]{3,2,1,0:T(8,128)S(1)}, u32[]{:S(2)}, u32[]{:S(2)}) %collective-permute-start.8) | collective-permute-done | bytes 245792 | tf_op jit(solution)/shard_map/ppermute | solution.py:429
  56.5 3.7 %collective-permute-done.9.right = f32[3,5,16,256]{3,2,1,0:T(8,128)S(1)} collective-permute-done((f32[3,5,16,256]{3,2,1,0:T(8,128)S(1)}, f32[3,5,16,256]{3,2,1,0:T(8,128)S(1)}, u32[]{:S(2)}, u32[]{:S(2)}) %collective-permute-start.9) | collective-permute-done | bytes 245792 | tf_op jit(solution)/shard_map/ppermute | solution.py:429
  60.2 1.1 %shard_map.89 = (f32[4,4,256]{2,1,0:T(4,128)}, f32[20,128]{1,0:T(8,128)S(1)}) custom-call(f32[3,5,16,256]{3,2,1,0:T(8,128)S(1)} %collective-permute-done.8.left, f32[3,5,16,256]{3,2,1,0:T(8,128)S(1)} %pad_maximum_fusion.here, f32[3,5,16,256]{3,2,1,0:T(8,128)S(1)} %collective-permute-done.9.right, f32[16,128]{1,0:T(8,128)S(1)} %get-tuple-element.26.c2), custom_call_target="tpu_custom_call" | custom-call | flops 1000000 | bytes 2000000 | tf_op jit(solution)/shard_map/pallas_call | solution.py:24
  61.2 0.0 collective-permute-start.14
  61.2 7.3 %collective-permute-start.11 = (f32[20,128]{1,0:T(8,128)S(1)}, f32[20,128]{1,0:T(8,128)S(1)}, u32[]{:S(2)}, u32[]{:S(2)}) collective-permute-start(f32[20,128]{1,0:T(8,128)S(1)} %get-tuple-element.28), channel_id=1, source_target_pairs={{1,0},{2,1},{3,2},{4,3},{5,4},{6,5},{7,6},{8,7},{9,8},{10,9},{11,1... | collective-permute-start | bytes 30728 | tf_op jit(solution)/shard_map/ppermute | solution.py:424
  68.6 1.9 %collective-permute-start.10 = (f32[20,128]{1,0:T(8,128)S(1)}, f32[20,128]{1,0:T(8,128)S(1)}, u32[]{:S(2)}, u32[]{:S(2)}) collective-permute-start(f32[20,128]{1,0:T(8,128)S(1)} %get-tuple-element.28), channel_id=1, source_target_pairs={{0,1},{1,2},{2,3},{3,4},{4,5},{5,6},{6,7},{7,8},{8,9},{9,10},{10,1... | collective-permute-start | bytes 30728 | tf_op jit(solution)/shard_map/ppermute | solution.py:424
  70.5 3.2 %collective-permute-start.12 = (f32[20,128]{1,0:T(8,128)S(1)}, f32[20,128]{1,0:T(8,128)S(1)}, u32[]{:S(2)}, u32[]{:S(2)}) collective-permute-start(f32[20,128]{1,0:T(8,128)S(1)} %get-tuple-element.28), channel_id=1, source_target_pairs={{0,64},{64,128},{128,192},{192,256},{256,320},{320,384},{384,448},... | collective-permute-start | bytes 30728 | tf_op jit(solution)/shard_map/ppermute | solution.py:429
  73.7 1.9 %collective-permute-start.16 = (f32[20,128]{1,0:T(8,128)S(1)}, f32[20,128]{1,0:T(8,128)S(1)}, u32[]{:S(2)}, u32[]{:S(2)}) collective-permute-start(f32[20,128]{1,0:T(8,128)S(1)} %get-tuple-element.28), channel_id=1, source_target_pairs={{0,2},{1,3},{2,4},{3,5},{4,6},{5,7},{6,8},{7,9},{8,10},{9,11},{10,... | collective-permute-start | bytes 30728 | tf_op jit(solution)/shard_map/ppermute | solution.py:424
  75.7 0.0 collective-permute-done.14
  75.7 7.6 %collective-permute-start.17 = (f32[20,128]{1,0:T(8,128)S(1)}, f32[20,128]{1,0:T(8,128)S(1)}, u32[]{:S(2)}, u32[]{:S(2)}) collective-permute-start(f32[20,128]{1,0:T(8,128)S(1)} %get-tuple-element.28), channel_id=1, source_target_pairs={{2,0},{3,1},{4,2},{5,3},{6,4},{7,5},{8,6},{9,7},{10,8},{11,9},{12,... | collective-permute-start | bytes 30728 | tf_op jit(solution)/shard_map/ppermute | solution.py:424
  83.2 0.0 collective-permute-done.11
  83.3 0.0 collective-permute-done.10
  83.3 0.0 collective-permute-done.12
  83.3 0.6 collective-permute-start.13
  83.9 0.0 collective-permute-start.15
  83.9 0.0 collective-permute-done.16.down
  83.9 0.1 collective-permute-done.17.up
  84.1 1.0 %collective-permute-done.13.left = f32[4,20,128]{2,1,0:T(8,128)S(1)} collective-permute-done((f32[4,20,128]{2,1,0:T(8,128)S(1)}, f32[4,20,128]{2,1,0:T(8,128)S(1)}, u32[]{:S(2)}, u32[]{:S(2)}) %collective-permute-start.13) | collective-permute-done | bytes 40992 | tf_op jit(solution)/shard_map/ppermute | solution.py:429
  85.1 3.5 %collective-permute-done.15.right = f32[4,20,128]{2,1,0:T(8,128)S(1)} collective-permute-done((f32[4,20,128]{2,1,0:T(8,128)S(1)}, f32[4,20,128]{2,1,0:T(8,128)S(1)}, u32[]{:S(2)}, u32[]{:S(2)}) %collective-permute-start.15) | collective-permute-done | bytes 40992 | tf_op jit(solution)/shard_map/ppermute | solution.py:429
  88.6 0.9 shard_map.90
  (4 shorter events, 0.1 us)
Async XLA Ops:
  2.0 25.6 %collective-permute-start.2 = (f32[24,8,512]{2,1,0:T(8,128)S(1)}, f32[24,8,512]{2,1,0:T(8,128)S(1)}, u32[]{:S(2)}, u32[]{:S(2)}) collective-permute-start(f32[24,8,512]{2,1,0:T(8,128)S(1)} %get-tuple-element.19), channel_id=1, source_target_pairs={{0,1},{1,2},{2,3},{3,4},{4,5},{5,6},{6,7},{7,8},{8,9},{9,10},{10,1... | collective-permute-start | bytes 1179656 | tf_op jit(solution)/shard_map/ppermute | solution.py:424
  6.9 21.6 %collective-permute-start.3 = (f32[24,8,512]{2,1,0:T(8,128)S(1)}, f32[24,8,512]{2,1,0:T(8,128)S(1)}, u32[]{:S(2)}, u32[]{:S(2)}) collective-permute-start(f32[24,8,512]{2,1,0:T(8,128)S(1)} %get-tuple-element.20), channel_id=1, source_target_pairs={{1,0},{2,1},{3,2},{4,3},{5,4},{6,5},{7,6},{8,7},{9,8},{10,9},{11,1... | collective-permute-start | bytes 1179656 | tf_op jit(solution)/shard_map/ppermute | solution.py:424
  20.7 11.7 %collective-permute-start.1 = (f32[24,8,512]{2,1,0:T(8,128)S(1)}, f32[24,8,512]{2,1,0:T(8,128)S(1)}, u32[]{:S(2)}, u32[]{:S(2)}) collective-permute-start(f32[24,8,512]{2,1,0:T(8,128)S(1)} %get-tuple-element.18), channel_id=1, source_target_pairs={{0,64},{64,128},{128,192},{192,256},{256,320},{320,384},{384,448},... | collective-permute-start | bytes 1179656 | tf_op jit(solution)/shard_map/ppermute | solution.py:429
  24.0 9.0 %collective-permute-start = (f32[24,8,512]{2,1,0:T(8,128)S(1)}, f32[24,8,512]{2,1,0:T(8,128)S(1)}, u32[]{:S(2)}, u32[]{:S(2)}) collective-permute-start(f32[24,8,512]{2,1,0:T(8,128)S(1)} %get-tuple-element.17), channel_id=1, source_target_pairs={{0,960},{64,0},{128,64},{192,128},{256,192},{320,256},{384,320},{4... | collective-permute-start | bytes 1179656 | tf_op jit(solution)/shard_map/ppermute | solution.py:429
  28.5 7.9 %collective-permute-start.4 = (f32[16,8,512]{2,1,0:T(8,128)S(1)}, f32[16,8,512]{2,1,0:T(8,128)S(1)}, u32[]{:S(2)}, u32[]{:S(2)}) collective-permute-start(f32[16,8,512]{2,1,0:T(8,128)S(1)} %get-tuple-element.21), channel_id=1, source_target_pairs={{0,960},{64,0},{128,64},{192,128},{256,192},{320,256},{384,320},{4... | collective-permute-start | bytes 786440 | tf_op jit(solution)/shard_map/ppermute | solution.py:429
  30.1 6.4 %collective-permute-start.5 = (f32[16,8,512]{2,1,0:T(8,128)S(1)}, f32[16,8,512]{2,1,0:T(8,128)S(1)}, u32[]{:S(2)}, u32[]{:S(2)}) collective-permute-start(f32[16,8,512]{2,1,0:T(8,128)S(1)} %get-tuple-element.22), channel_id=1, source_target_pairs={{0,64},{64,128},{128,192},{192,256},{256,320},{320,384},{384,448},... | collective-permute-start | bytes 786440 | tf_op jit(solution)/shard_map/ppermute | solution.py:429
  38.7 9.8 %collective-permute-start.7 = (f32[5,16,256]{2,1,0:T(8,128)S(1)}, f32[5,16,256]{2,1,0:T(8,128)S(1)}, u32[]{:S(2)}, u32[]{:S(2)}) collective-permute-start(f32[5,16,256]{2,1,0:T(8,128)S(1)} %get-tuple-element.25), channel_id=1, source_target_pairs={{0,1},{1,2},{2,3},{3,4},{4,5},{5,6},{6,7},{7,8},{8,9},{9,10},{10,1... | collective-permute-start | bytes 245768 | tf_op jit(solution)/shard_map/ppermute | solution.py:424
  40.6 9.7 %collective-permute-start.6 = (f32[5,16,256]{2,1,0:T(8,128)S(1)}, f32[5,16,256]{2,1,0:T(8,128)S(1)}, u32[]{:S(2)}, u32[]{:S(2)}) collective-permute-start(f32[5,16,256]{2,1,0:T(8,128)S(1)} %get-tuple-element.25), channel_id=1, source_target_pairs={{1,0},{2,1},{3,2},{4,3},{5,4},{6,5},{7,6},{8,7},{9,8},{10,9},{11,1... | collective-permute-start | bytes 245768 | tf_op jit(solution)/shard_map/ppermute | solution.py:424
  50.3 6.2 %collective-permute-start.8 = (f32[3,5,16,256]{3,2,1,0:T(8,128)S(1)}, f32[3,5,16,256]{3,2,1,0:T(8,128)S(1)}, u32[]{:S(2)}, u32[]{:S(2)}) collective-permute-start(f32[3,5,16,256]{3,2,1,0:T(8,128)S(1)} %pad_maximum_fusion.here), channel_id=1, source_target_pairs={{0,64},{64,128},{128,192},{192,256},{256,320},{320,384},{384,448},... | collective-permute-start | bytes 737288 | tf_op jit(solution)/shard_map/ppermute | solution.py:429
  53.3 6.8 %collective-permute-start.9 = (f32[3,5,16,256]{3,2,1,0:T(8,128)S(1)}, f32[3,5,16,256]{3,2,1,0:T(8,128)S(1)}, u32[]{:S(2)}, u32[]{:S(2)}) collective-permute-start(f32[3,5,16,256]{3,2,1,0:T(8,128)S(1)} %pad_maximum_fusion.here), channel_id=1, source_target_pairs={{0,960},{64,0},{128,64},{192,128},{256,192},{320,256},{384,320},{4... | collective-permute-start | bytes 737288 | tf_op jit(solution)/shard_map/ppermute | solution.py:429
  61.2 14.4 %collective-permute-start.14 = (f32[20,128]{1,0:T(8,128)S(1)}, f32[20,128]{1,0:T(8,128)S(1)}, u32[]{:S(2)}, u32[]{:S(2)}) collective-permute-start(f32[20,128]{1,0:T(8,128)S(1)} %get-tuple-element.28), channel_id=1, source_target_pairs={{0,960},{64,0},{128,64},{192,128},{256,192},{320,256},{384,320},{4... | collective-permute-start | bytes 30728 | tf_op jit(solution)/shard_map/ppermute | solution.py:429
  61.2 22.0 %collective-permute-start.11 = (f32[20,128]{1,0:T(8,128)S(1)}, f32[20,128]{1,0:T(8,128)S(1)}, u32[]{:S(2)}, u32[]{:S(2)}) collective-permute-start(f32[20,128]{1,0:T(8,128)S(1)} %get-tuple-element.28), channel_id=1, source_target_pairs={{1,0},{2,1},{3,2},{4,3},{5,4},{6,5},{7,6},{8,7},{9,8},{10,9},{11,1... | collective-permute-start | bytes 30728 | tf_op jit(solution)/shard_map/ppermute | solution.py:424
  68.6 14.7 %collective-permute-start.10 = (f32[20,128]{1,0:T(8,128)S(1)}, f32[20,128]{1,0:T(8,128)S(1)}, u32[]{:S(2)}, u32[]{:S(2)}) collective-permute-start(f32[20,128]{1,0:T(8,128)S(1)} %get-tuple-element.28), channel_id=1, source_target_pairs={{0,1},{1,2},{2,3},{3,4},{4,5},{5,6},{6,7},{7,8},{8,9},{9,10},{10,1... | collective-permute-start | bytes 30728 | tf_op jit(solution)/shard_map/ppermute | solution.py:424
  70.5 12.8 %collective-permute-start.12 = (f32[20,128]{1,0:T(8,128)S(1)}, f32[20,128]{1,0:T(8,128)S(1)}, u32[]{:S(2)}, u32[]{:S(2)}) collective-permute-start(f32[20,128]{1,0:T(8,128)S(1)} %get-tuple-element.28), channel_id=1, source_target_pairs={{0,64},{64,128},{128,192},{192,256},{256,320},{320,384},{384,448},... | collective-permute-start | bytes 30728 | tf_op jit(solution)/shard_map/ppermute | solution.py:429
  73.7 10.2 %collective-permute-start.16 = (f32[20,128]{1,0:T(8,128)S(1)}, f32[20,128]{1,0:T(8,128)S(1)}, u32[]{:S(2)}, u32[]{:S(2)}) collective-permute-start(f32[20,128]{1,0:T(8,128)S(1)} %get-tuple-element.28), channel_id=1, source_target_pairs={{0,2},{1,3},{2,4},{3,5},{4,6},{5,7},{6,8},{7,9},{8,10},{9,11},{10,... | collective-permute-start | bytes 30728 | tf_op jit(solution)/shard_map/ppermute | solution.py:424
  75.7 8.4 %collective-permute-start.17 = (f32[20,128]{1,0:T(8,128)S(1)}, f32[20,128]{1,0:T(8,128)S(1)}, u32[]{:S(2)}, u32[]{:S(2)}) collective-permute-start(f32[20,128]{1,0:T(8,128)S(1)} %get-tuple-element.28), channel_id=1, source_target_pairs={{2,0},{3,1},{4,2},{5,3},{6,4},{7,5},{8,6},{9,7},{10,8},{11,9},{12,... | collective-permute-start | bytes 30728 | tf_op jit(solution)/shard_map/ppermute | solution.py:424
  83.3 1.8 %collective-permute-start.13 = (f32[4,20,128]{2,1,0:T(8,128)S(1)}, f32[4,20,128]{2,1,0:T(8,128)S(1)}, u32[]{:S(2)}, u32[]{:S(2)}) collective-permute-start(f32[4,20,128]{2,1,0:T(8,128)S(1)} %get-tuple-element.30), channel_id=1, source_target_pairs={{0,64},{64,128},{128,192},{192,256},{256,320},{320,384},{384,448},... | collective-permute-start | bytes 122888 | tf_op jit(solution)/shard_map/ppermute | solution.py:429
  83.9 4.7 %collective-permute-start.15 = (f32[4,20,128]{2,1,0:T(8,128)S(1)}, f32[4,20,128]{2,1,0:T(8,128)S(1)}, u32[]{:S(2)}, u32[]{:S(2)}) collective-permute-start(f32[4,20,128]{2,1,0:T(8,128)S(1)} %get-tuple-element.29), channel_id=1, source_target_pairs={{0,960},{64,0},{128,64},{192,128},{256,192},{320,256},{384,320},{4... | collective-permute-start | bytes 122888 | tf_op jit(solution)/shard_map/ppermute | solution.py:429

commit v7 on v6

--- a/solution.py
+++ b/solution.py
@@ -424,6 +424,18 @@
     return lax.ppermute(block, "gy", [(i, i + by) for i in range(count) if 0 <= i + by < count])
 
 
+def swapped(block, odd):
+    count = lax.axis_size("gy")
+    firsts = range(int(odd), count - 1, 2)
+    return lax.ppermute(block, "gy", [(i, i + 1) for i in firsts] + [(i + 1, i) for i in firsts])
+
+
+def both_sides(block):
+    one, other = swapped(block, False), swapped(block, True)
+    first = lax.axis_index("gy") % 2 == 0
+    return jnp.where(first, other, one), jnp.where(first, one, other)
+
+
 def round_x(block, by):
     count = lax.axis_size("gx")
     return lax.ppermute(block, "gx", [(i, (i + by) % count) for i in range(count)])
@@ -474,7 +486,7 @@
         flops=20_000_000,
         nbytes=20_000_000,
     )
-    above, below = along_y(p1, -1), along_y(p1, 1)
+    below, above = both_sides(p1)
     here = jnp.stack([above, p1, below])
     left, right = round_x(here, 1), round_x(here, -1)
     middle, p2 = call(
@@ -489,7 +501,7 @@
         ],
     )
     before, after = round_x(p2, 1), round_x(p2, -1)
-    above, below = along_y(p2, -1), along_y(p2, 1)
+    below, above = both_sides(p2)
     down, up = along_y(p2, 2), along_y(p2, -2)
     left = round_x(jnp.stack([below, p2, above, before]), 1)
     right = round_x(jnp.stack([below, p2, above, after]), -1)

time: 89.8 us -> 89.6 us (level)
    ppermute x8 -> x4, starting transfers between devices: 46.8 us -> 28.2 us  [along_y(): lax.ppermute(block, 'gy', [(i, i + by) for i in range(count) if 0 <= i +...]
    ppermute x0 -> x4, starting transfers between devices: none -> 18.2 us  [swapped(): lax.ppermute(block, 'gy', [(i, i + 1) for i in firsts] + [(i + 1, i) for...]
    ppermute x0 -> x4, waiting for transfers between devices: none -> 2.33 us  [swapped(): lax.ppermute(block, 'gy', [(i, i + 1) for i in firsts] + [(i + 1, i) for...]
    ppermute x8 -> x4, waiting for transfers between devices: 6.87 us -> 4.64 us  [along_y(): lax.ppermute(block, 'gy', [(i, i + by) for i in range(count) if 0 <= i +...]
  transfers between devices with their start and end apart: 18 -> 18, of which waited for: 10 -> 9; matrix products, arithmetic and copies ran while one was open for 0% -> 0% of each run, Pallas kernels for 1% -> 1%
where the time goes in v7:
time: 89.6 us; the launch traced here: 89.2 us
  starting transfers between devices  60.4 us (67%)
  waiting for transfers between devices  21.8 us (24%)
  Pallas kernels  6.06 us (7%)
    ppermute x4, starting transfers between devices, along_y(): lax.ppermute(block, 'gy', [(i, i + by) for i in range(count) if 0 <= i +...  28.2 us
    ppermute x4, starting transfers between devices, swapped(): lax.ppermute(block, 'gy', [(i, i + 1) for i in firsts] + [(i + 1, i) for...  18.2 us
    ppermute x10, waiting for transfers between devices, round_x(): lax.ppermute(block, 'gx', [(i, (i + by) % count) for i in range(count)])  14.9 us
    ppermute x10, starting transfers between devices, round_x(): lax.ppermute(block, 'gx', [(i, (i + by) % count) for i in range(count)])  14 us
    pallas_call x6, Pallas kernels, call(): pl.pallas_call(body, out_shape=outs, in_specs=[pl.BlockSpec(memory_space=...  6.06 us
    ppermute x4, waiting for transfers between devices, along_y(): lax.ppermute(block, 'gy', [(i, i + by) for i in range(count) if 0 <= i +...  4.64 us
    ppermute x4, waiting for transfers between devices, swapped(): lax.ppermute(block, 'gy', [(i, i + 1) for i in firsts] + [(i + 1, i) for...  2.33 us
  transfers between devices with their start and end apart: 18, of which 9 were waited for; matrix products, arithmetic and copies ran while one was open for 0% of the time, Pallas kernels for 1%

profile of v7, /device:TPU:71, one launch (start us, length us, event | category | flops | bytes accessed | tf_op | source)
XLA Modules:
  0.0 89.2 jit_solution(16624814389353473293)
XLA Ops:
  0.6 1.3 %shard_map.85 = (f32[48,8,512]{2,1,0:T(8,128)S(1)}, f32[24,8,512]{2,1,0:T(8,128)S(1)}, f32[24,8,512]{2,1,0:T(8,128)S(1)}, f32[24,8,512]{2,1,0:T(8,128)S(1)}, f32[24,8,512]{2,1,0:T(8,128)S(1)}) custom-call(f32[8,8,512]{2,1,0:T(8,128)} %u.1, f32[8,8,512]{2,1,0:T(8,128)} %f.1, bf16[8,8,512]{2,1,0:T(8,128)(2,1)} %a.1, bf16[8,8,512]{2,1,0:T(8,128)(2,1)} %bx.1, ...), custom_call_target="tpu_custom_call" | custom-call | flops 1000000 | bytes 2000000 | tf_op jit(solution)/shard_map/pallas_call | solution.py:24
  2.0 4.9 %collective-permute-start.2 = (f32[24,8,512]{2,1,0:T(8,128)S(1)}, f32[24,8,512]{2,1,0:T(8,128)S(1)}, u32[]{:S(2)}, u32[]{:S(2)}) collective-permute-start(f32[24,8,512]{2,1,0:T(8,128)S(1)} %get-tuple-element.19), channel_id=1, source_target_pairs={{0,1},{1,2},{2,3},{3,4},{4,5},{5,6},{6,7},{7,8},{8,9},{9,10},{10,1... | collective-permute-start | bytes 1179656 | tf_op jit(solution)/shard_map/ppermute | solution.py:424
  6.9 13.8 %collective-permute-start.3 = (f32[24,8,512]{2,1,0:T(8,128)S(1)}, f32[24,8,512]{2,1,0:T(8,128)S(1)}, u32[]{:S(2)}, u32[]{:S(2)}) collective-permute-start(f32[24,8,512]{2,1,0:T(8,128)S(1)} %get-tuple-element.20), channel_id=1, source_target_pairs={{1,0},{2,1},{3,2},{4,3},{5,4},{6,5},{7,6},{8,7},{9,8},{10,9},{11,1... | collective-permute-start | bytes 1179656 | tf_op jit(solution)/shard_map/ppermute | solution.py:424
  20.7 3.3 %collective-permute-start.1 = (f32[24,8,512]{2,1,0:T(8,128)S(1)}, f32[24,8,512]{2,1,0:T(8,128)S(1)}, u32[]{:S(2)}, u32[]{:S(2)}) collective-permute-start(f32[24,8,512]{2,1,0:T(8,128)S(1)} %get-tuple-element.18), channel_id=1, source_target_pairs={{0,64},{64,128},{128,192},{192,256},{256,320},{320,384},{384,448},... | collective-permute-start | bytes 1179656 | tf_op jit(solution)/shard_map/ppermute | solution.py:441
  24.0 0.0 collective-permute-start
  24.0 3.6 %collective-permute-done.2.yhr = f32[24,8,512]{2,1,0:T(8,128)S(1)} collective-permute-done((f32[24,8,512]{2,1,0:T(8,128)S(1)}, f32[24,8,512]{2,1,0:T(8,128)S(1)}, u32[]{:S(2)}, u32[]{:S(2)}) %collective-permute-start.2) | collective-permute-done | bytes 393248 | tf_op jit(solution)/shard_map/ppermute | solution.py:424
  27.6 0.9 collective-permute-done.3.ylr
  28.5 1.6 %collective-permute-start.4 = (f32[16,8,512]{2,1,0:T(8,128)S(1)}, f32[16,8,512]{2,1,0:T(8,128)S(1)}, u32[]{:S(2)}, u32[]{:S(2)}) collective-permute-start(f32[16,8,512]{2,1,0:T(8,128)S(1)} %get-tuple-element.21), channel_id=1, source_target_pairs={{0,960},{64,0},{128,64},{192,128},{256,192},{320,256},{384,320},{4... | collective-permute-start | bytes 786440 | tf_op jit(solution)/shard_map/ppermute | solution.py:441
  30.1 2.3 %collective-permute-start.5 = (f32[16,8,512]{2,1,0:T(8,128)S(1)}, f32[16,8,512]{2,1,0:T(8,128)S(1)}, u32[]{:S(2)}, u32[]{:S(2)}) collective-permute-start(f32[16,8,512]{2,1,0:T(8,128)S(1)} %get-tuple-element.22), channel_id=1, source_target_pairs={{0,64},{64,128},{128,192},{192,256},{256,320},{320,384},{384,448},... | collective-permute-start | bytes 786440 | tf_op jit(solution)/shard_map/ppermute | solution.py:441
  32.4 0.0 collective-permute-done.1.xhr
  32.4 0.5 shard_map.87
  33.0 0.0 collective-permute-done.xlr
  33.0 3.5 %collective-permute-done.4.xclr = f32[16,8,512]{2,1,0:T(8,128)S(1)} collective-permute-done((f32[16,8,512]{2,1,0:T(8,128)S(1)}, f32[16,8,512]{2,1,0:T(8,128)S(1)}, u32[]{:S(2)}, u32[]{:S(2)}) %collective-permute-start.4) | collective-permute-done | bytes 262176 | tf_op jit(solution)/shard_map/ppermute | solution.py:441
  36.4 0.0 collective-permute-done.5.xchr
  36.4 2.2 %shard_map.88 = (f32[8,8,512]{2,1,0:T(8,128)}, f32[5,16,256]{2,1,0:T(8,128)S(1)}) custom-call(f32[48,8,512]{2,1,0:T(8,128)S(1)} %get-tuple-element.16.own, f32[24,8,512]{2,1,0:T(8,128)S(1)} %collective-permute-done.xlr, f32[24,8,512]{2,1,0:T(8,128)S(1)} %collective-permute-done.1.xhr, f32[24,8,512]{2,1,0:T(8,128)S(1)} %collective-permute-done.2.yhr, ...), custom_call_target="tpu_custom_call" | custom-call | flops 20000000 | bytes 20000000 | tf_op jit(solution)/shard_map/pallas_call | solution.py:24
  38.7 1.9 %collective-permute-start.6 = (f32[5,16,256]{2,1,0:T(8,128)S(1)}, f32[5,16,256]{2,1,0:T(8,128)S(1)}, u32[]{:S(2)}, u32[]{:S(2)}) collective-permute-start(f32[5,16,256]{2,1,0:T(8,128)S(1)} %get-tuple-element.25), channel_id=1, source_target_pairs={{0,1},{2,3},{4,5},{6,7},{8,9},{10,11},{12,13},{14,15},{16,17},{18,... | collective-permute-start | bytes 245768 | tf_op jit(solution)/shard_map/ppermute | solution.py:430
  40.6 7.4 %collective-permute-start.7 = (f32[5,16,256]{2,1,0:T(8,128)S(1)}, f32[5,16,256]{2,1,0:T(8,128)S(1)}, u32[]{:S(2)}, u32[]{:S(2)}) collective-permute-start(f32[5,16,256]{2,1,0:T(8,128)S(1)} %get-tuple-element.25), channel_id=1, source_target_pairs={{1,2},{3,4},{5,6},{7,8},{9,10},{11,12},{13,14},{15,16},{17,18},{19... | collective-permute-start | bytes 245768 | tf_op jit(solution)/shard_map/ppermute | solution.py:430
  48.0 0.0 collective-permute-done.6
  48.0 2.3 %collective-permute-done.7 = f32[5,16,256]{2,1,0:T(8,128)S(1)} collective-permute-done((f32[5,16,256]{2,1,0:T(8,128)S(1)}, f32[5,16,256]{2,1,0:T(8,128)S(1)}, u32[]{:S(2)}, u32[]{:S(2)}) %collective-permute-start.7) | collective-permute-done | bytes 81952 | tf_op jit(solution)/shard_map/ppermute | solution.py:430
  50.4 3.3 %collective-permute-start.8 = (f32[3,5,16,256]{3,2,1,0:T(8,128)S(1)}, f32[3,5,16,256]{3,2,1,0:T(8,128)S(1)}, u32[]{:S(2)}, u32[]{:S(2)}) collective-permute-start(f32[3,5,16,256]{3,2,1,0:T(8,128)S(1)} %pad_maximum_fusion.here), channel_id=1, source_target_pairs={{0,64},{64,128},{128,192},{192,256},{256,320},{320,384},{384,448},... | collective-permute-start | bytes 737288 | tf_op jit(solution)/shard_map/ppermute | solution.py:441
  53.7 0.0 collective-permute-start.9
  53.7 3.1 %collective-permute-done.8.left = f32[3,5,16,256]{3,2,1,0:T(8,128)S(1)} collective-permute-done((f32[3,5,16,256]{3,2,1,0:T(8,128)S(1)}, f32[3,5,16,256]{3,2,1,0:T(8,128)S(1)}, u32[]{:S(2)}, u32[]{:S(2)}) %collective-permute-start.8) | collective-permute-done | bytes 245792 | tf_op jit(solution)/shard_map/ppermute | solution.py:441
  56.9 3.7 %collective-permute-done.9.right = f32[3,5,16,256]{3,2,1,0:T(8,128)S(1)} collective-permute-done((f32[3,5,16,256]{3,2,1,0:T(8,128)S(1)}, f32[3,5,16,256]{3,2,1,0:T(8,128)S(1)}, u32[]{:S(2)}, u32[]{:S(2)}) %collective-permute-start.9) | collective-permute-done | bytes 245792 | tf_op jit(solution)/shard_map/ppermute | solution.py:441
  60.6 1.1 %shard_map.89 = (f32[4,4,256]{2,1,0:T(4,128)}, f32[20,128]{1,0:T(8,128)S(1)}) custom-call(f32[3,5,16,256]{3,2,1,0:T(8,128)S(1)} %collective-permute-done.8.left, f32[3,5,16,256]{3,2,1,0:T(8,128)S(1)} %pad_maximum_fusion.here, f32[3,5,16,256]{3,2,1,0:T(8,128)S(1)} %collective-permute-done.9.right, f32[16,128]{1,0:T(8,128)S(1)} %get-tuple-element.26.c2), custom_call_target="tpu_custom_call" | custom-call | flops 1000000 | bytes 2000000 | tf_op jit(solution)/shard_map/pallas_call | solution.py:24
  61.6 7.0 %collective-permute-start.10 = (f32[20,128]{1,0:T(8,128)S(1)}, f32[20,128]{1,0:T(8,128)S(1)}, u32[]{:S(2)}, u32[]{:S(2)}) collective-permute-start(f32[20,128]{1,0:T(8,128)S(1)} %get-tuple-element.28), channel_id=1, source_target_pairs={{1,2},{3,4},{5,6},{7,8},{9,10},{11,12},{13,14},{15,16},{17,18},{19... | collective-permute-start | bytes 30728 | tf_op jit(solution)/shard_map/ppermute | solution.py:430
  68.6 1.9 %collective-permute-start.11 = (f32[20,128]{1,0:T(8,128)S(1)}, f32[20,128]{1,0:T(8,128)S(1)}, u32[]{:S(2)}, u32[]{:S(2)}) collective-permute-start(f32[20,128]{1,0:T(8,128)S(1)} %get-tuple-element.28), channel_id=1, source_target_pairs={{0,1},{2,3},{4,5},{6,7},{8,9},{10,11},{12,13},{14,15},{16,17},{18,... | collective-permute-start | bytes 30728 | tf_op jit(solution)/shard_map/ppermute | solution.py:430
  70.5 0.0 collective-permute-start.14
  70.5 2.9 %collective-permute-start.12 = (f32[20,128]{1,0:T(8,128)S(1)}, f32[20,128]{1,0:T(8,128)S(1)}, u32[]{:S(2)}, u32[]{:S(2)}) collective-permute-start(f32[20,128]{1,0:T(8,128)S(1)} %get-tuple-element.28), channel_id=1, source_target_pairs={{0,64},{64,128},{128,192},{192,256},{256,320},{320,384},{384,448},... | collective-permute-start | bytes 30728 | tf_op jit(solution)/shard_map/ppermute | solution.py:441
  73.5 1.9 %collective-permute-start.16 = (f32[20,128]{1,0:T(8,128)S(1)}, f32[20,128]{1,0:T(8,128)S(1)}, u32[]{:S(2)}, u32[]{:S(2)}) collective-permute-start(f32[20,128]{1,0:T(8,128)S(1)} %get-tuple-element.28), channel_id=1, source_target_pairs={{0,2},{1,3},{2,4},{3,5},{4,6},{5,7},{6,8},{7,9},{8,10},{9,11},{10,... | collective-permute-start | bytes 30728 | tf_op jit(solution)/shard_map/ppermute | solution.py:424
  75.4 0.0 collective-permute-done.10
  75.4 7.6 %collective-permute-start.17 = (f32[20,128]{1,0:T(8,128)S(1)}, f32[20,128]{1,0:T(8,128)S(1)}, u32[]{:S(2)}, u32[]{:S(2)}) collective-permute-start(f32[20,128]{1,0:T(8,128)S(1)} %get-tuple-element.28), channel_id=1, source_target_pairs={{2,0},{3,1},{4,2},{5,3},{6,4},{7,5},{8,6},{9,7},{10,8},{11,9},{12,... | collective-permute-start | bytes 30728 | tf_op jit(solution)/shard_map/ppermute | solution.py:424
  83.0 0.0 collective-permute-done.11
  83.0 0.0 collective-permute-done.14
  83.0 0.0 collective-permute-done.12
  83.1 0.6 collective-permute-start.13
  83.6 0.0 collective-permute-start.15
  83.6 0.0 collective-permute-done.16.down
  83.7 0.1 collective-permute-done.17.up
  83.8 1.0 %collective-permute-done.13.left = f32[4,20,128]{2,1,0:T(8,128)S(1)} collective-permute-done((f32[4,20,128]{2,1,0:T(8,128)S(1)}, f32[4,20,128]{2,1,0:T(8,128)S(1)}, u32[]{:S(2)}, u32[]{:S(2)}) %collective-permute-start.13) | collective-permute-done | bytes 40992 | tf_op jit(solution)/shard_map/ppermute | solution.py:441
  84.8 3.5 %collective-permute-done.15.right = f32[4,20,128]{2,1,0:T(8,128)S(1)} collective-permute-done((f32[4,20,128]{2,1,0:T(8,128)S(1)}, f32[4,20,128]{2,1,0:T(8,128)S(1)}, u32[]{:S(2)}, u32[]{:S(2)}) %collective-permute-start.15) | collective-permute-done | bytes 40992 | tf_op jit(solution)/shard_map/ppermute | solution.py:441
  88.4 0.9 shard_map.90
  (6 shorter events, 0.1 us)
Async XLA Ops:
  2.0 25.6 %collective-permute-start.2 = (f32[24,8,512]{2,1,0:T(8,128)S(1)}, f32[24,8,512]{2,1,0:T(8,128)S(1)}, u32[]{:S(2)}, u32[]{:S(2)}) collective-permute-start(f32[24,8,512]{2,1,0:T(8,128)S(1)} %get-tuple-element.19), channel_id=1, source_target_pairs={{0,1},{1,2},{2,3},{3,4},{4,5},{5,6},{6,7},{7,8},{8,9},{9,10},{10,1... | collective-permute-start | bytes 1179656 | tf_op jit(solution)/shard_map/ppermute | solution.py:424
  6.9 21.6 %collective-permute-start.3 = (f32[24,8,512]{2,1,0:T(8,128)S(1)}, f32[24,8,512]{2,1,0:T(8,128)S(1)}, u32[]{:S(2)}, u32[]{:S(2)}) collective-permute-start(f32[24,8,512]{2,1,0:T(8,128)S(1)} %get-tuple-element.20), channel_id=1, source_target_pairs={{1,0},{2,1},{3,2},{4,3},{5,4},{6,5},{7,6},{8,7},{9,8},{10,9},{11,1... | collective-permute-start | bytes 1179656 | tf_op jit(solution)/shard_map/ppermute | solution.py:424
  20.7 11.7 %collective-permute-start.1 = (f32[24,8,512]{2,1,0:T(8,128)S(1)}, f32[24,8,512]{2,1,0:T(8,128)S(1)}, u32[]{:S(2)}, u32[]{:S(2)}) collective-permute-start(f32[24,8,512]{2,1,0:T(8,128)S(1)} %get-tuple-element.18), channel_id=1, source_target_pairs={{0,64},{64,128},{128,192},{192,256},{256,320},{320,384},{384,448},... | collective-permute-start | bytes 1179656 | tf_op jit(solution)/shard_map/ppermute | solution.py:441
  24.0 9.0 %collective-permute-start = (f32[24,8,512]{2,1,0:T(8,128)S(1)}, f32[24,8,512]{2,1,0:T(8,128)S(1)}, u32[]{:S(2)}, u32[]{:S(2)}) collective-permute-start(f32[24,8,512]{2,1,0:T(8,128)S(1)} %get-tuple-element.17), channel_id=1, source_target_pairs={{0,960},{64,0},{128,64},{192,128},{256,192},{320,256},{384,320},{4... | collective-permute-start | bytes 1179656 | tf_op jit(solution)/shard_map/ppermute | solution.py:441
  28.5 7.9 %collective-permute-start.4 = (f32[16,8,512]{2,1,0:T(8,128)S(1)}, f32[16,8,512]{2,1,0:T(8,128)S(1)}, u32[]{:S(2)}, u32[]{:S(2)}) collective-permute-start(f32[16,8,512]{2,1,0:T(8,128)S(1)} %get-tuple-element.21), channel_id=1, source_target_pairs={{0,960},{64,0},{128,64},{192,128},{256,192},{320,256},{384,320},{4... | collective-permute-start | bytes 786440 | tf_op jit(solution)/shard_map/ppermute | solution.py:441
  30.1 6.4 %collective-permute-start.5 = (f32[16,8,512]{2,1,0:T(8,128)S(1)}, f32[16,8,512]{2,1,0:T(8,128)S(1)}, u32[]{:S(2)}, u32[]{:S(2)}) collective-permute-start(f32[16,8,512]{2,1,0:T(8,128)S(1)} %get-tuple-element.22), channel_id=1, source_target_pairs={{0,64},{64,128},{128,192},{192,256},{256,320},{320,384},{384,448},... | collective-permute-start | bytes 786440 | tf_op jit(solution)/shard_map/ppermute | solution.py:441
  38.7 9.4 %collective-permute-start.6 = (f32[5,16,256]{2,1,0:T(8,128)S(1)}, f32[5,16,256]{2,1,0:T(8,128)S(1)}, u32[]{:S(2)}, u32[]{:S(2)}) collective-permute-start(f32[5,16,256]{2,1,0:T(8,128)S(1)} %get-tuple-element.25), channel_id=1, source_target_pairs={{0,1},{2,3},{4,5},{6,7},{8,9},{10,11},{12,13},{14,15},{16,17},{18,... | collective-permute-start | bytes 245768 | tf_op jit(solution)/shard_map/ppermute | solution.py:430
  40.6 9.8 %collective-permute-start.7 = (f32[5,16,256]{2,1,0:T(8,128)S(1)}, f32[5,16,256]{2,1,0:T(8,128)S(1)}, u32[]{:S(2)}, u32[]{:S(2)}) collective-permute-start(f32[5,16,256]{2,1,0:T(8,128)S(1)} %get-tuple-element.25), channel_id=1, source_target_pairs={{1,2},{3,4},{5,6},{7,8},{9,10},{11,12},{13,14},{15,16},{17,18},{19... | collective-permute-start | bytes 245768 | tf_op jit(solution)/shard_map/ppermute | solution.py:430
  50.4 6.5 %collective-permute-start.8 = (f32[3,5,16,256]{3,2,1,0:T(8,128)S(1)}, f32[3,5,16,256]{3,2,1,0:T(8,128)S(1)}, u32[]{:S(2)}, u32[]{:S(2)}) collective-permute-start(f32[3,5,16,256]{3,2,1,0:T(8,128)S(1)} %pad_maximum_fusion.here), channel_id=1, source_target_pairs={{0,64},{64,128},{128,192},{192,256},{256,320},{320,384},{384,448},... | collective-permute-start | bytes 737288 | tf_op jit(solution)/shard_map/ppermute | solution.py:441
  53.7 6.8 %collective-permute-start.9 = (f32[3,5,16,256]{3,2,1,0:T(8,128)S(1)}, f32[3,5,16,256]{3,2,1,0:T(8,128)S(1)}, u32[]{:S(2)}, u32[]{:S(2)}) collective-permute-start(f32[3,5,16,256]{3,2,1,0:T(8,128)S(1)} %pad_maximum_fusion.here), channel_id=1, source_target_pairs={{0,960},{64,0},{128,64},{192,128},{256,192},{320,256},{384,320},{4... | collective-permute-start | bytes 737288 | tf_op jit(solution)/shard_map/ppermute | solution.py:441
  61.6 13.8 %collective-permute-start.10 = (f32[20,128]{1,0:T(8,128)S(1)}, f32[20,128]{1,0:T(8,128)S(1)}, u32[]{:S(2)}, u32[]{:S(2)}) collective-permute-start(f32[20,128]{1,0:T(8,128)S(1)} %get-tuple-element.28), channel_id=1, source_target_pairs={{1,2},{3,4},{5,6},{7,8},{9,10},{11,12},{13,14},{15,16},{17,18},{19... | collective-permute-start | bytes 30728 | tf_op jit(solution)/shard_map/ppermute | solution.py:430
  68.6 14.4 %collective-permute-start.11 = (f32[20,128]{1,0:T(8,128)S(1)}, f32[20,128]{1,0:T(8,128)S(1)}, u32[]{:S(2)}, u32[]{:S(2)}) collective-permute-start(f32[20,128]{1,0:T(8,128)S(1)} %get-tuple-element.28), channel_id=1, source_target_pairs={{0,1},{2,3},{4,5},{6,7},{8,9},{10,11},{12,13},{14,15},{16,17},{18,... | collective-permute-start | bytes 30728 | tf_op jit(solution)/shard_map/ppermute | solution.py:430
  70.5 12.5 %collective-permute-start.14 = (f32[20,128]{1,0:T(8,128)S(1)}, f32[20,128]{1,0:T(8,128)S(1)}, u32[]{:S(2)}, u32[]{:S(2)}) collective-permute-start(f32[20,128]{1,0:T(8,128)S(1)} %get-tuple-element.28), channel_id=1, source_target_pairs={{0,960},{64,0},{128,64},{192,128},{256,192},{320,256},{384,320},{4... | collective-permute-start | bytes 30728 | tf_op jit(solution)/shard_map/ppermute | solution.py:441
  70.5 12.5 %collective-permute-start.12 = (f32[20,128]{1,0:T(8,128)S(1)}, f32[20,128]{1,0:T(8,128)S(1)}, u32[]{:S(2)}, u32[]{:S(2)}) collective-permute-start(f32[20,128]{1,0:T(8,128)S(1)} %get-tuple-element.28), channel_id=1, source_target_pairs={{0,64},{64,128},{128,192},{192,256},{256,320},{320,384},{384,448},... | collective-permute-start | bytes 30728 | tf_op jit(solution)/shard_map/ppermute | solution.py:441
  73.5 10.2 %collective-permute-start.16 = (f32[20,128]{1,0:T(8,128)S(1)}, f32[20,128]{1,0:T(8,128)S(1)}, u32[]{:S(2)}, u32[]{:S(2)}) collective-permute-start(f32[20,128]{1,0:T(8,128)S(1)} %get-tuple-element.28), channel_id=1, source_target_pairs={{0,2},{1,3},{2,4},{3,5},{4,6},{5,7},{6,8},{7,9},{8,10},{9,11},{10,... | collective-permute-start | bytes 30728 | tf_op jit(solution)/shard_map/ppermute | solution.py:424
  75.4 8.4 %collective-permute-start.17 = (f32[20,128]{1,0:T(8,128)S(1)}, f32[20,128]{1,0:T(8,128)S(1)}, u32[]{:S(2)}, u32[]{:S(2)}) collective-permute-start(f32[20,128]{1,0:T(8,128)S(1)} %get-tuple-element.28), channel_id=1, source_target_pairs={{2,0},{3,1},{4,2},{5,3},{6,4},{7,5},{8,6},{9,7},{10,8},{11,9},{12,... | collective-permute-start | bytes 30728 | tf_op jit(solution)/shard_map/ppermute | solution.py:424
  83.1 1.8 %collective-permute-start.13 = (f32[4,20,128]{2,1,0:T(8,128)S(1)}, f32[4,20,128]{2,1,0:T(8,128)S(1)}, u32[]{:S(2)}, u32[]{:S(2)}) collective-permute-start(f32[4,20,128]{2,1,0:T(8,128)S(1)} %get-tuple-element.32), channel_id=1, source_target_pairs={{0,64},{64,128},{128,192},{192,256},{256,320},{320,384},{384,448},... | collective-permute-start | bytes 122888 | tf_op jit(solution)/shard_map/ppermute | solution.py:441
  83.6 4.7 %collective-permute-start.15 = (f32[4,20,128]{2,1,0:T(8,128)S(1)}, f32[4,20,128]{2,1,0:T(8,128)S(1)}, u32[]{:S(2)}, u32[]{:S(2)}) collective-permute-start(f32[4,20,128]{2,1,0:T(8,128)S(1)} %get-tuple-element.31), channel_id=1, source_target_pairs={{0,960},{64,0},{128,64},{192,128},{256,192},{320,256},{384,320},{4... | collective-permute-start | bytes 122888 | tf_op jit(solution)/shard_map/ppermute | solution.py:441

commit v8 on v7

--- a/solution.py
+++ b/solution.py
@@ -391,17 +391,20 @@
     p2[4:20] = c2[...]
 
 
-def coarse_level_body(count, left, mid, right, down, up, out, win, weights, held):
+def coarse_level_body(count, left, mid, right, other, last, out, win, weights, held):
     win[...] = jnp.zeros(win.shape, F32)
     near = beside(count)
+    even = jnp.where(lax.axis_index("gy") % 2 == 0, 1.0, 0.0)
+    odd = 1.0 - even
     for k in range(5):
         factor = near if k == 1 else [1.0] * 4
         win[k, 1, 3:5] = left[3, 4 * k + 2 : 4 * k + 4] * factor[2]
         win[k, 8, 3:5] = right[3, 4 * k : 4 * k + 2] * factor[3]
         for i in range(2):
             at = 4 * k + 2 * i
-            win[k, 4 + i, 0:1] = down[at + 1 : at + 2]
-            win[k, 4 + i, 7:8] = up[at : at + 1]
+            far, passed = other[1, at : at + 2], last[at : at + 2]
+            win[k, 4 + i, 0:1] = (far * even + passed * odd)[1:2]
+            win[k, 4 + i, 7:8] = (passed * even + far * odd)[0:1]
             for b, (source, there) in enumerate(((left, factor[0]), (mid, 1.0), (right, factor[1]))):
                 for j in range(3):
                     win[k, 2 + 2 * b + i, 1 + 2 * j : 3 + 2 * j] = source[j, at : at + 2] * there
@@ -500,15 +503,19 @@
             pltpu.VMEM((nz // 256, 16, 128), F32),
         ],
     )
+    one = swapped(p2, False)
     before, after = round_x(p2, 1), round_x(p2, -1)
-    below, above = both_sides(p2)
-    down, up = along_y(p2, 2), along_y(p2, -2)
+    one, before, after = lax.optimization_barrier((one, before, after))
+    other = swapped(jnp.stack([p2, one]), True)
+    last = swapped(other[0], False)
+    first = lax.axis_index("gy") % 2 == 0
+    below, above = jnp.where(first, other[0], one), jnp.where(first, one, other[0])
     left = round_x(jnp.stack([below, p2, above, before]), 1)
     right = round_x(jnp.stack([below, p2, above, after]), -1)
     coarse = call(
         functools.partial(coarse_level_body, count),
         shape(2, 2, nz // 4),
-        (left, jnp.stack([below, p2, above]), right, down, up),
+        (left, jnp.stack([below, p2, above]), right, other, last),
         [
             pltpu.VMEM((5, 9, 8, nz // 4), F32),
             pltpu.VMEM((7, 8, 8, nz // 4), F32),

time: 89.6 us -> 85.1 us (0.950)
  the two profiles are of different devices: /device:TPU:71 before, /device:TPU:64 now
where the time goes in v8:
time: 85.1 us; the launch traced here: 84.8 us
  starting transfers between devices  53 us (62%)
  waiting for transfers between devices  24.9 us (29%)
  Pallas kernels  6.06 us (7%)
    ppermute x5, starting transfers between devices, swapped(): lax.ppermute(block, 'gy', [(i, i + 1) for i in firsts] + [(i + 1, i) for...  20.7 us
    ppermute x2, starting transfers between devices, along_y(): lax.ppermute(block, 'gy', [(i, i + by) for i in range(count) if 0 <= i +...  19 us
    ppermute x10, starting transfers between devices, round_x(): lax.ppermute(block, 'gx', [(i, (i + by) % count) for i in range(count)])  13.3 us
    ppermute x10, waiting for transfers between devices, round_x(): lax.ppermute(block, 'gx', [(i, (i + by) % count) for i in range(count)])  11.1 us
    ppermute x5, waiting for transfers between devices, swapped(): lax.ppermute(block, 'gy', [(i, i + 1) for i in firsts] + [(i + 1, i) for...  8.49 us
    pallas_call x6, Pallas kernels, call(): pl.pallas_call(body, out_shape=outs, in_specs=[pl.BlockSpec(memory_space=...  6.06 us
    ppermute x2, waiting for transfers between devices, along_y(): lax.ppermute(block, 'gy', [(i, i + by) for i in range(count) if 0 <= i +...  5.38 us
  transfers between devices with their start and end apart: 17, of which 10 were waited for; matrix products, arithmetic and copies ran while one was open for 0% of the time, Pallas kernels for 1%

profile of v8, /device:TPU:64, one launch (start us, length us, event | category | flops | bytes accessed | tf_op | source)
XLA Modules:
  0.0 84.8 jit_solution(9200937949951014769)
XLA Ops:
  0.6 1.3 %shard_map.85 = (f32[48,8,512]{2,1,0:T(8,128)S(1)}, f32[24,8,512]{2,1,0:T(8,128)S(1)}, f32[24,8,512]{2,1,0:T(8,128)S(1)}, f32[24,8,512]{2,1,0:T(8,128)S(1)}, f32[24,8,512]{2,1,0:T(8,128)S(1)}) custom-call(f32[8,8,512]{2,1,0:T(8,128)} %u.1, f32[8,8,512]{2,1,0:T(8,128)} %f.1, bf16[8,8,512]{2,1,0:T(8,128)(2,1)} %a.1, bf16[8,8,512]{2,1,0:T(8,128)(2,1)} %bx.1, ...), custom_call_target="tpu_custom_call" | custom-call | flops 1000000 | bytes 2000000 | tf_op jit(solution)/shard_map/pallas_call | solution.py:24
  2.0 5.2 %collective-permute-start.2 = (f32[24,8,512]{2,1,0:T(8,128)S(1)}, f32[24,8,512]{2,1,0:T(8,128)S(1)}, u32[]{:S(2)}, u32[]{:S(2)}) collective-permute-start(f32[24,8,512]{2,1,0:T(8,128)S(1)} %get-tuple-element.22), channel_id=1, source_target_pairs={{0,1},{1,2},{2,3},{3,4},{4,5},{5,6},{6,7},{7,8},{8,9},{9,10},{10,1... | collective-permute-start | bytes 1179656 | tf_op jit(solution)/shard_map/ppermute | solution.py:427
  7.2 13.8 %collective-permute-start.3 = (f32[24,8,512]{2,1,0:T(8,128)S(1)}, f32[24,8,512]{2,1,0:T(8,128)S(1)}, u32[]{:S(2)}, u32[]{:S(2)}) collective-permute-start(f32[24,8,512]{2,1,0:T(8,128)S(1)} %get-tuple-element.23), channel_id=1, source_target_pairs={{1,0},{2,1},{3,2},{4,3},{5,4},{6,5},{7,6},{8,7},{9,8},{10,9},{11,1... | collective-permute-start | bytes 1179656 | tf_op jit(solution)/shard_map/ppermute | solution.py:427
  21.0 0.0 collective-permute-start.1
  21.0 2.9 %collective-permute-start = (f32[24,8,512]{2,1,0:T(8,128)S(1)}, f32[24,8,512]{2,1,0:T(8,128)S(1)}, u32[]{:S(2)}, u32[]{:S(2)}) collective-permute-start(f32[24,8,512]{2,1,0:T(8,128)S(1)} %get-tuple-element.20), channel_id=1, source_target_pairs={{0,960},{64,0},{128,64},{192,128},{256,192},{320,256},{384,320},{4... | collective-permute-start | bytes 1179656 | tf_op jit(solution)/shard_map/ppermute | solution.py:444
  23.9 4.2 %collective-permute-done.2.yhr = f32[24,8,512]{2,1,0:T(8,128)S(1)} collective-permute-done((f32[24,8,512]{2,1,0:T(8,128)S(1)}, f32[24,8,512]{2,1,0:T(8,128)S(1)}, u32[]{:S(2)}, u32[]{:S(2)}) %collective-permute-start.2) | collective-permute-done | bytes 393248 | tf_op jit(solution)/shard_map/ppermute | solution.py:427
  28.2 1.2 %collective-permute-done.3.ylr = f32[24,8,512]{2,1,0:T(8,128)S(1)} collective-permute-done((f32[24,8,512]{2,1,0:T(8,128)S(1)}, f32[24,8,512]{2,1,0:T(8,128)S(1)}, u32[]{:S(2)}, u32[]{:S(2)}) %collective-permute-start.3) | collective-permute-done | bytes 393248 | tf_op jit(solution)/shard_map/ppermute | solution.py:427
  29.4 1.5 %collective-permute-start.4 = (f32[16,8,512]{2,1,0:T(8,128)S(1)}, f32[16,8,512]{2,1,0:T(8,128)S(1)}, u32[]{:S(2)}, u32[]{:S(2)}) collective-permute-start(f32[16,8,512]{2,1,0:T(8,128)S(1)} %get-tuple-element.24), channel_id=1, source_target_pairs={{0,960},{64,0},{128,64},{192,128},{256,192},{320,256},{384,320},{4... | collective-permute-start | bytes 786440 | tf_op jit(solution)/shard_map/ppermute | solution.py:444
  30.8 0.0 collective-permute-start.5
  30.8 0.0 collective-permute-done.1.xhr
  30.8 0.5 shard_map.87
  31.4 0.0 collective-permute-done.xlr
  31.4 3.3 %collective-permute-done.4.xclr = f32[16,8,512]{2,1,0:T(8,128)S(1)} collective-permute-done((f32[16,8,512]{2,1,0:T(8,128)S(1)}, f32[16,8,512]{2,1,0:T(8,128)S(1)}, u32[]{:S(2)}, u32[]{:S(2)}) %collective-permute-start.4) | collective-permute-done | bytes 262176 | tf_op jit(solution)/shard_map/ppermute | solution.py:444
  34.7 3.1 %collective-permute-done.5.xchr = f32[16,8,512]{2,1,0:T(8,128)S(1)} collective-permute-done((f32[16,8,512]{2,1,0:T(8,128)S(1)}, f32[16,8,512]{2,1,0:T(8,128)S(1)}, u32[]{:S(2)}, u32[]{:S(2)}) %collective-permute-start.5) | collective-permute-done | bytes 262176 | tf_op jit(solution)/shard_map/ppermute | solution.py:444
  37.8 2.2 %shard_map.88 = (f32[8,8,512]{2,1,0:T(8,128)}, f32[5,16,256]{2,1,0:T(8,128)S(1)}) custom-call(f32[48,8,512]{2,1,0:T(8,128)S(1)} %get-tuple-element.19.own, f32[24,8,512]{2,1,0:T(8,128)S(1)} %collective-permute-done.xlr, f32[24,8,512]{2,1,0:T(8,128)S(1)} %collective-permute-done.1.xhr, f32[24,8,512]{2,1,0:T(8,128)S(1)} %collective-permute-done.2.yhr, ...), custom_call_target="tpu_custom_call" | custom-call | flops 20000000 | bytes 20000000 | tf_op jit(solution)/shard_map/pallas_call | solution.py:24
  40.1 1.9 %collective-permute-start.6 = (f32[5,16,256]{2,1,0:T(8,128)S(1)}, f32[5,16,256]{2,1,0:T(8,128)S(1)}, u32[]{:S(2)}, u32[]{:S(2)}) collective-permute-start(f32[5,16,256]{2,1,0:T(8,128)S(1)} %get-tuple-element.28), channel_id=1, source_target_pairs={{0,1},{2,3},{4,5},{6,7},{8,9},{10,11},{12,13},{14,15},{16,17},{18,... | collective-permute-start | bytes 245768 | tf_op jit(solution)/shard_map/ppermute | solution.py:433
  42.0 7.7 %collective-permute-start.7 = (f32[5,16,256]{2,1,0:T(8,128)S(1)}, f32[5,16,256]{2,1,0:T(8,128)S(1)}, u32[]{:S(2)}, u32[]{:S(2)}) collective-permute-start(f32[5,16,256]{2,1,0:T(8,128)S(1)} %get-tuple-element.28), channel_id=1, source_target_pairs={{1,2},{3,4},{5,6},{7,8},{9,10},{11,12},{13,14},{15,16},{17,18},{19... | collective-permute-start | bytes 245768 | tf_op jit(solution)/shard_map/ppermute | solution.py:433
  49.7 0.0 collective-permute-done.6
  49.7 2.4 %collective-permute-done.7 = f32[5,16,256]{2,1,0:T(8,128)S(1)} collective-permute-done((f32[5,16,256]{2,1,0:T(8,128)S(1)}, f32[5,16,256]{2,1,0:T(8,128)S(1)}, u32[]{:S(2)}, u32[]{:S(2)}) %collective-permute-start.7) | collective-permute-done | bytes 81952 | tf_op jit(solution)/shard_map/ppermute | solution.py:433
  52.1 0.0 collective-permute-start.8
  52.2 2.9 %collective-permute-start.9 = (f32[3,5,16,256]{3,2,1,0:T(8,128)S(1)}, f32[3,5,16,256]{3,2,1,0:T(8,128)S(1)}, u32[]{:S(2)}, u32[]{:S(2)}) collective-permute-start(f32[3,5,16,256]{3,2,1,0:T(8,128)S(1)} %pad_maximum_fusion.here), channel_id=1, source_target_pairs={{0,960},{64,0},{128,64},{192,128},{256,192},{320,256},{384,320},{4... | collective-permute-start | bytes 737288 | tf_op jit(solution)/shard_map/ppermute | solution.py:444
  55.1 3.9 %collective-permute-done.8.left = f32[3,5,16,256]{3,2,1,0:T(8,128)S(1)} collective-permute-done((f32[3,5,16,256]{3,2,1,0:T(8,128)S(1)}, f32[3,5,16,256]{3,2,1,0:T(8,128)S(1)}, u32[]{:S(2)}, u32[]{:S(2)}) %collective-permute-start.8) | collective-permute-done | bytes 245792 | tf_op jit(solution)/shard_map/ppermute | solution.py:444
  59.0 0.0 collective-permute-done.9.right
  59.0 1.1 %shard_map.89 = (f32[4,4,256]{2,1,0:T(4,128)}, f32[20,128]{1,0:T(8,128)S(1)}) custom-call(f32[3,5,16,256]{3,2,1,0:T(8,128)S(1)} %collective-permute-done.8.left, f32[3,5,16,256]{3,2,1,0:T(8,128)S(1)} %pad_maximum_fusion.here, f32[3,5,16,256]{3,2,1,0:T(8,128)S(1)} %collective-permute-done.9.right, f32[16,128]{1,0:T(8,128)S(1)} %get-tuple-element.29.c2), custom_call_target="tpu_custom_call" | custom-call | flops 1000000 | bytes 2000000 | tf_op jit(solution)/shard_map/pallas_call | solution.py:24
  60.1 1.9 %collective-permute-start.10 = (f32[20,128]{1,0:T(8,128)S(1)}, f32[20,128]{1,0:T(8,128)S(1)}, u32[]{:S(2)}, u32[]{:S(2)}) collective-permute-start(f32[20,128]{1,0:T(8,128)S(1)} %get-tuple-element.31), channel_id=1, source_target_pairs={{0,1},{2,3},{4,5},{6,7},{8,9},{10,11},{12,13},{14,15},{16,17},{18,... | collective-permute-start | bytes 30728 | tf_op jit(solution)/shard_map/ppermute | solution.py:433
  62.0 0.0 collective-permute-start.11
  62.0 3.0 %collective-permute-start.12 = (f32[20,128]{1,0:T(8,128)S(1)}, f32[20,128]{1,0:T(8,128)S(1)}, u32[]{:S(2)}, u32[]{:S(2)}) collective-permute-start(f32[20,128]{1,0:T(8,128)S(1)} %get-tuple-element.31), channel_id=1, source_target_pairs={{0,960},{64,0},{128,64},{192,128},{256,192},{320,256},{384,320},{4... | collective-permute-start | bytes 30728 | tf_op jit(solution)/shard_map/ppermute | solution.py:444
  65.0 0.7 collective-permute-done.10
  65.6 0.7 collective-permute-done.11
  66.3 0.0 collective-permute-done.12
  66.4 7.2 %collective-permute-start.13 = (f32[2,20,128]{2,1,0:T(8,128)S(1)}, f32[2,20,128]{2,1,0:T(8,128)S(1)}, u32[]{:S(2)}, u32[]{:S(2)}) collective-permute-start(f32[2,20,128]{2,1,0:T(8,128)S(1)} %pad_maximum_fusion.5), channel_id=1, source_target_pairs={{1,2},{3,4},{5,6},{7,8},{9,10},{11,12},{13,14},{15,16},{17,18},{19... | collective-permute-start | bytes 61448 | tf_op jit(solution)/shard_map/ppermute | solution.py:433
  73.6 1.8 %collective-permute-done.13.other = f32[2,20,128]{2,1,0:T(8,128)S(1)} collective-permute-done((f32[2,20,128]{2,1,0:T(8,128)S(1)}, f32[2,20,128]{2,1,0:T(8,128)S(1)}, u32[]{:S(2)}, u32[]{:S(2)}) %collective-permute-start.13) | collective-permute-done | bytes 20512 | tf_op jit(solution)/shard_map/ppermute | solution.py:433
  75.4 0.0 collective-permute-start.14
  75.4 2.9 %collective-permute-start.15 = (f32[4,20,128]{2,1,0:T(8,128)S(1)}, f32[4,20,128]{2,1,0:T(8,128)S(1)}, u32[]{:S(2)}, u32[]{:S(2)}) collective-permute-start(f32[4,20,128]{2,1,0:T(8,128)S(1)} %get-tuple-element.37), channel_id=1, source_target_pairs={{0,960},{64,0},{128,64},{192,128},{256,192},{320,256},{384,320},{4... | collective-permute-start | bytes 122888 | tf_op jit(solution)/shard_map/ppermute | solution.py:444
  78.4 1.9 %collective-permute-start.16 = (f32[20,128]{1,0:T(8,128)S(1)}, f32[20,128]{1,0:T(8,128)S(1)}, u32[]{:S(2)}, u32[]{:S(2)}) collective-permute-start(f32[20,128]{1,0:T(8,128)S(1)} %slice_bitcast_fusion), channel_id=1, source_target_pairs={{0,1},{2,3},{4,5},{6,7},{8,9},{10,11},{12,13},{14,15},{16,17},{18,... | collective-permute-start | bytes 30728 | tf_op jit(solution)/shard_map/ppermute | solution.py:433
  80.3 3.6 %collective-permute-done.16.last = f32[20,128]{1,0:T(8,128)S(1)} collective-permute-done((f32[20,128]{1,0:T(8,128)S(1)}, f32[20,128]{1,0:T(8,128)S(1)}, u32[]{:S(2)}, u32[]{:S(2)}) %collective-permute-start.16) | collective-permute-done | bytes 10272 | tf_op jit(solution)/shard_map/ppermute | solution.py:433
  84.0 0.0 collective-permute-done.14.left
  84.0 0.0 collective-permute-done.15.right
  84.0 0.9 %shard_map.90 = f32[2,2,128]{2,1,0:T(2,128)} custom-call(f32[4,20,128]{2,1,0:T(8,128)S(1)} %collective-permute-done.14.left, f32[3,20,128]{2,1,0:T(8,128)S(1)} %pad_maximum_fusion.4.mid, f32[4,20,128]{2,1,0:T(8,128)S(1)} %collective-permute-done.15.right, f32[2,20,128]{2,1,0:T(8,128)S(1)} %collective-permute-done.13.other, ...), custom_call_target="tpu_custom_call" | custom-call | flops 1000000 | bytes 2000000 | tf_op jit(solution)/shard_map/pallas_call | solution.py:24
  (8 shorter events, 0.1 us)
Async XLA Ops:
  2.0 26.2 %collective-permute-start.2 = (f32[24,8,512]{2,1,0:T(8,128)S(1)}, f32[24,8,512]{2,1,0:T(8,128)S(1)}, u32[]{:S(2)}, u32[]{:S(2)}) collective-permute-start(f32[24,8,512]{2,1,0:T(8,128)S(1)} %get-tuple-element.22), channel_id=1, source_target_pairs={{0,1},{1,2},{2,3},{3,4},{4,5},{5,6},{6,7},{7,8},{8,9},{9,10},{10,1... | collective-permute-start | bytes 1179656 | tf_op jit(solution)/shard_map/ppermute | solution.py:427
  7.2 22.2 %collective-permute-start.3 = (f32[24,8,512]{2,1,0:T(8,128)S(1)}, f32[24,8,512]{2,1,0:T(8,128)S(1)}, u32[]{:S(2)}, u32[]{:S(2)}) collective-permute-start(f32[24,8,512]{2,1,0:T(8,128)S(1)} %get-tuple-element.23), channel_id=1, source_target_pairs={{1,0},{2,1},{3,2},{4,3},{5,4},{6,5},{7,6},{8,7},{9,8},{10,9},{11,1... | collective-permute-start | bytes 1179656 | tf_op jit(solution)/shard_map/ppermute | solution.py:427
  21.0 9.9 %collective-permute-start.1 = (f32[24,8,512]{2,1,0:T(8,128)S(1)}, f32[24,8,512]{2,1,0:T(8,128)S(1)}, u32[]{:S(2)}, u32[]{:S(2)}) collective-permute-start(f32[24,8,512]{2,1,0:T(8,128)S(1)} %get-tuple-element.21), channel_id=1, source_target_pairs={{0,64},{64,128},{128,192},{192,256},{256,320},{320,384},{384,448},... | collective-permute-start | bytes 1179656 | tf_op jit(solution)/shard_map/ppermute | solution.py:444
  21.0 10.4 %collective-permute-start = (f32[24,8,512]{2,1,0:T(8,128)S(1)}, f32[24,8,512]{2,1,0:T(8,128)S(1)}, u32[]{:S(2)}, u32[]{:S(2)}) collective-permute-start(f32[24,8,512]{2,1,0:T(8,128)S(1)} %get-tuple-element.20), channel_id=1, source_target_pairs={{0,960},{64,0},{128,64},{192,128},{256,192},{320,256},{384,320},{4... | collective-permute-start | bytes 1179656 | tf_op jit(solution)/shard_map/ppermute | solution.py:444
  29.4 5.3 %collective-permute-start.4 = (f32[16,8,512]{2,1,0:T(8,128)S(1)}, f32[16,8,512]{2,1,0:T(8,128)S(1)}, u32[]{:S(2)}, u32[]{:S(2)}) collective-permute-start(f32[16,8,512]{2,1,0:T(8,128)S(1)} %get-tuple-element.24), channel_id=1, source_target_pairs={{0,960},{64,0},{128,64},{192,128},{256,192},{320,256},{384,320},{4... | collective-permute-start | bytes 786440 | tf_op jit(solution)/shard_map/ppermute | solution.py:444
  30.8 7.0 %collective-permute-start.5 = (f32[16,8,512]{2,1,0:T(8,128)S(1)}, f32[16,8,512]{2,1,0:T(8,128)S(1)}, u32[]{:S(2)}, u32[]{:S(2)}) collective-permute-start(f32[16,8,512]{2,1,0:T(8,128)S(1)} %get-tuple-element.25), channel_id=1, source_target_pairs={{0,64},{64,128},{128,192},{192,256},{256,320},{320,384},{384,448},... | collective-permute-start | bytes 786440 | tf_op jit(solution)/shard_map/ppermute | solution.py:444
  40.1 9.6 %collective-permute-start.6 = (f32[5,16,256]{2,1,0:T(8,128)S(1)}, f32[5,16,256]{2,1,0:T(8,128)S(1)}, u32[]{:S(2)}, u32[]{:S(2)}) collective-permute-start(f32[5,16,256]{2,1,0:T(8,128)S(1)} %get-tuple-element.28), channel_id=1, source_target_pairs={{0,1},{2,3},{4,5},{6,7},{8,9},{10,11},{12,13},{14,15},{16,17},{18,... | collective-permute-start | bytes 245768 | tf_op jit(solution)/shard_map/ppermute | solution.py:433
  42.0 10.1 %collective-permute-start.7 = (f32[5,16,256]{2,1,0:T(8,128)S(1)}, f32[5,16,256]{2,1,0:T(8,128)S(1)}, u32[]{:S(2)}, u32[]{:S(2)}) collective-permute-start(f32[5,16,256]{2,1,0:T(8,128)S(1)} %get-tuple-element.28), channel_id=1, source_target_pairs={{1,2},{3,4},{5,6},{7,8},{9,10},{11,12},{13,14},{15,16},{17,18},{19... | collective-permute-start | bytes 245768 | tf_op jit(solution)/shard_map/ppermute | solution.py:433
  52.1 6.8 %collective-permute-start.8 = (f32[3,5,16,256]{3,2,1,0:T(8,128)S(1)}, f32[3,5,16,256]{3,2,1,0:T(8,128)S(1)}, u32[]{:S(2)}, u32[]{:S(2)}) collective-permute-start(f32[3,5,16,256]{3,2,1,0:T(8,128)S(1)} %pad_maximum_fusion.here), channel_id=1, source_target_pairs={{0,64},{64,128},{128,192},{192,256},{256,320},{320,384},{384,448},... | collective-permute-start | bytes 737288 | tf_op jit(solution)/shard_map/ppermute | solution.py:444
  52.2 6.8 %collective-permute-start.9 = (f32[3,5,16,256]{3,2,1,0:T(8,128)S(1)}, f32[3,5,16,256]{3,2,1,0:T(8,128)S(1)}, u32[]{:S(2)}, u32[]{:S(2)}) collective-permute-start(f32[3,5,16,256]{3,2,1,0:T(8,128)S(1)} %pad_maximum_fusion.here), channel_id=1, source_target_pairs={{0,960},{64,0},{128,64},{192,128},{256,192},{320,256},{384,320},{4... | collective-permute-start | bytes 737288 | tf_op jit(solution)/shard_map/ppermute | solution.py:444
  60.1 5.6 %collective-permute-start.10 = (f32[20,128]{1,0:T(8,128)S(1)}, f32[20,128]{1,0:T(8,128)S(1)}, u32[]{:S(2)}, u32[]{:S(2)}) collective-permute-start(f32[20,128]{1,0:T(8,128)S(1)} %get-tuple-element.31), channel_id=1, source_target_pairs={{0,1},{2,3},{4,5},{6,7},{8,9},{10,11},{12,13},{14,15},{16,17},{18,... | collective-permute-start | bytes 30728 | tf_op jit(solution)/shard_map/ppermute | solution.py:433
  62.0 4.3 %collective-permute-start.11 = (f32[20,128]{1,0:T(8,128)S(1)}, f32[20,128]{1,0:T(8,128)S(1)}, u32[]{:S(2)}, u32[]{:S(2)}) collective-permute-start(f32[20,128]{1,0:T(8,128)S(1)} %get-tuple-element.31), channel_id=1, source_target_pairs={{0,64},{64,128},{128,192},{192,256},{256,320},{320,384},{384,448},... | collective-permute-start | bytes 30728 | tf_op jit(solution)/shard_map/ppermute | solution.py:444
  62.0 4.4 %collective-permute-start.12 = (f32[20,128]{1,0:T(8,128)S(1)}, f32[20,128]{1,0:T(8,128)S(1)}, u32[]{:S(2)}, u32[]{:S(2)}) collective-permute-start(f32[20,128]{1,0:T(8,128)S(1)} %get-tuple-element.31), channel_id=1, source_target_pairs={{0,960},{64,0},{128,64},{192,128},{256,192},{320,256},{384,320},{4... | collective-permute-start | bytes 30728 | tf_op jit(solution)/shard_map/ppermute | solution.py:444
  66.4 9.0 %collective-permute-start.13 = (f32[2,20,128]{2,1,0:T(8,128)S(1)}, f32[2,20,128]{2,1,0:T(8,128)S(1)}, u32[]{:S(2)}, u32[]{:S(2)}) collective-permute-start(f32[2,20,128]{2,1,0:T(8,128)S(1)} %pad_maximum_fusion.5), channel_id=1, source_target_pairs={{1,2},{3,4},{5,6},{7,8},{9,10},{11,12},{13,14},{15,16},{17,18},{19... | collective-permute-start | bytes 61448 | tf_op jit(solution)/shard_map/ppermute | solution.py:433
  75.4 8.6 %collective-permute-start.14 = (f32[4,20,128]{2,1,0:T(8,128)S(1)}, f32[4,20,128]{2,1,0:T(8,128)S(1)}, u32[]{:S(2)}, u32[]{:S(2)}) collective-permute-start(f32[4,20,128]{2,1,0:T(8,128)S(1)} %get-tuple-element.38), channel_id=1, source_target_pairs={{0,64},{64,128},{128,192},{192,256},{256,320},{320,384},{384,448},... | collective-permute-start | bytes 122888 | tf_op jit(solution)/shard_map/ppermute | solution.py:444
  75.4 8.5 %collective-permute-start.15 = (f32[4,20,128]{2,1,0:T(8,128)S(1)}, f32[4,20,128]{2,1,0:T(8,128)S(1)}, u32[]{:S(2)}, u32[]{:S(2)}) collective-permute-start(f32[4,20,128]{2,1,0:T(8,128)S(1)} %get-tuple-element.37), channel_id=1, source_target_pairs={{0,960},{64,0},{128,64},{192,128},{256,192},{320,256},{384,320},{4... | collective-permute-start | bytes 122888 | tf_op jit(solution)/shard_map/ppermute | solution.py:444
  78.4 5.6 %collective-permute-start.16 = (f32[20,128]{1,0:T(8,128)S(1)}, f32[20,128]{1,0:T(8,128)S(1)}, u32[]{:S(2)}, u32[]{:S(2)}) collective-permute-start(f32[20,128]{1,0:T(8,128)S(1)} %slice_bitcast_fusion), channel_id=1, source_target_pairs={{0,1},{2,3},{4,5},{6,7},{8,9},{10,11},{12,13},{14,15},{16,17},{18,... | collective-permute-start | bytes 30728 | tf_op jit(solution)/shard_map/ppermute | solution.py:433

commit v9 on v8

--- a/solution.py
+++ b/solution.py
@@ -391,7 +391,7 @@
     p2[4:20] = c2[...]
 
 
-def coarse_level_body(count, left, mid, right, other, last, out, win, weights, held):
+def coarse_level_body(count, last, left, mid, right, other, out, win, weights, held):
     win[...] = jnp.zeros(win.shape, F32)
     near = beside(count)
     even = jnp.where(lax.axis_index("gy") % 2 == 0, 1.0, 0.0)
@@ -515,7 +515,7 @@
     coarse = call(
         functools.partial(coarse_level_body, count),
         shape(2, 2, nz // 4),
-        (left, jnp.stack([below, p2, above]), right, other, last),
+        (last, left, jnp.stack([below, p2, above]), right, other),
         [
             pltpu.VMEM((5, 9, 8, nz // 4), F32),
             pltpu.VMEM((7, 8, 8, nz // 4), F32),

time: 85.1 us -> 84.8 us (level)
  the two profiles are of different devices: /device:TPU:64 before, /device:TPU:71 now
where the time goes in v9:
time: 84.8 us; the launch traced here: 84.5 us
  starting transfers between devices  50.7 us (60%)
  waiting for transfers between devices  26.9 us (32%)
  Pallas kernels  6.05 us (7%)
    ppermute x5, starting transfers between devices, swapped(): lax.ppermute(block, 'gy', [(i, i + 1) for i in firsts] + [(i + 1, i) for...  20.1 us
    ppermute x2, starting transfers between devices, along_y(): lax.ppermute(block, 'gy', [(i, i + by) for i in range(count) if 0 <= i +...  18.7 us
    ppermute x10, waiting for transfers between devices, round_x(): lax.ppermute(block, 'gx', [(i, (i + by) % count) for i in range(count)])  15.3 us
    ppermute x10, starting transfers between devices, round_x(): lax.ppermute(block, 'gx', [(i, (i + by) % count) for i in range(count)])  11.9 us
    ppermute x5, waiting for transfers between devices, swapped(): lax.ppermute(block, 'gy', [(i, i + 1) for i in firsts] + [(i + 1, i) for...  7.07 us
    pallas_call x6, Pallas kernels, call(): pl.pallas_call(body, out_shape=outs, in_specs=[pl.BlockSpec(memory_space=...  6.05 us
    ppermute x2, waiting for transfers between devices, along_y(): lax.ppermute(block, 'gy', [(i, i + by) for i in range(count) if 0 <= i +...  4.49 us
  transfers between devices with their start and end apart: 17, of which 11 were waited for; matrix products, arithmetic and copies ran while one was open for 0% of the time, Pallas kernels for 1%

profile of v9, /device:TPU:71, one launch (start us, length us, event | category | flops | bytes accessed | tf_op | source)
XLA Modules:
  0.0 84.5 jit_solution(8810629921125699902)
XLA Ops:
  0.6 1.3 %shard_map.85 = (f32[48,8,512]{2,1,0:T(8,128)S(1)}, f32[24,8,512]{2,1,0:T(8,128)S(1)}, f32[24,8,512]{2,1,0:T(8,128)S(1)}, f32[24,8,512]{2,1,0:T(8,128)S(1)}, f32[24,8,512]{2,1,0:T(8,128)S(1)}) custom-call(f32[8,8,512]{2,1,0:T(8,128)} %u.1, f32[8,8,512]{2,1,0:T(8,128)} %f.1, bf16[8,8,512]{2,1,0:T(8,128)(2,1)} %a.1, bf16[8,8,512]{2,1,0:T(8,128)(2,1)} %bx.1, ...), custom_call_target="tpu_custom_call" | custom-call | flops 1000000 | bytes 2000000 | tf_op jit(solution)/shard_map/pallas_call | solution.py:24
  2.0 4.9 %collective-permute-start.2 = (f32[24,8,512]{2,1,0:T(8,128)S(1)}, f32[24,8,512]{2,1,0:T(8,128)S(1)}, u32[]{:S(2)}, u32[]{:S(2)}) collective-permute-start(f32[24,8,512]{2,1,0:T(8,128)S(1)} %get-tuple-element.22), channel_id=1, source_target_pairs={{0,1},{1,2},{2,3},{3,4},{4,5},{5,6},{6,7},{7,8},{8,9},{9,10},{10,1... | collective-permute-start | bytes 1179656 | tf_op jit(solution)/shard_map/ppermute | solution.py:427
  6.9 13.8 %collective-permute-start.3 = (f32[24,8,512]{2,1,0:T(8,128)S(1)}, f32[24,8,512]{2,1,0:T(8,128)S(1)}, u32[]{:S(2)}, u32[]{:S(2)}) collective-permute-start(f32[24,8,512]{2,1,0:T(8,128)S(1)} %get-tuple-element.23), channel_id=1, source_target_pairs={{1,0},{2,1},{3,2},{4,3},{5,4},{6,5},{7,6},{8,7},{9,8},{10,9},{11,1... | collective-permute-start | bytes 1179656 | tf_op jit(solution)/shard_map/ppermute | solution.py:427
  20.7 3.3 %collective-permute-start.1 = (f32[24,8,512]{2,1,0:T(8,128)S(1)}, f32[24,8,512]{2,1,0:T(8,128)S(1)}, u32[]{:S(2)}, u32[]{:S(2)}) collective-permute-start(f32[24,8,512]{2,1,0:T(8,128)S(1)} %get-tuple-element.21), channel_id=1, source_target_pairs={{0,64},{64,128},{128,192},{192,256},{256,320},{320,384},{384,448},... | collective-permute-start | bytes 1179656 | tf_op jit(solution)/shard_map/ppermute | solution.py:444
  24.0 0.0 collective-permute-start
  24.0 3.6 %collective-permute-done.2.yhr = f32[24,8,512]{2,1,0:T(8,128)S(1)} collective-permute-done((f32[24,8,512]{2,1,0:T(8,128)S(1)}, f32[24,8,512]{2,1,0:T(8,128)S(1)}, u32[]{:S(2)}, u32[]{:S(2)}) %collective-permute-start.2) | collective-permute-done | bytes 393248 | tf_op jit(solution)/shard_map/ppermute | solution.py:427
  27.6 0.9 %collective-permute-done.3.ylr = f32[24,8,512]{2,1,0:T(8,128)S(1)} collective-permute-done((f32[24,8,512]{2,1,0:T(8,128)S(1)}, f32[24,8,512]{2,1,0:T(8,128)S(1)}, u32[]{:S(2)}, u32[]{:S(2)}) %collective-permute-start.3) | collective-permute-done | bytes 393248 | tf_op jit(solution)/shard_map/ppermute | solution.py:427
  28.5 1.6 %collective-permute-start.4 = (f32[16,8,512]{2,1,0:T(8,128)S(1)}, f32[16,8,512]{2,1,0:T(8,128)S(1)}, u32[]{:S(2)}, u32[]{:S(2)}) collective-permute-start(f32[16,8,512]{2,1,0:T(8,128)S(1)} %get-tuple-element.24), channel_id=1, source_target_pairs={{0,960},{64,0},{128,64},{192,128},{256,192},{320,256},{384,320},{4... | collective-permute-start | bytes 786440 | tf_op jit(solution)/shard_map/ppermute | solution.py:444
  30.1 2.3 %collective-permute-start.5 = (f32[16,8,512]{2,1,0:T(8,128)S(1)}, f32[16,8,512]{2,1,0:T(8,128)S(1)}, u32[]{:S(2)}, u32[]{:S(2)}) collective-permute-start(f32[16,8,512]{2,1,0:T(8,128)S(1)} %get-tuple-element.25), channel_id=1, source_target_pairs={{0,64},{64,128},{128,192},{192,256},{256,320},{320,384},{384,448},... | collective-permute-start | bytes 786440 | tf_op jit(solution)/shard_map/ppermute | solution.py:444
  32.4 0.0 collective-permute-done.1.xhr
  32.4 0.5 shard_map.87
  33.0 0.0 collective-permute-done.xlr
  33.0 3.5 %collective-permute-done.4.xclr = f32[16,8,512]{2,1,0:T(8,128)S(1)} collective-permute-done((f32[16,8,512]{2,1,0:T(8,128)S(1)}, f32[16,8,512]{2,1,0:T(8,128)S(1)}, u32[]{:S(2)}, u32[]{:S(2)}) %collective-permute-start.4) | collective-permute-done | bytes 262176 | tf_op jit(solution)/shard_map/ppermute | solution.py:444
  36.4 0.0 collective-permute-done.5.xchr
  36.4 2.2 %shard_map.88 = (f32[8,8,512]{2,1,0:T(8,128)}, f32[5,16,256]{2,1,0:T(8,128)S(1)}) custom-call(f32[48,8,512]{2,1,0:T(8,128)S(1)} %get-tuple-element.19.own, f32[24,8,512]{2,1,0:T(8,128)S(1)} %collective-permute-done.xlr, f32[24,8,512]{2,1,0:T(8,128)S(1)} %collective-permute-done.1.xhr, f32[24,8,512]{2,1,0:T(8,128)S(1)} %collective-permute-done.2.yhr, ...), custom_call_target="tpu_custom_call" | custom-call | flops 20000000 | bytes 20000000 | tf_op jit(solution)/shard_map/pallas_call | solution.py:24
  38.7 1.9 %collective-permute-start.6 = (f32[5,16,256]{2,1,0:T(8,128)S(1)}, f32[5,16,256]{2,1,0:T(8,128)S(1)}, u32[]{:S(2)}, u32[]{:S(2)}) collective-permute-start(f32[5,16,256]{2,1,0:T(8,128)S(1)} %get-tuple-element.28), channel_id=1, source_target_pairs={{0,1},{2,3},{4,5},{6,7},{8,9},{10,11},{12,13},{14,15},{16,17},{18,... | collective-permute-start | bytes 245768 | tf_op jit(solution)/shard_map/ppermute | solution.py:433
  40.6 7.4 %collective-permute-start.7 = (f32[5,16,256]{2,1,0:T(8,128)S(1)}, f32[5,16,256]{2,1,0:T(8,128)S(1)}, u32[]{:S(2)}, u32[]{:S(2)}) collective-permute-start(f32[5,16,256]{2,1,0:T(8,128)S(1)} %get-tuple-element.28), channel_id=1, source_target_pairs={{1,2},{3,4},{5,6},{7,8},{9,10},{11,12},{13,14},{15,16},{17,18},{19... | collective-permute-start | bytes 245768 | tf_op jit(solution)/shard_map/ppermute | solution.py:433
  48.0 0.0 collective-permute-done.6
  48.0 2.3 %collective-permute-done.7 = f32[5,16,256]{2,1,0:T(8,128)S(1)} collective-permute-done((f32[5,16,256]{2,1,0:T(8,128)S(1)}, f32[5,16,256]{2,1,0:T(8,128)S(1)}, u32[]{:S(2)}, u32[]{:S(2)}) %collective-permute-start.7) | collective-permute-done | bytes 81952 | tf_op jit(solution)/shard_map/ppermute | solution.py:433
  50.4 3.3 %collective-permute-start.8 = (f32[3,5,16,256]{3,2,1,0:T(8,128)S(1)}, f32[3,5,16,256]{3,2,1,0:T(8,128)S(1)}, u32[]{:S(2)}, u32[]{:S(2)}) collective-permute-start(f32[3,5,16,256]{3,2,1,0:T(8,128)S(1)} %pad_maximum_fusion.here), channel_id=1, source_target_pairs={{0,64},{64,128},{128,192},{192,256},{256,320},{320,384},{384,448},... | collective-permute-start | bytes 737288 | tf_op jit(solution)/shard_map/ppermute | solution.py:444
  53.7 0.0 collective-permute-start.9
  53.7 3.1 %collective-permute-done.8.left = f32[3,5,16,256]{3,2,1,0:T(8,128)S(1)} collective-permute-done((f32[3,5,16,256]{3,2,1,0:T(8,128)S(1)}, f32[3,5,16,256]{3,2,1,0:T(8,128)S(1)}, u32[]{:S(2)}, u32[]{:S(2)}) %collective-permute-start.8) | collective-permute-done | bytes 245792 | tf_op jit(solution)/shard_map/ppermute | solution.py:444
  56.9 3.7 %collective-permute-done.9.right = f32[3,5,16,256]{3,2,1,0:T(8,128)S(1)} collective-permute-done((f32[3,5,16,256]{3,2,1,0:T(8,128)S(1)}, f32[3,5,16,256]{3,2,1,0:T(8,128)S(1)}, u32[]{:S(2)}, u32[]{:S(2)}) %collective-permute-start.9) | collective-permute-done | bytes 245792 | tf_op jit(solution)/shard_map/ppermute | solution.py:444
  60.6 1.1 %shard_map.89 = (f32[4,4,256]{2,1,0:T(4,128)}, f32[20,128]{1,0:T(8,128)S(1)}) custom-call(f32[3,5,16,256]{3,2,1,0:T(8,128)S(1)} %collective-permute-done.8.left, f32[3,5,16,256]{3,2,1,0:T(8,128)S(1)} %pad_maximum_fusion.here, f32[3,5,16,256]{3,2,1,0:T(8,128)S(1)} %collective-permute-done.9.right, f32[16,128]{1,0:T(8,128)S(1)} %get-tuple-element.29.c2), custom_call_target="tpu_custom_call" | custom-call | flops 1000000 | bytes 2000000 | tf_op jit(solution)/shard_map/pallas_call | solution.py:24
  61.6 1.9 %collective-permute-start.10 = (f32[20,128]{1,0:T(8,128)S(1)}, f32[20,128]{1,0:T(8,128)S(1)}, u32[]{:S(2)}, u32[]{:S(2)}) collective-permute-start(f32[20,128]{1,0:T(8,128)S(1)} %get-tuple-element.31), channel_id=1, source_target_pairs={{0,1},{2,3},{4,5},{6,7},{8,9},{10,11},{12,13},{14,15},{16,17},{18,... | collective-permute-start | bytes 30728 | tf_op jit(solution)/shard_map/ppermute | solution.py:433
  63.5 0.0 collective-permute-start.11
  63.6 0.5 collective-permute-start.12
  64.1 2.0 %collective-permute-done.10 = f32[20,128]{1,0:T(8,128)S(1)} collective-permute-done((f32[20,128]{1,0:T(8,128)S(1)}, f32[20,128]{1,0:T(8,128)S(1)}, u32[]{:S(2)}, u32[]{:S(2)}) %collective-permute-start.10) | collective-permute-done | bytes 10272 | tf_op jit(solution)/shard_map/ppermute | solution.py:433
  66.1 0.0 collective-permute-done.11
  66.1 1.9 %collective-permute-done.12 = f32[20,128]{1,0:T(8,128)S(1)} collective-permute-done((f32[20,128]{1,0:T(8,128)S(1)}, f32[20,128]{1,0:T(8,128)S(1)}, u32[]{:S(2)}, u32[]{:S(2)}) %collective-permute-start.12) | collective-permute-done | bytes 10272 | tf_op jit(solution)/shard_map/ppermute | solution.py:444
  67.9 7.0 %collective-permute-start.13 = (f32[2,20,128]{2,1,0:T(8,128)S(1)}, f32[2,20,128]{2,1,0:T(8,128)S(1)}, u32[]{:S(2)}, u32[]{:S(2)}) collective-permute-start(f32[2,20,128]{2,1,0:T(8,128)S(1)} %pad_maximum_fusion.5), channel_id=1, source_target_pairs={{1,2},{3,4},{5,6},{7,8},{9,10},{11,12},{13,14},{15,16},{17,18},{19... | collective-permute-start | bytes 61448 | tf_op jit(solution)/shard_map/ppermute | solution.py:433
  74.9 1.2 %collective-permute-done.13.other = f32[2,20,128]{2,1,0:T(8,128)S(1)} collective-permute-done((f32[2,20,128]{2,1,0:T(8,128)S(1)}, f32[2,20,128]{2,1,0:T(8,128)S(1)}, u32[]{:S(2)}, u32[]{:S(2)}) %collective-permute-start.13) | collective-permute-done | bytes 20512 | tf_op jit(solution)/shard_map/ppermute | solution.py:433
  76.1 1.9 %collective-permute-start.14 = (f32[20,128]{1,0:T(8,128)S(1)}, f32[20,128]{1,0:T(8,128)S(1)}, u32[]{:S(2)}, u32[]{:S(2)}) collective-permute-start(f32[20,128]{1,0:T(8,128)S(1)} %slice_bitcast_fusion), channel_id=1, source_target_pairs={{0,1},{2,3},{4,5},{6,7},{8,9},{10,11},{12,13},{14,15},{16,17},{18,... | collective-permute-start | bytes 30728 | tf_op jit(solution)/shard_map/ppermute | solution.py:433
  78.0 0.9 %collective-permute-start.15 = (f32[4,20,128]{2,1,0:T(8,128)S(1)}, f32[4,20,128]{2,1,0:T(8,128)S(1)}, u32[]{:S(2)}, u32[]{:S(2)}) collective-permute-start(f32[4,20,128]{2,1,0:T(8,128)S(1)} %get-tuple-element.38), channel_id=1, source_target_pairs={{0,64},{64,128},{128,192},{192,256},{256,320},{320,384},{384,448},... | collective-permute-start | bytes 122888 | tf_op jit(solution)/shard_map/ppermute | solution.py:444
  78.9 0.0 collective-permute-start.16
  78.9 1.6 %collective-permute-done.14.last = f32[20,128]{1,0:T(8,128)S(1)} collective-permute-done((f32[20,128]{1,0:T(8,128)S(1)}, f32[20,128]{1,0:T(8,128)S(1)}, u32[]{:S(2)}, u32[]{:S(2)}) %collective-permute-start.14) | collective-permute-done | bytes 10272 | tf_op jit(solution)/shard_map/ppermute | solution.py:433
  80.5 0.0 collective-permute-done.15.left
  80.5 3.2 %collective-permute-done.16.right = f32[4,20,128]{2,1,0:T(8,128)S(1)} collective-permute-done((f32[4,20,128]{2,1,0:T(8,128)S(1)}, f32[4,20,128]{2,1,0:T(8,128)S(1)}, u32[]{:S(2)}, u32[]{:S(2)}) %collective-permute-start.16) | collective-permute-done | bytes 40992 | tf_op jit(solution)/shard_map/ppermute | solution.py:444
  83.7 0.9 %shard_map.90 = f32[2,2,128]{2,1,0:T(2,128)} custom-call(f32[20,128]{1,0:T(8,128)S(1)} %collective-permute-done.14.last, f32[4,20,128]{2,1,0:T(8,128)S(1)} %collective-permute-done.15.left, f32[3,20,128]{2,1,0:T(8,128)S(1)} %pad_maximum_fusion.4.mid, f32[4,20,128]{2,1,0:T(8,128)S(1)} %collective-permute-done.16.right, ...), custom_call_target="tpu_custom_call" | custom-call | flops 1000000 | bytes 2000000 | tf_op jit(solution)/shard_map/pallas_call | solution.py:24
  (8 shorter events, 0.1 us)
Async XLA Ops:
  2.0 25.6 %collective-permute-start.2 = (f32[24,8,512]{2,1,0:T(8,128)S(1)}, f32[24,8,512]{2,1,0:T(8,128)S(1)}, u32[]{:S(2)}, u32[]{:S(2)}) collective-permute-start(f32[24,8,512]{2,1,0:T(8,128)S(1)} %get-tuple-element.22), channel_id=1, source_target_pairs={{0,1},{1,2},{2,3},{3,4},{4,5},{5,6},{6,7},{7,8},{8,9},{9,10},{10,1... | collective-permute-start | bytes 1179656 | tf_op jit(solution)/shard_map/ppermute | solution.py:427
  6.9 21.6 %collective-permute-start.3 = (f32[24,8,512]{2,1,0:T(8,128)S(1)}, f32[24,8,512]{2,1,0:T(8,128)S(1)}, u32[]{:S(2)}, u32[]{:S(2)}) collective-permute-start(f32[24,8,512]{2,1,0:T(8,128)S(1)} %get-tuple-element.23), channel_id=1, source_target_pairs={{1,0},{2,1},{3,2},{4,3},{5,4},{6,5},{7,6},{8,7},{9,8},{10,9},{11,1... | collective-permute-start | bytes 1179656 | tf_op jit(solution)/shard_map/ppermute | solution.py:427
  20.7 11.7 %collective-permute-start.1 = (f32[24,8,512]{2,1,0:T(8,128)S(1)}, f32[24,8,512]{2,1,0:T(8,128)S(1)}, u32[]{:S(2)}, u32[]{:S(2)}) collective-permute-start(f32[24,8,512]{2,1,0:T(8,128)S(1)} %get-tuple-element.21), channel_id=1, source_target_pairs={{0,64},{64,128},{128,192},{192,256},{256,320},{320,384},{384,448},... | collective-permute-start | bytes 1179656 | tf_op jit(solution)/shard_map/ppermute | solution.py:444
  24.0 9.0 %collective-permute-start = (f32[24,8,512]{2,1,0:T(8,128)S(1)}, f32[24,8,512]{2,1,0:T(8,128)S(1)}, u32[]{:S(2)}, u32[]{:S(2)}) collective-permute-start(f32[24,8,512]{2,1,0:T(8,128)S(1)} %get-tuple-element.20), channel_id=1, source_target_pairs={{0,960},{64,0},{128,64},{192,128},{256,192},{320,256},{384,320},{4... | collective-permute-start | bytes 1179656 | tf_op jit(solution)/shard_map/ppermute | solution.py:444
  28.5 7.9 %collective-permute-start.4 = (f32[16,8,512]{2,1,0:T(8,128)S(1)}, f32[16,8,512]{2,1,0:T(8,128)S(1)}, u32[]{:S(2)}, u32[]{:S(2)}) collective-permute-start(f32[16,8,512]{2,1,0:T(8,128)S(1)} %get-tuple-element.24), channel_id=1, source_target_pairs={{0,960},{64,0},{128,64},{192,128},{256,192},{320,256},{384,320},{4... | collective-permute-start | bytes 786440 | tf_op jit(solution)/shard_map/ppermute | solution.py:444
  30.1 6.4 %collective-permute-start.5 = (f32[16,8,512]{2,1,0:T(8,128)S(1)}, f32[16,8,512]{2,1,0:T(8,128)S(1)}, u32[]{:S(2)}, u32[]{:S(2)}) collective-permute-start(f32[16,8,512]{2,1,0:T(8,128)S(1)} %get-tuple-element.25), channel_id=1, source_target_pairs={{0,64},{64,128},{128,192},{192,256},{256,320},{320,384},{384,448},... | collective-permute-start | bytes 786440 | tf_op jit(solution)/shard_map/ppermute | solution.py:444
  38.7 9.4 %collective-permute-start.6 = (f32[5,16,256]{2,1,0:T(8,128)S(1)}, f32[5,16,256]{2,1,0:T(8,128)S(1)}, u32[]{:S(2)}, u32[]{:S(2)}) collective-permute-start(f32[5,16,256]{2,1,0:T(8,128)S(1)} %get-tuple-element.28), channel_id=1, source_target_pairs={{0,1},{2,3},{4,5},{6,7},{8,9},{10,11},{12,13},{14,15},{16,17},{18,... | collective-permute-start | bytes 245768 | tf_op jit(solution)/shard_map/ppermute | solution.py:433
  40.6 9.8 %collective-permute-start.7 = (f32[5,16,256]{2,1,0:T(8,128)S(1)}, f32[5,16,256]{2,1,0:T(8,128)S(1)}, u32[]{:S(2)}, u32[]{:S(2)}) collective-permute-start(f32[5,16,256]{2,1,0:T(8,128)S(1)} %get-tuple-element.28), channel_id=1, source_target_pairs={{1,2},{3,4},{5,6},{7,8},{9,10},{11,12},{13,14},{15,16},{17,18},{19... | collective-permute-start | bytes 245768 | tf_op jit(solution)/shard_map/ppermute | solution.py:433
  50.4 6.5 %collective-permute-start.8 = (f32[3,5,16,256]{3,2,1,0:T(8,128)S(1)}, f32[3,5,16,256]{3,2,1,0:T(8,128)S(1)}, u32[]{:S(2)}, u32[]{:S(2)}) collective-permute-start(f32[3,5,16,256]{3,2,1,0:T(8,128)S(1)} %pad_maximum_fusion.here), channel_id=1, source_target_pairs={{0,64},{64,128},{128,192},{192,256},{256,320},{320,384},{384,448},... | collective-permute-start | bytes 737288 | tf_op jit(solution)/shard_map/ppermute | solution.py:444
  53.7 6.8 %collective-permute-start.9 = (f32[3,5,16,256]{3,2,1,0:T(8,128)S(1)}, f32[3,5,16,256]{3,2,1,0:T(8,128)S(1)}, u32[]{:S(2)}, u32[]{:S(2)}) collective-permute-start(f32[3,5,16,256]{3,2,1,0:T(8,128)S(1)} %pad_maximum_fusion.here), channel_id=1, source_target_pairs={{0,960},{64,0},{128,64},{192,128},{256,192},{320,256},{384,320},{4... | collective-permute-start | bytes 737288 | tf_op jit(solution)/shard_map/ppermute | solution.py:444
  61.6 4.4 %collective-permute-start.10 = (f32[20,128]{1,0:T(8,128)S(1)}, f32[20,128]{1,0:T(8,128)S(1)}, u32[]{:S(2)}, u32[]{:S(2)}) collective-permute-start(f32[20,128]{1,0:T(8,128)S(1)} %get-tuple-element.31), channel_id=1, source_target_pairs={{0,1},{2,3},{4,5},{6,7},{8,9},{10,11},{12,13},{14,15},{16,17},{18,... | collective-permute-start | bytes 30728 | tf_op jit(solution)/shard_map/ppermute | solution.py:433
  63.5 2.5 %collective-permute-start.11 = (f32[20,128]{1,0:T(8,128)S(1)}, f32[20,128]{1,0:T(8,128)S(1)}, u32[]{:S(2)}, u32[]{:S(2)}) collective-permute-start(f32[20,128]{1,0:T(8,128)S(1)} %get-tuple-element.31), channel_id=1, source_target_pairs={{0,64},{64,128},{128,192},{192,256},{256,320},{320,384},{384,448},... | collective-permute-start | bytes 30728 | tf_op jit(solution)/shard_map/ppermute | solution.py:444
  63.6 4.3 %collective-permute-start.12 = (f32[20,128]{1,0:T(8,128)S(1)}, f32[20,128]{1,0:T(8,128)S(1)}, u32[]{:S(2)}, u32[]{:S(2)}) collective-permute-start(f32[20,128]{1,0:T(8,128)S(1)} %get-tuple-element.31), channel_id=1, source_target_pairs={{0,960},{64,0},{128,64},{192,128},{256,192},{320,256},{384,320},{4... | collective-permute-start | bytes 30728 | tf_op jit(solution)/shard_map/ppermute | solution.py:444
  67.9 8.2 %collective-permute-start.13 = (f32[2,20,128]{2,1,0:T(8,128)S(1)}, f32[2,20,128]{2,1,0:T(8,128)S(1)}, u32[]{:S(2)}, u32[]{:S(2)}) collective-permute-start(f32[2,20,128]{2,1,0:T(8,128)S(1)} %pad_maximum_fusion.5), channel_id=1, source_target_pairs={{1,2},{3,4},{5,6},{7,8},{9,10},{11,12},{13,14},{15,16},{17,18},{19... | collective-permute-start | bytes 61448 | tf_op jit(solution)/shard_map/ppermute | solution.py:433
  76.1 4.4 %collective-permute-start.14 = (f32[20,128]{1,0:T(8,128)S(1)}, f32[20,128]{1,0:T(8,128)S(1)}, u32[]{:S(2)}, u32[]{:S(2)}) collective-permute-start(f32[20,128]{1,0:T(8,128)S(1)} %slice_bitcast_fusion), channel_id=1, source_target_pairs={{0,1},{2,3},{4,5},{6,7},{8,9},{10,11},{12,13},{14,15},{16,17},{18,... | collective-permute-start | bytes 30728 | tf_op jit(solution)/shard_map/ppermute | solution.py:433
  78.0 2.5 %collective-permute-start.15 = (f32[4,20,128]{2,1,0:T(8,128)S(1)}, f32[4,20,128]{2,1,0:T(8,128)S(1)}, u32[]{:S(2)}, u32[]{:S(2)}) collective-permute-start(f32[4,20,128]{2,1,0:T(8,128)S(1)} %get-tuple-element.38), channel_id=1, source_target_pairs={{0,64},{64,128},{128,192},{192,256},{256,320},{320,384},{384,448},... | collective-permute-start | bytes 122888 | tf_op jit(solution)/shard_map/ppermute | solution.py:444
  78.9 4.7 %collective-permute-start.16 = (f32[4,20,128]{2,1,0:T(8,128)S(1)}, f32[4,20,128]{2,1,0:T(8,128)S(1)}, u32[]{:S(2)}, u32[]{:S(2)}) collective-permute-start(f32[4,20,128]{2,1,0:T(8,128)S(1)} %get-tuple-element.37), channel_id=1, source_target_pairs={{0,960},{64,0},{128,64},{192,128},{256,192},{320,256},{384,320},{4... | collective-permute-start | bytes 122888 | tf_op jit(solution)/shard_map/ppermute | solution.py:444
